TPU v7x, 512 devices: a whole 4x8x8 slice. The times are simulated.
512 devices in a mesh: seq: 32 (over y, x), head: 16 (over z, core).
Axes of the slice: x: 4, y: 8, z: 8, core: 2. Of those that a mesh axis runs over, the one named last changes fastest.
Arguments:
- queries: float32 [32, 8192, 128], P('head', 'seq'), may hold values from -8 to 8
- keys: float32 [32, 8192, 128], P('head', 'seq'), may hold values from -8 to 8
- values: float32 [32, 8192, 128], P('head', 'seq'), may hold values from -6 to 6
- output: float32 [32, 8192, 128], P('head', 'seq'), may hold values from -3 to 3
- grad_output: float32 [32, 8192, 128], P(None, ('seq', 'head')), may hold values from -6 to 6
- mid_offsets: int32 [32, 9], P('head'), may hold values from 0 to 3
- far_offsets: int32 [32], P('head'), may hold values from 0 to 31
- drop_local: int32 [32, 8192, 64], P('head', 'seq'), may hold values from 0 to 4095
- drop_mid: int32 [32, 2048, 64], P('head', 'seq'), may hold values from 0 to 4095
- drop_far: int32 [32, 256, 64], P('head'), may hold values from 0 to 4095
Outputs:
- grad_queries: float32 [32, 8192, 128], P(None, ('seq', 'head'))
- grad_keys: float32 [32, 8192, 128], P(None, ('seq', 'head'))
- grad_values: float32 [32, 8192, 128], P(None, ('seq', 'head'))
All inputs are finite; a program needn't handle non-finite values.
Results may differ from a plain program's by a relative error of at most 0.0003.
Values sent between devices are 32-bit elements; how exact they have to be, the bound alone decides.
No kernel may reach another device: no remote copies, remote signals or barrier semaphores. Data moves between devices by JAX's collectives and lax.ppermute only.
A program may use at most 64 MiB of HBM per device.

v0:
```python
import jax
import jax.numpy as jnp
from jax import lax
from jax.sharding import PartitionSpec as P

GROUP = 4


keep_level = 7
keep_scale = 8.0 / 7.0
highest = lax.Precision.HIGHEST


def shifted(value, axis, steps):
    count = lax.axis_size(axis)
    initial, last = (max(0, -steps), min(count, count - steps))
    return lax.ppermute(value, axis, [(source, source + steps) for source in range(initial, last)])


def unpack_keep(words):
    bit_starts = jnp.arange(4, dtype=jnp.int32) * 3
    levels = jnp.bitwise_and(jnp.right_shift(words[..., None], bit_starts), 7)
    kept = jnp.where(levels < keep_level, keep_scale, 0.0).astype(jnp.float32)
    return kept.reshape(words.shape[:-1] + (words.shape[-1] * 4,))


def masked_lse(scores, allowed):
    return jax.nn.logsumexp(jnp.where(allowed, scores, -jnp.inf), axis=-1)


def chosen_mask(offsets, stride, extra_dims):
    chosen = jnp.arange(stride, dtype=jnp.int32)[None, None, :] == offsets[:, None, None]
    return chosen.reshape(chosen.shape + (1,) * extra_dims)


def pick_rows(source, offsets, stride):
    split_rows = source.reshape(
        (source.shape[0], source.shape[1] // stride, stride) + source.shape[2:]
    )
    chosen = chosen_mask(offsets, stride, source.ndim - 2)
    return jnp.sum(jnp.where(chosen, split_rows, 0.0), axis=2)


def add_rows(target, addend, offsets, stride):
    split_rows = target.reshape(
        (target.shape[0], target.shape[1] // stride, stride) + target.shape[2:]
    )
    chosen = chosen_mask(offsets, stride, target.ndim - 2)
    return (split_rows + jnp.where(chosen, jnp.expand_dims(addend, 2), 0.0)).reshape(target.shape)


def merge_lse(target, addend, offsets, stride):
    split_rows = target.reshape((target.shape[0], target.shape[1] // stride, stride))
    chosen = chosen_mask(offsets, stride, 0)
    merged = jnp.where(chosen, jnp.logaddexp(split_rows, jnp.expand_dims(addend, 2)), split_rows)
    return merged.reshape(target.shape)


def score_terms(scores, allowed, lse_rows, delta_rows, kept, value_rows, grad_rows):
    probs = jnp.where(allowed, jnp.exp(scores - lse_rows[..., None]), 0.0)
    dropped = probs * kept
    grad_probs = jnp.einsum("hqd,hkd->hqk", grad_rows, value_rows, precision=highest) * kept
    return (dropped, probs * (grad_probs - delta_rows[..., None]))


def per_device(
    queries,
    keys,
    values,
    output,
    grad_output,
    mid_offsets,
    far_offsets,
    drop_local,
    drop_mid,
    drop_far,
):
    row_count = queries.shape[1]
    score_scale = queries.shape[2] ** (-0.5)
    cycle_size = lax.axis_size("seq")
    cycle_place = lax.axis_index("seq")
    grad_rows = lax.all_to_all(grad_output, "head", split_axis=0, concat_axis=1, tiled=True)
    delta = jnp.sum(grad_rows * output, axis=-1)
    row_order = jnp.arange(row_count, dtype=jnp.int32)
    local_scores = jnp.einsum("hqd,hkd->hqk", queries, keys, precision=highest) * score_scale
    local_allowed = (row_order[:, None] >= row_order[None, :])[None]
    total_lse = masked_lse(local_scores, local_allowed)
    quarter_rows = row_count // GROUP
    shifted_place = cycle_place + GROUP // 2
    group_pos = shifted_place % GROUP
    mid_off = lax.dynamic_index_in_dim(mid_offsets, shifted_place // GROUP, 1, keepdims=False)
    mid_q = pick_rows(queries, mid_off, GROUP)
    mid_k = pick_rows(keys, mid_off, GROUP)
    mid_v = pick_rows(values, mid_off, GROUP)
    mid_grad = pick_rows(grad_rows, mid_off, GROUP)
    mid_delta = pick_rows(delta, mid_off, GROUP)
    mid_pair = jnp.stack([mid_k, mid_v])
    quarter_order = jnp.arange(quarter_rows, dtype=jnp.int32)
    key_blocks = [mid_k]
    value_blocks = [mid_v]
    allowed_blocks = [quarter_order[:, None] >= quarter_order[None, :]]
    mid_words = unpack_keep(drop_mid)
    keep_blocks = [lax.dynamic_slice_in_dim(mid_words, group_pos * quarter_rows, quarter_rows, 2)]
    for distance in range(1, GROUP):
        received = shifted(mid_pair, "seq", distance)
        key_blocks.append(received[0])
        value_blocks.append(received[1])
        allowed_blocks.append(
            jnp.broadcast_to(
                (group_pos >= distance) & (cycle_place >= distance), (quarter_rows, quarter_rows)
            )
        )
        keep_blocks.append(
            lax.dynamic_slice_in_dim(
                mid_words, jnp.maximum(group_pos - distance, 0) * quarter_rows, quarter_rows, 2
            )
        )
    mid_keys_all = jnp.concatenate(key_blocks, axis=1)
    mid_values_all = jnp.concatenate(value_blocks, axis=1)
    mid_allowed = jnp.concatenate(allowed_blocks, axis=1)[None]
    mid_keep = jnp.concatenate(keep_blocks, axis=2)
    mid_scores = jnp.einsum("hqd,hkd->hqk", mid_q, mid_keys_all, precision=highest) * score_scale
    mid_lse = masked_lse(mid_scores, mid_allowed)
    far_rows = row_count // cycle_size
    far_q = pick_rows(queries, far_offsets, cycle_size)
    far_k = pick_rows(keys, far_offsets, cycle_size)
    far_v = pick_rows(values, far_offsets, cycle_size)
    far_grad = pick_rows(grad_rows, far_offsets, cycle_size)
    far_delta = pick_rows(delta, far_offsets, cycle_size)
    far_all = lax.all_gather(jnp.stack([far_k, far_v]), "seq", axis=2, tiled=True)
    own_index = cycle_place * far_rows + jnp.arange(far_rows, dtype=jnp.int32)
    far_allowed = (row_order[None, :] <= own_index[:, None])[None]
    far_keep = unpack_keep(lax.dynamic_slice_in_dim(drop_far, cycle_place * far_rows, far_rows, 1))
    far_scores = jnp.einsum("hqd,hkd->hqk", far_q, far_all[0], precision=highest) * score_scale
    far_lse = masked_lse(far_scores, far_allowed)
    total_lse = merge_lse(total_lse, mid_lse, mid_off, GROUP)
    total_lse = merge_lse(total_lse, far_lse, far_offsets, cycle_size)
    local_keep = unpack_keep(drop_local)
    dropped, grad_scores = score_terms(
        local_scores, local_allowed, total_lse, delta, local_keep, values, grad_rows
    )
    grad_v = jnp.einsum("hqk,hqd->hkd", dropped, grad_rows, precision=highest)
    grad_q = jnp.einsum("hqk,hkd->hqd", grad_scores, keys, precision=highest) * score_scale
    grad_k = jnp.einsum("hqk,hqd->hkd", grad_scores, queries, precision=highest) * score_scale
    mid_lse_rows = pick_rows(total_lse, mid_off, GROUP)
    dropped, grad_scores = score_terms(
        mid_scores, mid_allowed, mid_lse_rows, mid_delta, mid_keep, mid_values_all, mid_grad
    )
    mid_gv = jnp.einsum("hqk,hqd->hkd", dropped, mid_grad, precision=highest)
    mid_gq = jnp.einsum("hqk,hkd->hqd", grad_scores, mid_keys_all, precision=highest) * score_scale
    mid_gk = jnp.einsum("hqk,hqd->hkd", grad_scores, mid_q, precision=highest) * score_scale
    own_gk = mid_gk[:, :quarter_rows]
    own_gv = mid_gv[:, :quarter_rows]
    for distance in range(1, GROUP):
        outgoing = jnp.stack(
            [
                mid_gk[:, distance * quarter_rows : (distance + 1) * quarter_rows],
                mid_gv[:, distance * quarter_rows : (distance + 1) * quarter_rows],
            ]
        )
        returned = shifted(outgoing, "seq", -distance)
        own_gk = own_gk + returned[0]
        own_gv = own_gv + returned[1]
    far_lse_rows = pick_rows(total_lse, far_offsets, cycle_size)
    dropped, grad_scores = score_terms(
        far_scores, far_allowed, far_lse_rows, far_delta, far_keep, far_all[1], far_grad
    )
    far_gq = jnp.einsum("hqk,hkd->hqd", grad_scores, far_all[0], precision=highest) * score_scale
    far_gv_all = jnp.einsum("hqk,hqd->hkd", dropped, far_grad, precision=highest)
    far_gk_all = jnp.einsum("hqk,hqd->hkd", grad_scores, far_q, precision=highest) * score_scale
    shares = lax.psum_scatter(
        jnp.stack([far_gk_all, far_gv_all]), "seq", scatter_dimension=2, tiled=True
    )
    far_gk = shares[0]
    far_gv = shares[1]
    grad_q = add_rows(add_rows(grad_q, mid_gq, mid_off, GROUP), far_gq, far_offsets, cycle_size)
    grad_k = add_rows(add_rows(grad_k, own_gk, mid_off, GROUP), far_gk, far_offsets, cycle_size)
    grad_v = add_rows(add_rows(grad_v, own_gv, mid_off, GROUP), far_gv, far_offsets, cycle_size)
    result = lax.all_to_all(
        jnp.stack([grad_q, grad_k, grad_v]), "head", split_axis=2, concat_axis=1, tiled=True
    )
    return (result[0], result[1], result[2])


def solution(mesh):
    placed = (
        P("head", "seq", None),
        P("head", "seq", None),
        P("head", "seq", None),
        P("head", "seq", None),
        P(None, ("seq", "head"), None),
        P("head", None),
        P("head"),
        P("head", "seq", None),
        P("head", "seq", None),
        P("head", None, None),
    )
    return jax.shard_map(
        per_device,
        mesh=mesh,
        in_specs=placed,
        out_specs=(
            P(None, ("seq", "head"), None),
            P(None, ("seq", "head"), None),
            P(None, ("seq", "head"), None),
        ),
        check_vma=False,
    )
```

profile of v0, /device:TPU:1, one launch (start us, length us, event | category | flops | bytes accessed | tf_op | source)
XLA Modules:
  0.0 363.3 jit_solution(801214255351252391)
XLA Ops:
  7.2 12.0 %all-to-all-start = ((f32[32,16,128]{2,1,0:T(8,128)}), f32[32,16,128]{2,1,0:T(8,128)S(1)}, u32[]{:S(2)}, u32[]{:S(2)}) async-start(f32[32,16,128]{2,1,0:T(8,128)} %param.14), calls=%async_computation | async-start | bytes 524288 | tf_op jit(solution)/shard_map/all_to_all | solution.py:82
  21.9 33.7 %all_gather.3 = f32[2,2,256,128]{3,2,1,0:T(8,128)S(1)} all-gather(f32[2,2,8,128]{3,2,1,0:T(8,128)S(1)} %pad_maximum_fusion.10), channel_id=1, replica_groups=mesh['seq'=32,'head'=16] {'seq'}, dimensions={2}, use_global_device_ids=true | all-gather | bytes 540672 | tf_op jit(solution)/shard_map/all_gather | solution.py:130
  58.3 0.8 constant_dynamic-slice_fusion.4
  61.2 0.7 reduce_max.32
  65.9 0.9 copy-done.6
  67.7 0.8 select_reduce_fusion.1
  68.5 4.0 %collective-permute-start.2 = (f32[2,2,64,128]{3,2,1,0:T(8,128)S(1)}, f32[2,2,64,128]{3,2,1,0:T(8,128)}, u32[]{:S(2)}, u32[]{:S(2)}) collective-permute-start(f32[2,2,64,128]{3,2,1,0:T(8,128)S(1)} %pad_maximum_fusion.5), channel_id=1, source_target_pairs={{0,48},{16,64},{32,80},{48,96},{64,112},{80,128},{96,144},{112,160... | collective-permute-start | bytes 393224 | tf_op jit(solution)/shard_map/ppermute | solution.py:17
  72.5 2.5 collective-permute-start.1
  75.0 1.8 collective-permute-start
  78.3 1.5 slice_bitcast_fusion.17
  84.1 0.8 select_reduce_fusion.11
  90.3 0.8 pad_maximum_fusion.1
  91.2 1.3 collective-permute-start.4
  92.5 1.3 collective-permute-start.5
  93.8 1.6 collective-permute-start.3
  97.5 1.3 collective-permute-done.4
  98.8 2.1 collective-permute-done.5
  101.1 212.0 %reduce-scatter.2.cloned.1.call-done = f32[2,2,8,128]{3,2,1,0:T(8,128)} async-done(((f32[2,2,256,128]{3,2,1,0:T(8,128)}), f32[2,2,8,128]{3,2,1,0:T(8,128)}) %reduce-scatter.2.cloned.1.call-update) | async-done | bytes 16400 | tf_op jit(solution)/shard_map/reduce_scatter | solution.py:171
  314.7 0.8 fusion.10
  315.5 1.0 fusion.5
  317.9 36.0 %all_to_all.33 = f32[3,2,256,128]{3,1,0,2:T(2,128)S(1)} all-to-all(f32[3,2,256,128]{3,1,0,2:T(2,128)S(1)} %copy.56), channel_id=1, replica_groups=mesh['seq'=32,'head'=16] {'head'}, dimensions={2} | all-to-all | bytes 1572864 | tf_op jit(solution)/shard_map/all_to_all | solution.py:179
  354.3 0.7 copy.59
  355.0 0.7 copy.58
  355.7 0.7 copy.57
  (198 shorter events, 28.7 us)
Async XLA Ops:
  7.2 51.9 %copy-start = (s32[2,256,64]{1,2,0:T(8,128)S(1)}, s32[2,256,64]{1,2,0:T(8,128)}, u32[]{:S(2)}) copy-start(s32[2,256,64]{1,2,0:T(8,128)} %param.19) | copy-start | bytes 393220
  7.2 58.7 %all-to-all-start = ((f32[32,16,128]{2,1,0:T(8,128)}), f32[32,16,128]{2,1,0:T(8,128)S(1)}, u32[]{:S(2)}, u32[]{:S(2)}) async-start(f32[32,16,128]{2,1,0:T(8,128)} %param.14), calls=%async_computation | async-start | bytes 524288 | tf_op jit(solution)/shard_map/all_to_all | solution.py:82
  19.2 294.0 %reduce-scatter.2.cloned.1.call-start = ((), (), s32[]{:S(2)}) async-start(), calls=%async_computation.3 | async-start | bytes 540672 | tf_op jit(solution)/shard_map/reduce_scatter | solution.py:171
  19.3 37.6 %copy-start.4 = (pred[256,256]{0,1:T(8,128)(4,1)}, pred[256,256]{0,1:T(8,128)(4,1)S(1)}, u32[]{:S(2)}) copy-start(pred[256,256]{0,1:T(8,128)(4,1)S(1)} %iota_compare_fusion) | copy-start | bytes 196612
  19.3 1.1 copy-start.17
  20.2 41.7 %copy-start.39 = (pred[2,4]{1,0:T(4,128)(4,1)}, pred[2,4]{1,0:T(4,128)(4,1)S(1)}, u32[]{:S(2)}) copy-start(pred[2,4]{1,0:T(4,128)(4,1)S(1)} %iota_compare_fusion.3) | copy-start | bytes 28
  20.3 38.9 %copy-start.42 = (pred[2,32]{1,0:T(4,128)(4,1)}, pred[2,32]{1,0:T(4,128)(4,1)S(1)}, u32[]{:S(2)}) copy-start(pred[2,32]{1,0:T(4,128)(4,1)S(1)} %iota_compare_fusion.4) | copy-start | bytes 196
  20.4 35.7 %copy-start.26 = (pred[8,256]{1,0:T(8,128)(4,1)}, pred[8,256]{1,0:T(8,128)(4,1)S(1)}, u32[]{:S(2)}) copy-start(pred[8,256]{1,0:T(8,128)(4,1)S(1)} %iota_compare_fusion.2) | copy-start | bytes 6148
  20.5 36.4 %copy-start.33 = (s32[256]{0:T(256)}, s32[256]{0:T(256)S(1)}, u32[]{:S(2)}) copy-start(s32[256]{0:T(256)S(1)} %shift_right_arithmetic.63) | copy-start | bytes 3076
  20.6 1.0 copy-start.2
  20.7 1.0 copy-start.1
  21.9 33.8 %copy-start.14 = (f32[2,8,128]{2,1,0:T(8,128)}, f32[2,8,128]{2,1,0:T(8,128)S(1)}, u32[]{:S(2)}) copy-start(f32[2,8,128]{2,1,0:T(8,128)S(1)} %get-tuple-element.12) | copy-start | bytes 24580
  56.9 4.4 %copy-start.28 = (f32[2,256]{1,0:T(2,128)}, f32[2,256]{1,0:T(2,128)S(1)}, u32[]{:S(2)}) copy-start(f32[2,256]{1,0:T(2,128)S(1)} %get-tuple-element.45) | copy-start | bytes 6148
  62.7 2.2 copy-start.13
  68.5 8.3 %copy-start.32 = (pred[2,16,16]{2,1,0:T(8,128)(4,1)S(1)}, pred[2,16,16]{2,1,0:T(8,128)(4,1)}, u32[]{:S(2)}) copy-start(pred[2,16,16]{2,1,0:T(8,128)(4,1)} %broadcast_in_dim.383) | copy-start | bytes 1540
  68.5 9.8 %collective-permute-start.2 = (f32[2,2,64,128]{3,2,1,0:T(8,128)S(1)}, f32[2,2,64,128]{3,2,1,0:T(8,128)}, u32[]{:S(2)}, u32[]{:S(2)}) collective-permute-start(f32[2,2,64,128]{3,2,1,0:T(8,128)S(1)} %pad_maximum_fusion.5), channel_id=1, source_target_pairs={{0,48},{16,64},{32,80},{48,96},{64,112},{80,128},{96,144},{112,160... | collective-permute-start | bytes 393224 | tf_op jit(solution)/shard_map/ppermute | solution.py:17
  72.5 7.3 %collective-permute-start.1 = (f32[2,2,64,128]{3,2,1,0:T(8,128)S(1)}, f32[2,2,64,128]{3,2,1,0:T(8,128)S(1)}, u32[]{:S(2)}, u32[]{:S(2)}) collective-permute-start(f32[2,2,64,128]{3,2,1,0:T(8,128)S(1)} %pad_maximum_fusion.5), channel_id=1, source_target_pairs={{0,32},{16,48},{32,64},{48,80},{64,96},{80,112},{96,128},{112,144}... | collective-permute-start | bytes 393224 | tf_op jit(solution)/shard_map/ppermute | solution.py:17
  75.0 5.5 %collective-permute-start = (f32[2,2,64,128]{3,2,1,0:T(8,128)S(1)}, f32[2,2,64,128]{3,2,1,0:T(8,128)S(1)}, u32[]{:S(2)}, u32[]{:S(2)}) collective-permute-start(f32[2,2,64,128]{3,2,1,0:T(8,128)S(1)} %pad_maximum_fusion.5), channel_id=1, source_target_pairs={{0,16},{16,32},{32,48},{48,64},{64,80},{80,96},{96,112},{112,128},... | collective-permute-start | bytes 393224 | tf_op jit(solution)/shard_map/ppermute | solution.py:17
  82.0 1.4 copy-start.7
  84.8 1.8 copy-start.44
  91.2 7.6 %collective-permute-start.4 = (f32[2,2,64,128]{3,2,1,0:T(8,128)S(1)}, f32[2,2,64,128]{3,2,1,0:T(8,128)S(1)}, u32[]{:S(2)}, u32[]{:S(2)}) collective-permute-start(f32[2,2,64,128]{3,2,1,0:T(8,128)S(1)} %pad_maximum_fusion.8), channel_id=1, source_target_pairs={{32,0},{48,16},{64,32},{80,48},{96,64},{112,80},{128,96},{144,112}... | collective-permute-start | bytes 393224 | tf_op jit(solution)/shard_map/ppermute | solution.py:17
  92.5 8.4 %collective-permute-start.5 = (f32[2,2,64,128]{3,2,1,0:T(8,128)S(1)}, f32[2,2,64,128]{3,2,1,0:T(8,128)S(1)}, u32[]{:S(2)}, u32[]{:S(2)}) collective-permute-start(f32[2,2,64,128]{3,2,1,0:T(8,128)S(1)} %pad_maximum_fusion.9), channel_id=1, source_target_pairs={{48,0},{64,16},{80,32},{96,48},{112,64},{128,80},{144,96},{160,112... | collective-permute-start | bytes 393224 | tf_op jit(solution)/shard_map/ppermute | solution.py:17
  93.8 1.9 copy-start.5
  93.8 7.2 %collective-permute-start.3 = (f32[2,2,64,128]{3,2,1,0:T(8,128)S(1)}, f32[2,2,64,128]{3,2,1,0:T(8,128)S(1)}, u32[]{:S(2)}, u32[]{:S(2)}) collective-permute-start(f32[2,2,64,128]{3,2,1,0:T(8,128)S(1)} %pad_maximum_fusion.7), channel_id=1, source_target_pairs={{16,0},{32,16},{48,32},{64,48},{80,64},{96,80},{112,96},{128,112},... | collective-permute-start | bytes 393224 | tf_op jit(solution)/shard_map/ppermute | solution.py:17
  (35 other events, 26.5 us)
Sparse Core Ops, SparseCore 0:
  91.3 221.8 reduce-scatter.1
where the time goes:
time: 364 us; the launch traced here: 363 us
  waiting for transfers between devices  216 us (59%)
  blocking collectives  69.7 us (19%)
  starting transfers between devices  24.5 us (7%)
  local copies, waits for them, and re-layouts  23.7 us (7%)
  between operations  14.9 us (4%)
  matrix products  8.36 us (2%)
  other arithmetic  6.66 us (2%)
    reduce_scatter x1, waiting for transfers between devices, per_device(): lax.psum_scatter(jnp.stack([far_gk_all, far_gv_all]), 'seq', scatter_dime...  212 us
    all_to_all x1, blocking collectives, per_device(): lax.all_to_all(jnp.stack([grad_q, grad_k, grad_v]), 'head', split_axis=2,...  36 us
    all_gather x1, blocking collectives, per_device(): lax.all_gather(jnp.stack([far_k, far_v]), 'seq', axis=2, tiled=True)  33.7 us
    ppermute x6, starting transfers between devices, shifted(): lax.ppermute(value, axis, [(source, source + steps) for source in range(i...  12.5 us
    all_to_all x1, starting transfers between devices, per_device(): lax.all_to_all(grad_output, 'head', split_axis=0, concat_axis=1, tiled=True)  12 us
    unnamed x103, local copies, waits for them, and re-layouts  8.8 us
  transfers between devices with their start and end apart: 8, of which 4 were waited for; matrix products, arithmetic and copies ran while one was open for 4% of the time, Pallas kernels for 0%

commit v1 on v0

v1 whole, which is shorter than its diff:
```python
import functools

import jax
import jax.numpy as jnp
from jax import lax
from jax.experimental import pallas as pl
from jax.experimental.pallas import tpu as pltpu
from jax.sharding import PartitionSpec as P

GROUP = 4
HALF = GROUP // 2
LANES = 128
KEEP_LEVEL = 7
KEEP_SCALE = 8.0 / 7.0
HIGHEST = lax.Precision.HIGHEST
NEG = -1e30


def dot(a, b, dims):
    return lax.dot_general(
        a, b, (dims, ((), ())), precision=HIGHEST, preferred_element_type=jnp.float32
    )


def dot_nt(a, b):
    return dot(a, b, ((1,), (1,)))


def dot_nn(a, b):
    return dot(a, b, ((1,), (0,)))


def dot_tn(a, b):
    return dot(a, b, ((0,), (0,)))


def wide(rows, lanes):
    return rows if lanes == LANES else jnp.concatenate([rows] * (lanes // LANES), axis=1)


def row_max(x):
    return jnp.broadcast_to(jnp.max(x, axis=1, keepdims=True), (x.shape[0], LANES))


def row_sum(x):
    return jnp.broadcast_to(jnp.sum(x, axis=1, keepdims=True), (x.shape[0], LANES))


def log_add(a, b):
    return jnp.maximum(a, b) + jnp.log(1.0 + jnp.exp(-jnp.abs(a - b)))


def masked_lse(scores, allowed):
    masked = jnp.where(allowed, scores, NEG)
    top = row_max(masked)
    return top + jnp.log(row_sum(jnp.exp(masked - wide(top, scores.shape[1]))))


def iotas(rows, cols):
    shape = (rows, cols)
    return lax.broadcasted_iota(jnp.int32, shape, 0), lax.broadcasted_iota(jnp.int32, shape, 1)


def spread_matrix(words):
    source, column = iotas(4 * words, 4 * words)
    chosen = (column % 4 == source // words) & (column // 4 == source % words)
    return jnp.where(chosen, 1.0, 0.0).astype(jnp.bfloat16)


def unpack_keep(words, spread, words_axis):
    kept = [
        jnp.where(((words >> (3 * level)) & 7) < KEEP_LEVEL, 1.0, 0.0) for level in range(4)
    ]
    flags = jnp.concatenate(kept, axis=words_axis).astype(jnp.bfloat16)
    whole = lax.dot_general(
        flags, spread, (((words_axis,), (0,)), ((), ())), preferred_element_type=jnp.float32
    )
    return whole * jnp.float32(KEEP_SCALE)


def pair_terms(scores, allowed, lse, delta, keep, grad_rows, values):
    cols = scores.shape[1]
    probs = jnp.where(allowed, jnp.exp(scores - wide(lse, cols)), 0.0)
    grad_probs = dot_nt(grad_rows, values) * keep
    return probs * keep, probs * (grad_probs - wide(delta, cols))


def place_info():
    place = lax.axis_index("seq")
    shifted = place + HALF
    return place, shifted // GROUP, shifted % GROUP


def prep_kernel(mid_off, far_off, k_ref, v_ref, mid_out, far_out):
    _, segment, _ = place_info()
    heads, rows, _ = k_ref.shape
    count = far_out.shape[0]
    far_rows = rows // count
    for head in range(heads):
        mid = mid_off[head, segment]
        far = far_off[head]
        for side, ref in enumerate((k_ref, v_ref)):
            mid_out[side, head] = ref[head, pl.ds(mid, rows // GROUP, stride=GROUP), :]
            picked = ref[head, pl.ds(far, far_rows, stride=count), :]
            for dest in range(count):
                far_out[dest, side * heads + head] = picked


def local_kernel(q_ref, k_ref, words_ref, scores_out, lse_out, keep_out, keep_buf):
    place, _, _ = place_info()
    heads, rows, width = q_ref.shape
    far_rows = keep_out.shape[1]
    spread = spread_matrix(words_ref.shape[1])
    row, col = iotas(rows, rows)
    for head in range(heads):
        scores = dot_nt(q_ref[head], k_ref[head]) * (width**-0.5)
        scores_out[head] = scores
        lse_out[head] = masked_lse(scores, row >= col)
        keep_buf[...] = unpack_keep(words_ref[head], spread, 0)
        keep_out[head] = keep_buf[pl.ds(place * far_rows, far_rows), :]


def mid_allowed(place, pos, quarter, cols):
    row, col = iotas(quarter, cols)
    return (col <= pos * quarter + row) & (place - pos + col // quarter >= 0)


def mid_kernel(
    mid_off, q_ref, g_ref, o_ref, lse_ref, kv0, kv1, kv2, kv3,
    g_out, delta_out, lse_out, scores_out, kv_out,
):
    place, segment, pos = place_info()
    heads, rows, width = q_ref.shape
    quarter = rows // GROUP
    for distance, ref in enumerate((kv0, kv1, kv2, kv3)):
        start = ((pos - distance) % GROUP) * quarter
        for side in range(2):
            for head in range(heads):
                kv_out[side, head, pl.ds(start, quarter), :] = ref[side, head]
    allowed = mid_allowed(place, pos, quarter, rows)
    for head in range(heads):
        g = g_ref[:, head].reshape(rows, width)
        g_out[head] = g
        delta_out[head] = row_sum(g * o_ref[head])
        picked = pl.ds(mid_off[head, segment], quarter, stride=GROUP)
        scores = dot_nt(q_ref[head, picked, :], kv_out[0, head]) * (width**-0.5)
        scores_out[head] = scores
        lse_out[head] = lse_ref[head]
        lse_out[head, picked, :] = log_add(lse_ref[head, picked, :], masked_lse(scores, allowed))


def far_kernel(
    far_off, q_ref, g_ref, delta_ref, lse_ref, keep_ref, kv_ref,
    lse_out, back_out, gq_out,
):
    place, _, _ = place_info()
    heads, rows, width = q_ref.shape
    count = kv_ref.shape[0]
    far_rows = rows // count
    scale = width**-0.5
    row, col = iotas(far_rows, rows)
    allowed = col <= place * far_rows + row
    for head in range(heads):
        picked = pl.ds(far_off[head], far_rows, stride=count)
        far_q = q_ref[head, picked, :]
        far_g = g_ref[head, picked, :]
        far_k = kv_ref[:, head].reshape(rows, width)
        far_v = kv_ref[:, heads + head].reshape(rows, width)
        scores = dot_nt(far_q, far_k) * scale
        lse = log_add(lse_ref[head, picked, :], masked_lse(scores, allowed))
        lse_out[head] = lse_ref[head]
        lse_out[head, picked, :] = lse
        dropped, grad_scores = pair_terms(
            scores, allowed, lse, delta_ref[head, picked, :], keep_ref[head], far_g, far_v
        )
        gq_out[head] = dot_nn(grad_scores, far_k) * scale
        gk = dot_tn(grad_scores, far_q) * scale
        gv = dot_tn(dropped, far_g)
        back_out[:, head] = gk.reshape(count, far_rows, width)
        back_out[:, heads + head] = gv.reshape(count, far_rows, width)


def mid_grad_kernel(
    mid_off, q_ref, g_ref, delta_ref, lse_ref, words_ref, scores_ref, kv_ref,
    gq_out, own_out, out1, out2, out3, gk_buf, gv_buf,
):
    place, segment, pos = place_info()
    heads, rows, width = q_ref.shape
    quarter = rows // GROUP
    scale = width**-0.5
    spread = spread_matrix(words_ref.shape[2])
    allowed = mid_allowed(place, pos, quarter, rows)
    for head in range(heads):
        picked = pl.ds(mid_off[head, segment], quarter, stride=GROUP)
        mid_q = q_ref[head, picked, :]
        mid_g = g_ref[head, picked, :]
        keep = unpack_keep(words_ref[head], spread, 1)
        dropped, grad_scores = pair_terms(
            scores_ref[head], allowed, lse_ref[head, picked, :], delta_ref[head, picked, :],
            keep, mid_g, kv_ref[1, head],
        )
        gq_out[head] = dot_nn(grad_scores, kv_ref[0, head]) * scale
        gk_buf[...] = dot_tn(grad_scores, mid_q) * scale
        gv_buf[...] = dot_tn(dropped, mid_g)
        for distance, ref in enumerate((own_out, out1, out2, out3)):
            block = pl.ds(((pos - distance) % GROUP) * quarter, quarter)
            ref[0, head] = gk_buf[block, :]
            ref[1, head] = gv_buf[block, :]


def local_grad_kernel(
    mid_off, far_off, q_ref, k_ref, v_ref, g_ref, delta_ref, lse_ref, words_ref, scores_ref,
    mid_gq, far_gq, gq_out, gk_out, gv_out,
):
    _, segment, _ = place_info()
    heads, rows, width = q_ref.shape
    quarter = rows // GROUP
    far_rows = far_gq.shape[1]
    scale = width**-0.5
    spread = spread_matrix(words_ref.shape[1])
    row, col = iotas(rows, rows)
    allowed = row >= col
    for head in range(heads):
        keep = unpack_keep(words_ref[head], spread, 0)
        dropped, grad_scores = pair_terms(
            scores_ref[head], allowed, lse_ref[head], delta_ref[head], keep,
            g_ref[head], v_ref[head],
        )
        gq_out[head] = dot_nn(grad_scores, k_ref[head]) * scale
        gk_out[head] = dot_tn(grad_scores, q_ref[head]) * scale
        gv_out[head] = dot_tn(dropped, g_ref[head])
        mid = pl.ds(mid_off[head, segment], quarter, stride=GROUP)
        far = pl.ds(far_off[head], far_rows, stride=rows // far_rows)
        gq_out[head, mid, :] = gq_out[head, mid, :] + mid_gq[head]
        gq_out[head, far, :] = gq_out[head, far, :] + far_gq[head]


def final_kernel(
    mid_off, far_off, gq_ref, gk_ref, gv_ref, own_ref, back1, back2, back3, far_ref,
    out, gk_buf, gv_buf,
):
    _, segment, _ = place_info()
    heads, rows, width = gq_ref.shape
    quarter = rows // GROUP
    count = far_ref.shape[0]
    far_rows = rows // count
    parts = out.shape[0]
    far_sum = jnp.sum(far_ref[...], axis=0)
    for head in range(heads):
        mid = pl.ds(mid_off[head, segment], quarter, stride=GROUP)
        far = pl.ds(far_off[head], far_rows, stride=count)
        out[:, 0, head] = gq_ref[head].reshape(parts, rows // parts, width)
        for side, (ref, buf) in enumerate(((gk_ref, gk_buf), (gv_ref, gv_buf))):
            buf[...] = ref[head]
            returned = own_ref[side, head] + back1[side, head] + back2[side, head] + back3[side, head]
            buf[mid, :] = buf[mid, :] + returned
            buf[far, :] = buf[far, :] + far_sum[side * heads + head]
            out[:, 1 + side, head] = buf[...].reshape(parts, rows // parts, width)


def call(kernel, scalars, arrays, outs, scratch=(), flops=0):
    smem = [pl.BlockSpec(memory_space=pltpu.SMEM)] * len(scalars)
    vmem = [pl.BlockSpec(memory_space=pltpu.VMEM)] * len(arrays)
    shapes = [jax.ShapeDtypeStruct(shape, jnp.float32) for shape in outs]
    moved = 4 * sum(a.size for a in arrays) + 4 * sum(s.size for s in shapes)
    result = pl.pallas_call(
        kernel,
        out_shape=shapes,
        in_specs=smem + vmem,
        out_specs=[pl.BlockSpec(memory_space=pltpu.VMEM)] * len(outs),
        scratch_shapes=[pltpu.VMEM(shape, jnp.float32) for shape in scratch],
        cost_estimate=pl.CostEstimate(flops=flops, transcendentals=0, bytes_accessed=moved),
        compiler_params=pltpu.CompilerParams(vmem_limit_bytes=40 * 1024 * 1024),
    )(*scalars, *arrays)
    return result


def shifted(value, steps):
    count = lax.axis_size("seq")
    first, last = max(0, -steps), min(count, count - steps)
    return lax.ppermute(value, "seq", [(source, source + steps) for source in range(first, last)])


def exchange(value, axis):
    return lax.all_to_all(value, axis, split_axis=0, concat_axis=0, tiled=True)


def per_device(q, k, v, output, grad_output, mid_off, far_off, drop_local, drop_mid, drop_far):
    heads, rows, width = q.shape
    count = lax.axis_size("seq")
    parts = lax.axis_size("head")
    quarter = rows // GROUP
    far_rows = rows // count
    whole = (heads, rows, width)
    pairs = (heads, rows, rows)
    mid_kv = (2, heads, quarter, width)
    far_kv = (count, 2 * heads, far_rows, width)
    block = 6 * 2 * heads * rows * rows * width

    g_parts = exchange(grad_output.reshape(parts, heads, rows // parts, width), "head")
    own_kv, far_send = call(prep_kernel, (mid_off, far_off), (k, v), (mid_kv, far_kv))
    received = [shifted(own_kv, distance) for distance in range(1, GROUP)]
    far_received = exchange(far_send, "seq")
    drop_local = jnp.swapaxes(drop_local, 1, 2)
    drop_far = jnp.swapaxes(drop_far, 1, 2)
    scores, lse, far_keep = call(
        local_kernel,
        (),
        (q, k, drop_far),
        (pairs, whole, (heads, far_rows, rows)),
        scratch=((rows, rows),),
        flops=block,
    )
    g, delta, lse, mid_scores, mid_kv_all = call(
        mid_kernel,
        (mid_off,),
        (q, g_parts, output, lse, own_kv, *received),
        (whole, whole, whole, (heads, quarter, rows), (2, heads, rows, width)),
        flops=block // GROUP,
    )
    lse, far_back, far_gq = call(
        far_kernel,
        (far_off,),
        (q, g, delta, lse, far_keep, far_received),
        (whole, far_kv, (heads, far_rows, width)),
        flops=block // GROUP,
    )
    far_returned = exchange(far_back, "seq")
    mid_gq, mid_own, *outgoing = call(
        mid_grad_kernel,
        (mid_off,),
        (q, g, delta, lse, drop_mid, mid_scores, mid_kv_all),
        ((heads, quarter, width), mid_kv, mid_kv, mid_kv, mid_kv),
        scratch=((rows, width), (rows, width)),
        flops=block,
    )
    returned = [shifted(value, -distance - 1) for distance, value in enumerate(outgoing)]
    gq, gk, gv = call(
        local_grad_kernel,
        (mid_off, far_off),
        (q, k, v, g, delta, lse, drop_local, scores, mid_gq, far_gq),
        (whole, whole, whole),
        flops=4 * block,
    )
    (stacked,) = call(
        final_kernel,
        (mid_off, far_off),
        (gq, gk, gv, mid_own, *returned, far_returned),
        ((parts, 3, heads, rows // parts, width),),
        scratch=((rows, width), (rows, width)),
    )
    result = exchange(stacked, "head")
    shape = (parts * heads, rows // parts, width)
    return tuple(result[:, part].reshape(shape) for part in range(3))


def solution(mesh):
    tokens = P(None, ("seq", "head"), None)
    placed = P("head", "seq", None)
    return jax.shard_map(
        per_device,
        mesh=mesh,
        in_specs=(
            placed, placed, placed, placed, tokens,
            P("head", None), P("head"), placed, placed, P("head", None, None),
        ),
        out_specs=(tokens, tokens, tokens),
        check_vma=False,
    )
```

time: 364 us -> 121 us (0.33)
  the two profiles are of different devices: /device:TPU:1 before, /device:TPU:27 now
where the time goes in v1:
time: 121 us; the launch traced here: 120 us
  starting transfers between devices  52.3 us (43%)
  blocking collectives  26.7 us (22%)
  waiting for transfers between devices  24 us (20%)
  Pallas kernels  12.7 us (10%)
  local copies, waits for them, and re-layouts  3.72 us (3%)
    all_to_all x3, starting transfers between devices, exchange(): return lax.all_to_all(value, axis, split_axis=0, concat_axis=0, tiled=True)  31.1 us
    all_to_all x1, blocking collectives, exchange(): return lax.all_to_all(value, axis, split_axis=0, concat_axis=0, tiled=True)  26.7 us
    ppermute x6, starting transfers between devices, shifted(): lax.ppermute(value, 'seq', [(source, source + steps) for source in range(...  21.3 us
    ppermute x6, waiting for transfers between devices, shifted(): lax.ppermute(value, 'seq', [(source, source + steps) for source in range(...  15.1 us
    pallas_call x7, Pallas kernels, call(): pl.pallas_call(kernel, out_shape=shapes, in_specs=smem + vmem, out_specs=...  12.7 us
    all_to_all x3, waiting for transfers between devices, exchange(): return lax.all_to_all(value, axis, split_axis=0, concat_axis=0, tiled=True)  8.92 us
    unnamed x26, local copies, waits for them, and re-layouts  2.82 us
  transfers between devices with their start and end apart: 9, of which 5 were waited for; matrix products, arithmetic and copies ran while one was open for 0% of the time, Pallas kernels for 7%

profile of v1, /device:TPU:27, one launch (start us, length us, event | category | flops | bytes accessed | tf_op | source)
XLA Modules:
  0.0 120.3 jit_solution(2154780055916788266)
XLA Ops:
  0.7 11.1 %all-to-all-start = ((f32[16,2,16,128]{3,2,1,0:T(8,128)}), f32[16,2,16,128]{3,2,1,0:T(8,128)S(1)}, u32[]{:S(2)}, u32[]{:S(2)}) async-start(f32[16,2,16,128]{3,2,1,0:T(8,128)} %bitcast.8), calls=%async_computation | async-start | bytes 524288 | tf_op jit(solution)/shard_map/all_to_all | solution.py:285
  11.8 0.7 copy-done.5
  13.2 1.4 %shard_map.122 = (f32[2,2,64,128]{3,2,1,0:T(8,128)S(1)}, f32[32,4,8,128]{3,2,1,0:T(8,128)}) custom-call(s32[2,9]{1,0:T(2,128)S(1)} %copy-done.5, s32[2]{0:T(128)S(1)} %copy-done.7, f32[2,256,128]{2,1,0:T(8,128)S(1)} %copy-done.1, f32[2,256,128]{2,1,0:T(8,128)S(1)} %copy-done.2), custom_call_target="tpu_custom_call" | custom-call | bytes 1179648 | tf_op jit(solution)/shard_map/pallas_call | solution.py:266
  14.6 8.9 %all-to-all-done.g_ref = f32[16,2,16,128]{3,2,1,0:T(8,128)S(1)} async-done(((f32[16,2,16,128]{3,2,1,0:T(8,128)}), f32[16,2,16,128]{3,2,1,0:T(8,128)S(1)}, u32[]{:S(2)}, u32[]{:S(2)}) %all-to-all-start) | async-done | bytes 262176 | tf_op jit(solution)/shard_map/all_to_all | solution.py:285
  23.5 9.5 %all-to-all-start.1 = ((f32[32,4,8,128]{3,2,1,0:T(8,128)}), f32[32,4,8,128]{3,2,1,0:T(8,128)S(1)}, u32[]{:S(2)}, u32[]{:S(2)}) async-start(f32[32,4,8,128]{3,2,1,0:T(8,128)} %get-tuple-element.30), calls=%async_computation.1 | async-start | bytes 1048576 | tf_op jit(solution)/shard_map/all_to_all | solution.py:285
  33.0 4.3 %collective-permute-start.2 = (f32[2,2,64,128]{3,2,1,0:T(8,128)S(1)}, f32[2,2,64,128]{3,2,1,0:T(8,128)S(1)}, u32[]{:S(2)}, u32[]{:S(2)}) collective-permute-start(f32[2,2,64,128]{3,2,1,0:T(8,128)S(1)} %get-tuple-element.25.kv0), channel_id=1, source_target_pairs={{0,48},{16,64},{32,80},{48,96},{64,112},{80,128},{96,144},{112,160... | collective-permute-start | bytes 393224 | tf_op jit(solution)/shard_map/ppermute | solution.py:281
  37.3 4.0 %collective-permute-start.1 = (f32[2,2,64,128]{3,2,1,0:T(8,128)S(1)}, f32[2,2,64,128]{3,2,1,0:T(8,128)S(1)}, u32[]{:S(2)}, u32[]{:S(2)}) collective-permute-start(f32[2,2,64,128]{3,2,1,0:T(8,128)S(1)} %get-tuple-element.25.kv0), channel_id=1, source_target_pairs={{0,32},{16,48},{32,64},{48,80},{64,96},{80,112},{96,128},{112,144}... | collective-permute-start | bytes 393224 | tf_op jit(solution)/shard_map/ppermute | solution.py:281
  41.3 3.4 %collective-permute-start = (f32[2,2,64,128]{3,2,1,0:T(8,128)S(1)}, f32[2,2,64,128]{3,2,1,0:T(8,128)S(1)}, u32[]{:S(2)}, u32[]{:S(2)}) collective-permute-start(f32[2,2,64,128]{3,2,1,0:T(8,128)S(1)} %get-tuple-element.25.kv0), channel_id=1, source_target_pairs={{0,16},{16,32},{32,48},{48,64},{64,80},{80,96},{96,112},{112,128},... | collective-permute-start | bytes 393224 | tf_op jit(solution)/shard_map/ppermute | solution.py:281
  44.8 0.9 shard_map.121
  45.6 0.8 copy-done.11
  46.4 3.4 %collective-permute-done.2.kv3 = f32[2,2,64,128]{3,2,1,0:T(8,128)S(1)} collective-permute-done((f32[2,2,64,128]{3,2,1,0:T(8,128)S(1)}, f32[2,2,64,128]{3,2,1,0:T(8,128)S(1)}, u32[]{:S(2)}, u32[]{:S(2)}) %collective-permute-start.2) | collective-permute-done | bytes 131104 | tf_op jit(solution)/shard_map/ppermute | solution.py:281
  49.9 3.3 %collective-permute-done.1.kv2 = f32[2,2,64,128]{3,2,1,0:T(8,128)S(1)} collective-permute-done((f32[2,2,64,128]{3,2,1,0:T(8,128)S(1)}, f32[2,2,64,128]{3,2,1,0:T(8,128)S(1)}, u32[]{:S(2)}, u32[]{:S(2)}) %collective-permute-start.1) | collective-permute-done | bytes 131104 | tf_op jit(solution)/shard_map/ppermute | solution.py:281
  53.1 1.2 %shard_map.123 = (f32[2,256,128]{2,1,0:T(8,128)S(1)}, f32[2,256,128]{2,1,0:T(8,128)S(1)}, f32[2,256,128]{2,1,0:T(8,128)S(1)}, f32[2,64,256]{2,1,0:T(8,128)S(1)}, f32[2,2,256,128]{3,2,1,0:T(8,128)S(1)}) custom-call(s32[2,9]{1,0:T(2,128)S(1)} %copy-done.6, f32[2,256,128]{2,1,0:T(8,128)S(1)} %copy-done, f32[16,2,16,128]{3,2,1,0:T(8,128)S(1)} %all-to-all-done.g_ref, ...), custom_call_target="tpu_custom_call" | custom-call | flops 50331648 | bytes 3014656 | tf_op jit(solution)/shard_map/pallas_call | solution.py:266
  55.0 3.1 %shard_map.124 = (f32[2,256,128]{2,1,0:T(8,128)S(1)}, f32[32,4,8,128]{3,2,1,0:T(8,128)}, f32[2,8,128]{2,1,0:T(8,128)S(1)}) custom-call(s32[2]{0:T(128)S(1)} %copy-done.8, f32[2,256,128]{2,1,0:T(8,128)S(1)} %copy-done, f32[2,256,128]{2,1,0:T(8,128)S(1)} %get-tuple-element.26.g_ref, f32[2,256,128]{2,1,0:T(8,128)S(1)} %get-tuple-element.27.delta_ref, ...), custom_call_target="tpu_custom_call" | custom-call | flops 50331648 | bytes 2383872 | tf_op jit(solution)/shard_map/pallas_call | solution.py:266
  58.1 10.4 %all-to-all-start.2 = ((f32[32,4,8,128]{3,2,1,0:T(8,128)}), f32[32,4,8,128]{3,2,1,0:T(8,128)S(1)}, u32[]{:S(2)}, u32[]{:S(2)}) async-start(f32[32,4,8,128]{3,2,1,0:T(8,128)} %get-tuple-element.44), calls=%async_computation.2 | async-start | bytes 1048576 | tf_op jit(solution)/shard_map/all_to_all | solution.py:285
  68.6 1.9 %shard_map.125 = (f32[2,64,128]{2,1,0:T(8,128)S(1)}, f32[2,2,64,128]{3,2,1,0:T(8,128)S(1)}, f32[2,2,64,128]{3,2,1,0:T(8,128)S(1)}, f32[2,2,64,128]{3,2,1,0:T(8,128)S(1)}, f32[2,2,64,128]{3,2,1,0:T(8,128)S(1)}) custom-call(s32[2,9]{1,0:T(2,128)S(1)} %copy-done.6, f32[2,256,128]{2,1,0:T(8,128)S(1)} %copy-done, f32[2,256,128]{2,1,0:T(8,128)S(1)} %get-tuple-element.26.g_ref, ...), custom_call_target="tpu_custom_call" | custom-call | flops 201326592 | bytes 2326528 | tf_op jit(solution)/shard_map/pallas_call | solution.py:266
  70.6 2.2 %collective-permute-start.3 = (f32[2,2,64,128]{3,2,1,0:T(8,128)S(1)}, f32[2,2,64,128]{3,2,1,0:T(8,128)S(1)}, u32[]{:S(2)}, u32[]{:S(2)}) collective-permute-start(f32[2,2,64,128]{3,2,1,0:T(8,128)S(1)} %get-tuple-element.41), channel_id=1, source_target_pairs={{16,0},{32,16},{48,32},{64,48},{80,64},{96,80},{112,96},{128,112},... | collective-permute-start | bytes 393224 | tf_op jit(solution)/shard_map/ppermute | solution.py:281
  72.8 4.0 %collective-permute-start.4 = (f32[2,2,64,128]{3,2,1,0:T(8,128)S(1)}, f32[2,2,64,128]{3,2,1,0:T(8,128)S(1)}, u32[]{:S(2)}, u32[]{:S(2)}) collective-permute-start(f32[2,2,64,128]{3,2,1,0:T(8,128)S(1)} %get-tuple-element.42), channel_id=1, source_target_pairs={{32,0},{48,16},{64,32},{80,48},{96,64},{112,80},{128,96},{144,112}... | collective-permute-start | bytes 393224 | tf_op jit(solution)/shard_map/ppermute | solution.py:281
  76.8 3.4 %collective-permute-start.5 = (f32[2,2,64,128]{3,2,1,0:T(8,128)S(1)}, f32[2,2,64,128]{3,2,1,0:T(8,128)S(1)}, u32[]{:S(2)}, u32[]{:S(2)}) collective-permute-start(f32[2,2,64,128]{3,2,1,0:T(8,128)S(1)} %get-tuple-element.43), channel_id=1, source_target_pairs={{48,0},{64,16},{80,32},{96,48},{112,64},{128,80},{144,96},{160,112... | collective-permute-start | bytes 393224 | tf_op jit(solution)/shard_map/ppermute | solution.py:281
  80.2 3.3 %shard_map.126 = (f32[2,256,128]{2,1,0:T(8,128)S(1)}, f32[2,256,128]{2,1,0:T(8,128)S(1)}, f32[2,256,128]{2,1,0:T(8,128)S(1)}) custom-call(s32[2,9]{1,0:T(2,128)S(1)} %copy-done.6, s32[2]{0:T(128)S(1)} %copy-done.8, f32[2,256,128]{2,1,0:T(8,128)S(1)} %copy-done, f32[2,256,128]{2,1,0:T(8,128)S(1)} %copy-done.1, f32[2,256,128]{2,1,0:T(8,128)S(1)} %copy-done.2, ...), custom_call_target="tpu_custom_call" | custom-call | flops 805306368 | bytes 3088384 | tf_op jit(solution)/shard_map/pallas_call | solution.py:266
  83.8 8.1 %collective-permute-done.5.back3 = f32[2,2,64,128]{3,2,1,0:T(8,128)S(1)} collective-permute-done((f32[2,2,64,128]{3,2,1,0:T(8,128)S(1)}, f32[2,2,64,128]{3,2,1,0:T(8,128)S(1)}, u32[]{:S(2)}, u32[]{:S(2)}) %collective-permute-start.5) | collective-permute-done | bytes 131104 | tf_op jit(solution)/shard_map/ppermute | solution.py:281
  92.0 0.7 shard_map.127
  92.7 26.7 %all_to_all.20 = f32[16,3,2,16,128]{4,3,2,1,0:T(8,128)S(1)} all-to-all(f32[16,3,2,16,128]{4,3,2,1,0:T(8,128)S(1)} %shard_map.127), channel_id=1, replica_groups=mesh['seq'=32,'head'=16] {'head'}, dimensions={0} | all-to-all | bytes 1572864 | tf_op jit(solution)/shard_map/all_to_all | solution.py:285
  119.4 0.9 fusion
  (29 shorter events, 1.7 us)
Async XLA Ops:
  0.6 11.2 %copy-start.1 = (f32[2,256,128]{2,1,0:T(8,128)S(1)}, f32[2,256,128]{2,1,0:T(8,128)}, u32[]{:S(2)}) copy-start(f32[2,256,128]{2,1,0:T(8,128)} %k_ref.5) | copy-start | bytes 786436
  0.6 11.2 %copy-start.2 = (f32[2,256,128]{2,1,0:T(8,128)S(1)}, f32[2,256,128]{2,1,0:T(8,128)}, u32[]{:S(2)}) copy-start(f32[2,256,128]{2,1,0:T(8,128)} %v_ref.3) | copy-start | bytes 786436
  0.7 22.9 %all-to-all-start = ((f32[16,2,16,128]{3,2,1,0:T(8,128)}), f32[16,2,16,128]{3,2,1,0:T(8,128)S(1)}, u32[]{:S(2)}, u32[]{:S(2)}) async-start(f32[16,2,16,128]{3,2,1,0:T(8,128)} %bitcast.8), calls=%async_computation | async-start | bytes 524288 | tf_op jit(solution)/shard_map/all_to_all | solution.py:285
  11.8 0.7 copy-start.5
  12.5 0.7 copy-start.7
  23.5 21.2 %copy-start = (f32[2,256,128]{2,1,0:T(8,128)S(1)}, f32[2,256,128]{2,1,0:T(8,128)}, u32[]{:S(2)}) copy-start(f32[2,256,128]{2,1,0:T(8,128)} %q_ref.9) | copy-start | bytes 786436
  23.5 21.2 %copy-start.9 = (s32[2,256,64]{1,2,0:T(8,128)S(1)}, s32[2,256,64]{1,2,0:T(8,128)}, u32[]{:S(2)}) copy-start(s32[2,256,64]{1,2,0:T(8,128)} %param.19) | copy-start | bytes 393220
  23.5 30.8 %all-to-all-start.1 = ((f32[32,4,8,128]{3,2,1,0:T(8,128)}), f32[32,4,8,128]{3,2,1,0:T(8,128)S(1)}, u32[]{:S(2)}, u32[]{:S(2)}) async-start(f32[32,4,8,128]{3,2,1,0:T(8,128)} %get-tuple-element.30), calls=%async_computation.1 | async-start | bytes 1048576 | tf_op jit(solution)/shard_map/all_to_all | solution.py:285
  33.0 16.8 %collective-permute-start.2 = (f32[2,2,64,128]{3,2,1,0:T(8,128)S(1)}, f32[2,2,64,128]{3,2,1,0:T(8,128)S(1)}, u32[]{:S(2)}, u32[]{:S(2)}) collective-permute-start(f32[2,2,64,128]{3,2,1,0:T(8,128)S(1)} %get-tuple-element.25.kv0), channel_id=1, source_target_pairs={{0,48},{16,64},{32,80},{48,96},{64,112},{80,128},{96,144},{112,160... | collective-permute-start | bytes 393224 | tf_op jit(solution)/shard_map/ppermute | solution.py:281
  37.3 15.8 %collective-permute-start.1 = (f32[2,2,64,128]{3,2,1,0:T(8,128)S(1)}, f32[2,2,64,128]{3,2,1,0:T(8,128)S(1)}, u32[]{:S(2)}, u32[]{:S(2)}) collective-permute-start(f32[2,2,64,128]{3,2,1,0:T(8,128)S(1)} %get-tuple-element.25.kv0), channel_id=1, source_target_pairs={{0,32},{16,48},{32,64},{48,80},{64,96},{80,112},{96,128},{112,144}... | collective-permute-start | bytes 393224 | tf_op jit(solution)/shard_map/ppermute | solution.py:281
  41.3 11.8 %collective-permute-start = (f32[2,2,64,128]{3,2,1,0:T(8,128)S(1)}, f32[2,2,64,128]{3,2,1,0:T(8,128)S(1)}, u32[]{:S(2)}, u32[]{:S(2)}) collective-permute-start(f32[2,2,64,128]{3,2,1,0:T(8,128)S(1)} %get-tuple-element.25.kv0), channel_id=1, source_target_pairs={{0,16},{16,32},{32,48},{48,64},{64,80},{80,96},{96,112},{112,128},... | collective-permute-start | bytes 393224 | tf_op jit(solution)/shard_map/ppermute | solution.py:281
  44.7 8.4 %copy-start.3 = (f32[2,256,128]{2,1,0:T(8,128)S(1)}, f32[2,256,128]{2,1,0:T(8,128)}, u32[]{:S(2)}) copy-start(f32[2,256,128]{2,1,0:T(8,128)} %o_ref.1) | copy-start | bytes 786436
  45.6 0.8 copy-start.11
  46.4 6.7 %copy-start.6 = (s32[2,9]{1,0:T(2,128)S(1)}, s32[2,9]{1,0:T(2,128)}, u32[]{:S(2)}) copy-start(s32[2,9]{1,0:T(2,128)} %mid_off.9) | copy-start | bytes 220
  54.3 0.7 copy-start.8
  58.1 10.4 %copy-start.4 = (s32[2,64,64]{2,1,0:T(8,128)S(1)}, s32[2,64,64]{2,1,0:T(8,128)}, u32[]{:S(2)}) copy-start(s32[2,64,64]{2,1,0:T(8,128)} %words_ref.1) | copy-start | bytes 98308
  58.1 33.8 %all-to-all-start.2 = ((f32[32,4,8,128]{3,2,1,0:T(8,128)}), f32[32,4,8,128]{3,2,1,0:T(8,128)S(1)}, u32[]{:S(2)}, u32[]{:S(2)}) async-start(f32[32,4,8,128]{3,2,1,0:T(8,128)} %get-tuple-element.44), calls=%async_computation.2 | async-start | bytes 1048576 | tf_op jit(solution)/shard_map/all_to_all | solution.py:285
  68.6 11.6 %copy-start.10 = (s32[2,256,64]{1,2,0:T(8,128)S(1)}, s32[2,256,64]{1,2,0:T(8,128)}, u32[]{:S(2)}) copy-start(s32[2,256,64]{1,2,0:T(8,128)} %param.17) | copy-start | bytes 393220
  68.6 11.6 %copy-start.12 = (f32[2,256,256]{2,1,0:T(8,128)S(1)}, f32[2,256,256]{2,1,0:T(8,128)}, u32[]{:S(2)}) copy-start(f32[2,256,256]{2,1,0:T(8,128)} %copy-done.11) | copy-start | bytes 1572868
  70.6 12.9 %collective-permute-start.3 = (f32[2,2,64,128]{3,2,1,0:T(8,128)S(1)}, f32[2,2,64,128]{3,2,1,0:T(8,128)S(1)}, u32[]{:S(2)}, u32[]{:S(2)}) collective-permute-start(f32[2,2,64,128]{3,2,1,0:T(8,128)S(1)} %get-tuple-element.41), channel_id=1, source_target_pairs={{16,0},{32,16},{48,32},{64,48},{80,64},{96,80},{112,96},{128,112},... | collective-permute-start | bytes 393224 | tf_op jit(solution)/shard_map/ppermute | solution.py:281
  72.8 11.1 %collective-permute-start.4 = (f32[2,2,64,128]{3,2,1,0:T(8,128)S(1)}, f32[2,2,64,128]{3,2,1,0:T(8,128)S(1)}, u32[]{:S(2)}, u32[]{:S(2)}) collective-permute-start(f32[2,2,64,128]{3,2,1,0:T(8,128)S(1)} %get-tuple-element.42), channel_id=1, source_target_pairs={{32,0},{48,16},{64,32},{80,48},{96,64},{112,80},{128,96},{144,112}... | collective-permute-start | bytes 393224 | tf_op jit(solution)/shard_map/ppermute | solution.py:281
  76.8 15.2 %collective-permute-start.5 = (f32[2,2,64,128]{3,2,1,0:T(8,128)S(1)}, f32[2,2,64,128]{3,2,1,0:T(8,128)S(1)}, u32[]{:S(2)}, u32[]{:S(2)}) collective-permute-start(f32[2,2,64,128]{3,2,1,0:T(8,128)S(1)} %get-tuple-element.43), channel_id=1, source_target_pairs={{48,0},{64,16},{80,32},{96,48},{112,64},{128,80},{144,96},{160,112... | collective-permute-start | bytes 393224 | tf_op jit(solution)/shard_map/ppermute | solution.py:281

commit v2 on v1

v2 whole, which is shorter than its diff:
```python
import math

import jax
import jax.numpy as jnp
from jax import lax
from jax.experimental import pallas as pl
from jax.experimental.pallas import tpu as pltpu
from jax.sharding import PartitionSpec as P

GROUP = 4
HALF = GROUP // 2
LANES = 128
ACROSS = 4
KEEP_LEVEL = 7
KEEP_SCALE = 8.0 / 7.0
HIGHEST = lax.Precision.HIGHEST
NEG = -1e30


def dot(a, b, dims):
    return lax.dot_general(
        a, b, (dims, ((), ())), precision=HIGHEST, preferred_element_type=jnp.float32
    )


def dot_nt(a, b):
    return dot(a, b, ((1,), (1,)))


def dot_nn(a, b):
    return dot(a, b, ((1,), (0,)))


def dot_tn(a, b):
    return dot(a, b, ((0,), (0,)))


def wide(rows, lanes):
    if lanes <= LANES:
        return rows[:, :lanes]
    return jnp.concatenate([rows] * (lanes // LANES), axis=1)


def row_max(x):
    return jnp.broadcast_to(jnp.max(x, axis=1, keepdims=True), (x.shape[0], LANES))


def row_sum(x):
    return jnp.broadcast_to(jnp.sum(x, axis=1, keepdims=True), (x.shape[0], LANES))


def log_add(a, b):
    return jnp.maximum(a, b) + jnp.log(1.0 + jnp.exp(-jnp.abs(a - b)))


def masked_lse(scores, allowed):
    masked = jnp.where(allowed, scores, NEG)
    top = row_max(masked)
    return top + jnp.log(row_sum(jnp.exp(masked - wide(top, scores.shape[1]))))


def iotas(rows, cols):
    shape = (rows, cols)
    return lax.broadcasted_iota(jnp.int32, shape, 0), lax.broadcasted_iota(jnp.int32, shape, 1)


def spread_matrix(words, first, cols):
    source, column = iotas(4 * words, cols)
    column = column + first
    chosen = (column % 4 == source // words) & (column // 4 == source % words)
    return jnp.where(chosen, 1.0, 0.0).astype(jnp.bfloat16)


def keep_flags(words, axis):
    kept = [
        jnp.where(((words >> (3 * level)) & 7) < KEEP_LEVEL, 1.0, 0.0) for level in range(4)
    ]
    return jnp.concatenate(kept, axis=axis).astype(jnp.bfloat16)


def spread_flags(flags, spread, axis):
    whole = lax.dot_general(
        flags, spread, (((axis,), (0,)), ((), ())), preferred_element_type=jnp.float32
    )
    return whole * jnp.float32(KEEP_SCALE)


def pair_terms(scores, allowed, lse, delta, keep, grad_rows, values):
    cols = scores.shape[1]
    probs = jnp.where(allowed, jnp.exp(scores - wide(lse, cols)), 0.0)
    grad_probs = dot_nt(grad_rows, values) * keep
    return probs * keep, probs * (grad_probs - wide(delta, cols))


def place_info():
    place = lax.axis_index("seq")
    shifted = place + HALF
    return place, shifted // GROUP, shifted % GROUP


def place_masks(place, pos, quarter, rows):
    row, col = iotas(quarter, rows)
    return (col <= pos * quarter + row) & (place - pos + col // quarter >= 0)


def prep_kernel(mid_off, x, o):
    _, segment, _ = place_info()
    heads, rows, _ = x.k.shape
    for head in range(heads):
        picked = pl.ds(mid_off[head, segment], rows // GROUP, stride=GROUP)
        o.own_kv[0, head] = x.k[head, picked, :]
        o.own_kv[1, head] = x.v[head, picked, :]


def local_kernel(mid_off, far_off, x, o):
    heads, rows, width = x.q.shape
    row, col = iotas(rows, rows)
    for head in range(heads):
        o.lse[head] = masked_lse(dot_nt(x.q[head], x.k[head]) * (width**-0.5), row >= col)


def gather_mid(x, side, head, buf):
    _, _, pos = place_info()
    quarter = x.kv0.shape[2]
    for distance in range(GROUP):
        start = ((pos - distance) % GROUP) * quarter
        buf[pl.ds(start, quarter), :] = x[f"kv{distance}"][side, head]


def mid_kernel(mid_off, far_off, x, o, buf):
    place, segment, pos = place_info()
    heads, rows, width = x.q.shape
    quarter = rows // GROUP
    count, sends = lax.axis_size("seq"), o.far_send.shape[0]
    far_rows = rows // count
    line = place // (count // sends)
    for head in range(heads):
        o.g[head] = x.g_parts[:, head].reshape(rows, width)
        far = pl.ds(far_off[head], far_rows, stride=count)
        far_q, far_k, far_v = x.q[head, far, :], x.k[head, far, :], x.v[head, far, :]
        far_g = o.g[head, far, :]
        for dest in range(sends):
            o.far_send[dest, head] = far_k
            o.far_send[dest, heads + head] = jnp.where(dest >= line, far_v, far_q)
            o.far_send[dest, 2 * heads + head] = far_g
    allowed = place_masks(place, pos, quarter, rows)
    _, lane = iotas(far_rows, LANES)
    part = lane // (LANES // (2 * heads))
    row_facts = jnp.zeros((far_rows, LANES), jnp.float32)
    for head in range(heads):
        o.delta[head] = row_sum(o.g[head] * x.output[head])
        gather_mid(x, 0, head, buf)
        mid = pl.ds(mid_off[head, segment], quarter, stride=GROUP)
        far = pl.ds(far_off[head], far_rows, stride=count)
        scores = dot_nt(x.q[head, mid, :], buf[...]) * (width**-0.5)
        o.lse[head] = x.lse[head]
        o.lse[head, mid, :] = log_add(x.lse[head, mid, :], masked_lse(scores, allowed))
        row_facts = jnp.where(part == 2 * head, o.lse[head, far, :], row_facts)
        row_facts = jnp.where(part == 2 * head + 1, o.delta[head, far, :], row_facts)
    for dest in range(sends):
        o.far_send[dest, 3 * heads] = row_facts


def relay_kernel(mid_off, far_off, x, o):
    place, _, _ = place_info()
    heads, rows, _ = x.q.shape
    sends = o.relay.shape[0]
    lines = x.column.shape[0]
    for dest in range(sends):
        o.relay[dest] = x.column[...]
    for head in range(heads):
        far_q = x.q[head, pl.ds(far_off[head], rows // (lines * sends), stride=lines * sends), :]
        far_v = x.column[place // sends, heads + head]
        for dest in range(sends):
            o.relay[dest, place // sends, heads + head] = jnp.where(
                dest >= place % sends, far_v, far_q
            )


def rows_kernel(mid_off, far_off, x, o):
    _, segment, _ = place_info()
    heads, rows, width = x.q.shape
    quarter = rows // GROUP
    words = x.drop_mid.shape[2]
    _, lane = iotas(quarter, LANES)
    for head in range(heads):
        mid = pl.ds(mid_off[head, segment], quarter, stride=GROUP)
        o.rows[0, head] = x.q[head, mid, :]
        o.rows[1, head] = x.g[head, mid, :]
        o.rows[2, head] = jnp.where(
            lane < words + (LANES - words) // 2, x.lse[head, mid, :], x.delta[head, mid, :]
        )
        o.rows[2, head, :, 0:words] = x.drop_mid[head].astype(jnp.float32)


def terms_kernel(mid_off, far_off, x, o, buf, keep_buf):
    place, segment, _ = place_info()
    heads, rows, width = x.q.shape
    scale = width**-0.5
    words = x.drop_local.shape[1]
    far_rows = o.far_keep.shape[1]
    spread = spread_matrix(words, 0, rows)
    far_spread = spread_matrix(words, place * far_rows, far_rows)
    for head in range(heads):
        o.scores[head] = dot_nt(x.q[head], x.k[head]) * scale
        keep = spread_flags(keep_flags(x.drop_local[head], 0), spread, 0)
        o.keep[head] = keep
        o.terms[head] = dot_nt(x.g[head], x.v[head]) * keep - wide(x.delta[head], rows)
        mid = pl.ds(mid_off[head, segment], rows // GROUP, stride=GROUP)
        gather_mid(x, 0, head, buf)
        o.mid_k[head] = buf[...]
        o.mid_scores[head] = dot_nt(x.q[head, mid, :], buf[...]) * scale
        gather_mid(x, 1, head, buf)
        keep = spread_flags(keep_flags(x.drop_mid[head], 1), spread, 1)
        o.mid_terms[head] = dot_nt(x.g[head, mid, :], buf[...]) * keep - wide(
            x.delta[head, mid, :], rows
        )
        flags = keep_flags(x.drop_far[head], 0)
        keep_buf[...] = spread_flags(flags, spread, 0)
        o.far_keep[head] = keep_buf[pl.ds(place * far_rows, far_rows), :]
        o.far_cols[:, head * far_rows : (head + 1) * far_rows] = spread_flags(flags, far_spread, 0)


def fact(facts, index, share):
    return jnp.broadcast_to(facts[:, index * share : index * share + 1], facts.shape)


def grad_kernel(
    mid_off, far_off, x, o, q_buf, lse_buf, far_lse, key_lse, gq_buf, gk_buf, gv_buf, score_buf,
    far_ref,
):
    place, segment, pos = place_info()
    heads, rows, width = x.q.shape
    quarter = rows // GROUP
    parts = o.stacked.shape[0]
    count = far_ref.shape[0]
    across, lines = x.far.shape[:2]
    for source in range(count):
        far_ref[source] = x.far[source % across, source // across]
    far_rows = rows // count
    scale = width**-0.5
    share = LANES // (2 * heads)
    words = quarter
    row, col = iotas(rows, rows)
    causal = row >= col
    far_row, far_col = iotas(far_rows, rows)
    far_allowed = far_col <= place * far_rows + far_row
    key_row, key_col = iotas(rows, far_rows)
    far_key_allowed = place * far_rows + key_col <= key_row
    mid_allowed = place_masks(place, pos, quarter, rows)
    mid_row, mid_col = iotas(rows, quarter)
    distance = mid_row // quarter
    later = (distance > 0) & (pos + distance < GROUP) & (place + distance < count)
    mid_key_allowed = later | ((distance == 0) & (mid_row >= mid_col))
    facts = far_ref[:, 3 * heads].reshape(rows, LANES)
    own = pl.ds(place * far_rows, far_rows)
    spread = spread_matrix(words, pos * quarter, quarter)
    for head in range(heads):
        mid_start = mid_off[head, segment]
        mid = pl.ds(mid_start, quarter, stride=GROUP)
        far = pl.ds(far_off[head], far_rows, stride=count)
        all_k = far_ref[:, head].reshape(rows, width)
        all_v = far_ref[:, heads + head].reshape(rows, width)
        all_g = far_ref[:, 2 * heads + head].reshape(rows, width)
        far_q = x.q[head, far, :]
        q_buf[...] = all_v
        q_buf[own, :] = far_q
        all_q = q_buf[...]
        score_buf[...] = dot_nt(all_q, all_k) * scale
        far_lse[...] = log_add(fact(facts, 2 * head, share), masked_lse(score_buf[...], causal))
        lse_buf[...] = x.lse[head]
        lse_buf[far, :] = far_lse[own, :]

        probs = jnp.where(causal, jnp.exp(x.scores[head] - wide(lse_buf[...], rows)), 0.0)
        grad_scores = probs * x.terms[head]
        gq_buf[...] = dot_nn(grad_scores, x.k[head]) * scale
        gk_buf[...] = dot_tn(grad_scores, x.q[head]) * scale
        gv_buf[...] = dot_tn(probs * x.keep[head], x.g[head])

        probs = jnp.where(
            mid_allowed, jnp.exp(x.mid_scores[head] - wide(lse_buf[mid, :], rows)), 0.0
        )
        grad_scores = probs * x.mid_terms[head]
        gq_buf[mid, :] = gq_buf[mid, :] + dot_nn(grad_scores, x.mid_k[head]) * scale

        dropped, grad_scores = pair_terms(
            score_buf[own, :], far_allowed, lse_buf[far, :],
            fact(far_ref[place, 3 * heads], 2 * head + 1, share),
            x.far_keep[head], far_ref[place, 2 * heads + head], all_v,
        )
        gq_buf[far, :] = gq_buf[far, :] + dot_nn(grad_scores, all_k) * scale
        o.stacked[:, 0, head] = gq_buf[...].reshape(parts, rows // parts, width)

        key_lse[0:quarter, :] = lse_buf[mid, :]
        meets = far_off[head] % GROUP == mid_start
        first = jnp.where(meets, (far_off[head] - mid_start) // GROUP, 0)
        for step in range(1, GROUP):
            key_lse[step * quarter : (step + 1) * quarter, :] = jnp.broadcast_to(
                x[f"rows{step}"][2, head][:, words : words + 1], (quarter, LANES)
            )
            spots = pl.ds(step * quarter + first, far_rows, stride=count // GROUP)
            source = jnp.minimum(place + step, count - 1) * far_rows
            key_lse[spots, :] = jnp.where(
                meets, far_lse[pl.ds(source, far_rows), :], key_lse[spots, :]
            )
        mid_q = jnp.concatenate([x[f"rows{step}"][0, head] for step in range(GROUP)], axis=0)
        mid_g = jnp.concatenate([x[f"rows{step}"][1, head] for step in range(GROUP)], axis=0)
        mid_facts = jnp.concatenate([x[f"rows{step}"][2, head] for step in range(GROUP)], axis=0)
        keep = spread_flags(keep_flags(mid_facts[:, 0:words].astype(jnp.int32), 1), spread, 1)
        dropped, grad_scores = pair_terms(
            dot_nt(mid_q, x.own_kv[0, head]) * scale, mid_key_allowed, key_lse[...],
            jnp.broadcast_to(mid_facts[:, LANES - 1 : LANES], (rows, LANES)),
            keep, mid_g, x.own_kv[1, head],
        )
        gk_buf[mid, :] = gk_buf[mid, :] + dot_tn(grad_scores, mid_q) * scale
        gv_buf[mid, :] = gv_buf[mid, :] + dot_tn(dropped, mid_g)

        far_k, far_v = far_ref[place, head], far_ref[place, heads + head]
        dropped, grad_scores = pair_terms(
            dot_nt(all_q, far_k) * scale, far_key_allowed, far_lse[...],
            fact(facts, 2 * head + 1, share),
            x.far_cols[:, head * far_rows : (head + 1) * far_rows], all_g, far_v,
        )
        gk_buf[far, :] = gk_buf[far, :] + dot_tn(grad_scores, all_q) * scale
        gv_buf[far, :] = gv_buf[far, :] + dot_tn(dropped, all_g)
        o.stacked[:, 1, head] = gk_buf[...].reshape(parts, rows // parts, width)
        o.stacked[:, 2, head] = gv_buf[...].reshape(parts, rows // parts, width)


class Loaded:
    def __init__(self, direct, fetched):
        self.__dict__.update(direct=direct, fetched=fetched, seen=set())

    def __getitem__(self, name):
        if name in self.direct:
            return self.direct[name]
        copy, ref = self.fetched[name]
        if name not in self.seen:
            self.seen.add(name)
            copy.wait()
        return ref

    def __getattr__(self, name):
        return self[name]


class Stored:
    def __init__(self, refs, sends):
        self.__dict__.update(refs, sends=sends)

    def send(self, name, part=slice(None)):
        self.sends(name, part)


def call(kernel, scalars, arrays, outs, scratch=(), flops=0, fetched=()):
    names = list(arrays)
    loads = [name for name in names if name in fetched]
    out_names = [name.rstrip("+") for name in outs]
    shapes = dict(zip(out_names, outs.values()))
    saves = [name for name in outs if not name.endswith("+")]
    hbm, vmem = pl.BlockSpec(memory_space=pltpu.HBM), pl.BlockSpec(memory_space=pltpu.VMEM)

    def run(*refs):
        refs = list(refs)

        def take(count):
            taken, refs[:] = refs[:count], refs[count:]
            return taken

        scalar_refs, in_refs, out_refs = take(len(scalars)), take(len(names)), take(len(outs))
        in_bufs, out_bufs, extra = take(len(loads)), take(len(saves)), take(len(scratch))
        in_sems, out_sems = refs
        given, written = dict(zip(names, in_refs)), dict(zip(out_names, out_refs))
        copies = {
            name: (pltpu.make_async_copy(given[name], buf, in_sems.at[i]), buf)
            for i, (name, buf) in enumerate(zip(loads, in_bufs))
        }
        for copy, _ in copies.values():
            copy.start()
        loaded = Loaded({name: given[name] for name in names if name not in loads}, copies)
        buffers = dict(zip(saves, out_bufs))
        writes = []

        def send(name, part=slice(None)):
            write = pltpu.make_async_copy(
                buffers[name].at[part], written[name].at[part], out_sems.at[len(writes)]
            )
            write.start()
            writes.append(write)
            sent.add(name)

        sent = set()
        kernel(*scalar_refs, loaded, Stored({**written, **buffers}, send), *extra)
        for name in loads:
            loaded[name]
        for name in saves:
            if name not in sent:
                send(name)
        for write in writes:
            write.wait()

    values = list(arrays.values())
    moved = 4 * sum(math.prod(shape) for shape in [v.shape for v in values] + [*shapes.values()])
    result = pl.pallas_call(
        run,
        out_shape=[
            pltpu.HBM(shape, jnp.float32)
            if name in saves
            else jax.ShapeDtypeStruct(shape, jnp.float32)
            for name, shape in shapes.items()
        ],
        in_specs=[pl.BlockSpec(memory_space=pltpu.SMEM)] * len(scalars)
        + [hbm if name in loads else vmem for name in names],
        out_specs=[hbm if name in saves else vmem for name in shapes],
        scratch_shapes=[pltpu.VMEM(arrays[name].shape, arrays[name].dtype) for name in loads]
        + [pltpu.VMEM(shapes[name], jnp.float32) for name in saves]
        + [pltpu.VMEM(shape, jnp.float32) for shape in scratch]
        + [
            pltpu.SemaphoreType.DMA((max(len(loads), 1),)),
            pltpu.SemaphoreType.DMA((max(2 * len(saves), 1),)),
        ],
        cost_estimate=pl.CostEstimate(flops=flops, transcendentals=0, bytes_accessed=moved),
        compiler_params=pltpu.CompilerParams(vmem_limit_bytes=40 * 1024 * 1024),
    )(
        *scalars,
        *[
            pltpu.with_memory_space_constraint(value, pltpu.HBM) if name in loads else value
            for name, value in arrays.items()
        ],
    )
    return dict(zip(out_names, result))


def shifted(value, steps):
    count = lax.axis_size("seq")
    first, last = max(0, -steps), min(count, count - steps)
    return lax.ppermute(value, "seq", [(source, source + steps) for source in range(first, last)])


def exchange(value, axis, groups=None):
    return lax.all_to_all(
        value, axis, split_axis=0, concat_axis=0, tiled=True, axis_index_groups=groups
    )


def per_device(q, k, v, output, grad_output, mid_off, far_off, drop_local, drop_mid, drop_far):
    heads, rows, width = q.shape
    count = lax.axis_size("seq")
    parts = lax.axis_size("head")
    quarter = rows // GROUP
    far_rows = rows // count
    whole = (heads, rows, width)
    pairs = (heads, rows, rows)
    mid_pairs = (heads, quarter, rows)
    key_pairs = (heads, rows, quarter)
    block = 6 * 2 * heads * rows * rows * width
    drop_local = jnp.swapaxes(drop_local, 1, 2)
    drop_far = jnp.swapaxes(drop_far, 1, 2)
    offsets = (mid_off, far_off)
    lines = count // ACROSS
    rows_of = [[line * ACROSS + i for i in range(ACROSS)] for line in range(lines)]
    columns = [list(group) for group in zip(*rows_of)]

    g_parts = exchange(grad_output.reshape(parts, heads, rows // parts, width), "head")
    own_kv = call(
        prep_kernel, (mid_off,), {"k": k, "v": v}, {"own_kv+": (2, heads, quarter, width)}
    )["own_kv"]
    kv = {f"kv{step}": shifted(own_kv, step) if step else own_kv for step in range(GROUP)}
    lse = call(local_kernel, offsets, {"q": q, "k": k}, {"lse+": whole}, flops=block)["lse"]
    mid = call(
        mid_kernel,
        offsets,
        {"g_parts": g_parts, "q": q, "k": k, "v": v, **kv, "output": output, "lse": lse},
        {
            "g+": whole,
            "delta+": whole,
            "lse+": whole,
            "far_send+": (lines, 3 * heads + 1, far_rows, width),
        },
        scratch=((rows, width),),
        flops=block // GROUP,
    )
    column = exchange(mid.pop("far_send"), "seq", columns)
    own_rows = call(
        rows_kernel, offsets, {"q": q, **mid, "drop_mid": drop_mid},
        {"rows+": (3, heads, quarter, width)},
    )["rows"]
    mid_rows = {
        f"rows{step}": shifted(own_rows, -step) if step else own_rows for step in range(GROUP)
    }
    relay = call(
        relay_kernel,
        offsets,
        {"column": column, "q": q},
        {"relay+": (ACROSS, lines, 3 * heads + 1, far_rows, width)},
    )["relay"]
    far = exchange(relay, "seq", rows_of)
    terms = call(
        terms_kernel,
        offsets,
        {
            "q": q, "k": k, "v": v, "g": mid["g"], "delta": mid["delta"], **kv,
            "drop_local": drop_local, "drop_mid": drop_mid, "drop_far": drop_far,
        },
        {
            "scores": pairs,
            "keep": pairs,
            "terms": pairs,
            "mid_scores": mid_pairs,
            "mid_terms": mid_pairs,
            "mid_k": whole,
            "far_keep": (heads, far_rows, rows),
            "far_cols": (rows, heads * far_rows),
        },
        scratch=((rows, width), (rows, rows)),
        flops=2 * block,
    )
    stacked = call(
        grad_kernel,
        offsets,
        {
            "far": far, "q": q, "k": k, "g": mid["g"], "lse": mid["lse"],
            **terms, **mid_rows, "own_kv": own_kv,
        },
        {"stacked+": (parts, 3, heads, rows // parts, width)},
        scratch=((rows, width),) * 7
        + ((rows, rows), (count, 3 * heads + 1, far_rows, width)),
        flops=8 * block,
        fetched=("k", "rows1", "rows2", "rows3", *terms),
    )["stacked"]
    result = exchange(stacked, "head")
    shape = (parts * heads, rows // parts, width)
    return tuple(result[:, part].reshape(shape) for part in range(3))


def solution(mesh):
    tokens = P(None, ("seq", "head"), None)
    placed = P("head", "seq", None)
    return jax.shard_map(
        per_device,
        mesh=mesh,
        in_specs=(
            placed, placed, placed, placed, tokens,
            P("head", None), P("head"), placed, placed, P("head", None, None),
        ),
        out_specs=(tokens, tokens, tokens),
        check_vma=False,
    )
```

time: 121 us -> 117 us (0.967)
  the two profiles are of different devices: /device:TPU:27 before, /device:TPU:1 now
where the time goes in v2:
time: 117 us; the launch traced here: 116 us
  blocking collectives  53 us (45%)
  starting transfers between devices  30 us (26%)
  Pallas kernels  18 us (15%)
  waiting for transfers between devices  12.3 us (11%)
  local copies, waits for them, and re-layouts  2.3 us (2%)
    all_to_all x2, blocking collectives, exchange(): lax.all_to_all(value, axis, split_axis=0, concat_axis=0, tiled=True, axis...  53 us
    pallas_call x7, Pallas kernels, call(): pl.pallas_call(run, out_shape=[pltpu.HBM(shape, jnp.float32) if name in s...  18 us
    all_to_all x2, starting transfers between devices, exchange(): lax.all_to_all(value, axis, split_axis=0, concat_axis=0, tiled=True, axis...  15.6 us
    ppermute x6, starting transfers between devices, shifted(): lax.ppermute(value, 'seq', [(source, source + steps) for source in range(...  14.4 us
    ppermute x6, waiting for transfers between devices, shifted(): lax.ppermute(value, 'seq', [(source, source + steps) for source in range(...  12.3 us
  transfers between devices with their start and end apart: 8, of which 3 were waited for; matrix products, arithmetic and copies ran while one was open for 0% of the time, Pallas kernels for 5%

profile of v2, /device:TPU:1, one launch (start us, length us, event | category | flops | bytes accessed | tf_op | source)
XLA Modules:
  0.0 116.4 jit_solution(14825923721566934146)
XLA Ops:
  0.7 12.0 %all-to-all-start = ((f32[16,2,16,128]{3,2,1,0:T(8,128)}), f32[16,2,16,128]{3,2,1,0:T(8,128)S(1)}, u32[]{:S(2)}, u32[]{:S(2)}) async-start(f32[16,2,16,128]{3,2,1,0:T(8,128)} %bitcast.8), calls=%async_computation | async-start | bytes 524288 | tf_op jit(solution)/shard_map/all_to_all | solution.py:441
  12.6 0.0 copy-start.7
  12.7 0.7 copy-done.7
  13.3 0.6 shard_map.121.refs_6_.refs_7_.refs_19_
  14.0 4.5 %collective-permute-start.2 = (f32[2,2,64,128]{3,2,1,0:T(8,128)S(1)}, f32[2,2,64,128]{3,2,1,0:T(8,128)S(1)}, u32[]{:S(2)}, u32[]{:S(2)}) collective-permute-start(f32[2,2,64,128]{3,2,1,0:T(8,128)S(1)} %shard_map.121.refs_6_.refs_7_.refs_19_), channel_id=1, source_target_pairs={{0,48},{16,64},{32,80},{48,96},{64,112},{80,128},{96,144},{112,160... | collective-permute-start | bytes 393224 | tf_op jit(solution)/shard_map/ppermute | solution.py:437
  18.5 3.4 %collective-permute-start.1 = (f32[2,2,64,128]{3,2,1,0:T(8,128)S(1)}, f32[2,2,64,128]{3,2,1,0:T(8,128)S(1)}, u32[]{:S(2)}, u32[]{:S(2)}) collective-permute-start(f32[2,2,64,128]{3,2,1,0:T(8,128)S(1)} %shard_map.121.refs_6_.refs_7_.refs_19_), channel_id=1, source_target_pairs={{0,32},{16,48},{32,64},{48,80},{64,96},{80,112},{96,128},{112,144}... | collective-permute-start | bytes 393224 | tf_op jit(solution)/shard_map/ppermute | solution.py:437
  22.0 2.5 %collective-permute-start = (f32[2,2,64,128]{3,2,1,0:T(8,128)S(1)}, f32[2,2,64,128]{3,2,1,0:T(8,128)S(1)}, u32[]{:S(2)}, u32[]{:S(2)}) collective-permute-start(f32[2,2,64,128]{3,2,1,0:T(8,128)S(1)} %shard_map.121.refs_6_.refs_7_.refs_19_), channel_id=1, source_target_pairs={{0,16},{16,32},{32,48},{48,64},{64,80},{80,96},{96,112},{112,128},... | collective-permute-start | bytes 393224 | tf_op jit(solution)/shard_map/ppermute | solution.py:437
  24.5 1.3 %shard_map.122.refs_11_ = f32[2,256,128]{2,1,0:T(8,128)S(1)} custom-call(s32[2,9]{1,0:T(2,128)S(1)} %copy-done.7, s32[2]{0:T(128)S(1)} %copy-done.9, f32[2,256,128]{2,1,0:T(8,128)S(1)} %copy-done, f32[2,256,128]{2,1,0:T(8,128)S(1)} %copy-done.1), custom_call_target="tpu_custom_call" | custom-call | flops 201326592 | bytes 786432 | tf_op jit(solution)/shard_map/pallas_call | solution.py:404
  25.9 1.4 %collective-permute-done.refs_7_.refs_8_ = f32[2,2,64,128]{3,2,1,0:T(8,128)S(1)} collective-permute-done((f32[2,2,64,128]{3,2,1,0:T(8,128)S(1)}, f32[2,2,64,128]{3,2,1,0:T(8,128)S(1)}, u32[]{:S(2)}, u32[]{:S(2)}) %collective-permute-start) | collective-permute-done | bytes 131104 | tf_op jit(solution)/shard_map/ppermute | solution.py:437
  27.3 1.2 %shard_map.123 = (f32[2,256,128]{2,1,0:T(8,128)S(1)}, f32[2,256,128]{2,1,0:T(8,128)S(1)}, f32[2,256,128]{2,1,0:T(8,128)S(1)}, f32[8,7,8,128]{3,2,1,0:T(8,128)S(1)}) custom-call(s32[2,9]{1,0:T(2,128)S(1)} %copy-done.8, s32[2]{0:T(128)S(1)} %copy-done.9, f32[16,2,16,128]{3,2,1,0:T(8,128)S(1)} %all-to-all-done.refs_2_, f32[2,256,128]{2,1,0:T(8,128)S(1)} %copy-done, ...), custom_call_target="tpu_custom_call" | custom-call | flops 50331648 | bytes 3112960 | tf_op jit(solution)/shard_map/pallas_call | solution.py:404
  28.5 19.5 %all_to_all.20.refs_2_ = f32[8,7,8,128]{3,2,1,0:T(8,128)S(1)} all-to-all(f32[8,7,8,128]{3,2,1,0:T(8,128)S(1)} %get-tuple-element.15), channel_id=1, replica_groups={{0,64,128,192,256,320,384,448},{16,80,144,208,272,336,400,464},{32,96,1..., dimensions={0} | all-to-all | bytes 458752 | tf_op jit(solution)/shard_map/all_to_all | solution.py:441
  48.0 1.6 %shard_map.124 = f32[4,8,7,8,128]{4,3,2,1,0:T(8,128)} custom-call(s32[2,9]{1,0:T(2,128)S(1)} %copy-done.8, s32[2]{0:T(128)S(1)} %copy-done.9, f32[8,7,8,128]{3,2,1,0:T(8,128)S(1)} %all_to_all.20.refs_2_, f32[2,256,128]{2,1,0:T(8,128)S(1)} %copy-done), custom_call_target="tpu_custom_call" | custom-call | bytes 1409024 | tf_op jit(solution)/shard_map/pallas_call | solution.py:404
  49.6 3.6 %all-to-all-start.2 = ((f32[4,8,7,8,128]{4,3,2,1,0:T(8,128)}), f32[4,8,7,8,128]{4,3,2,1,0:T(8,128)S(1)}, u32[]{:S(2)}, u32[]{:S(2)}) async-start(f32[4,8,7,8,128]{4,3,2,1,0:T(8,128)} %shard_map.124), calls=%async_computation.2 | async-start | bytes 1835008 | tf_op jit(solution)/shard_map/all_to_all | solution.py:441
  53.2 0.6 shard_map.126.refs_15_
  53.9 1.3 %collective-permute-start.5 = (f32[3,2,64,128]{3,2,1,0:T(8,128)S(1)}, f32[3,2,64,128]{3,2,1,0:T(8,128)S(1)}, u32[]{:S(2)}, u32[]{:S(2)}) collective-permute-start(f32[3,2,64,128]{3,2,1,0:T(8,128)S(1)} %shard_map.126.refs_15_), channel_id=1, source_target_pairs={{48,0},{64,16},{80,32},{96,48},{112,64},{128,80},{144,96},{160,112... | collective-permute-start | bytes 589832 | tf_op jit(solution)/shard_map/ppermute | solution.py:437
  55.2 1.3 %collective-permute-start.4 = (f32[3,2,64,128]{3,2,1,0:T(8,128)S(1)}, f32[3,2,64,128]{3,2,1,0:T(8,128)S(1)}, u32[]{:S(2)}, u32[]{:S(2)}) collective-permute-start(f32[3,2,64,128]{3,2,1,0:T(8,128)S(1)} %shard_map.126.refs_15_), channel_id=1, source_target_pairs={{32,0},{48,16},{64,32},{80,48},{96,64},{112,80},{128,96},{144,112}... | collective-permute-start | bytes 589832 | tf_op jit(solution)/shard_map/ppermute | solution.py:437
  56.5 1.3 %collective-permute-start.3 = (f32[3,2,64,128]{3,2,1,0:T(8,128)S(1)}, f32[3,2,64,128]{3,2,1,0:T(8,128)}, u32[]{:S(2)}, u32[]{:S(2)}) collective-permute-start(f32[3,2,64,128]{3,2,1,0:T(8,128)S(1)} %shard_map.126.refs_15_), channel_id=1, source_target_pairs={{16,0},{32,16},{48,32},{64,48},{80,64},{96,80},{112,96},{128,112},... | collective-permute-start | bytes 589832 | tf_op jit(solution)/shard_map/ppermute | solution.py:437
  57.8 3.5 %shard_map.125 = (f32[2,256,256]{2,1,0:T(8,128)}, f32[2,256,256]{2,1,0:T(8,128)}, f32[2,256,256]{2,1,0:T(8,128)}, f32[2,64,256]{2,1,0:T(8,128)}, f32[2,64,256]{2...) custom-call(s32[2,9]{1,0:T(2,128)S(1)} %copy-done.8, s32[2]{0:T(128)S(1)} %copy-done.9, ...), custom_call_target="tpu_custom_call" | custom-call | flops 402653184 | bytes 4259840 | tf_op jit(solution)/shard_map/pallas_call | solution.py:404
  61.4 4.5 %collective-permute-done.5.refs_18_ = f32[3,2,64,128]{3,2,1,0:T(8,128)S(1)} collective-permute-done((f32[3,2,64,128]{3,2,1,0:T(8,128)S(1)}, f32[3,2,64,128]{3,2,1,0:T(8,128)S(1)}, u32[]{:S(2)}, u32[]{:S(2)}) %collective-permute-start.5) | collective-permute-done | bytes 196640 | tf_op jit(solution)/shard_map/ppermute | solution.py:437
  65.8 6.5 %collective-permute-done.4.refs_17_ = f32[3,2,64,128]{3,2,1,0:T(8,128)S(1)} collective-permute-done((f32[3,2,64,128]{3,2,1,0:T(8,128)S(1)}, f32[3,2,64,128]{3,2,1,0:T(8,128)S(1)}, u32[]{:S(2)}, u32[]{:S(2)}) %collective-permute-start.4) | collective-permute-done | bytes 196640 | tf_op jit(solution)/shard_map/ppermute | solution.py:437
  72.3 0.7 copy-done.11
  73.0 9.1 %shard_map.127 = f32[16,3,2,16,128]{4,3,2,1,0:T(8,128)S(1)} custom-call(s32[2,9]{1,0:T(2,128)S(1)} %copy-done.8, s32[2]{0:T(128)S(1)} %copy-done.9, f32[4,8,7,8,128]{4,3,2,1,0:T(8,128)S(1)} %all-to-all-done.2.refs_2_, f32[2,256,128]{2,1,0:T(8,128)S(1)} %copy-done, f32[2,256,128]{2,1,0:T(8,128)} %refs_4_.5, ...), custom_call_target="tpu_custom_call" | custom-call | flops 1610612736 | bytes 5799936 | tf_op jit(solution)/shard_map/pallas_call | solution.py:404
  82.1 33.5 %all_to_all.21 = f32[16,3,2,16,128]{4,3,2,1,0:T(8,128)S(1)} all-to-all(f32[16,3,2,16,128]{4,3,2,1,0:T(8,128)S(1)} %shard_map.127), channel_id=1, replica_groups=mesh['seq'=32,'head'=16] {'head'}, dimensions={0} | all-to-all | bytes 1572864 | tf_op jit(solution)/shard_map/all_to_all | solution.py:441
  115.5 0.9 fusion
  (26 shorter events, 0.1 us)
Async XLA Ops:
  0.6 12.0 %copy-start.1 = (f32[2,256,128]{2,1,0:T(8,128)S(1)}, f32[2,256,128]{2,1,0:T(8,128)}, u32[]{:S(2)}) copy-start(f32[2,256,128]{2,1,0:T(8,128)} %refs_4_.5) | copy-start | bytes 786436
  0.6 12.0 %copy-start.2 = (f32[2,256,128]{2,1,0:T(8,128)S(1)}, f32[2,256,128]{2,1,0:T(8,128)}, u32[]{:S(2)}) copy-start(f32[2,256,128]{2,1,0:T(8,128)} %refs_4_.4) | copy-start | bytes 786436
  0.7 26.6 %all-to-all-start = ((f32[16,2,16,128]{3,2,1,0:T(8,128)}), f32[16,2,16,128]{3,2,1,0:T(8,128)S(1)}, u32[]{:S(2)}, u32[]{:S(2)}) async-start(f32[16,2,16,128]{3,2,1,0:T(8,128)} %bitcast.8), calls=%async_computation | async-start | bytes 524288 | tf_op jit(solution)/shard_map/all_to_all | solution.py:441
  12.6 0.7 copy-start.7
  13.3 11.2 %copy-start = (f32[2,256,128]{2,1,0:T(8,128)S(1)}, f32[2,256,128]{2,1,0:T(8,128)}, u32[]{:S(2)}) copy-start(f32[2,256,128]{2,1,0:T(8,128)} %refs_3_.9) | copy-start | bytes 786436
  13.3 11.2 %copy-start.9 = (s32[2]{0:T(128)S(1)}, s32[2]{0:T(128)}, u32[]{:S(2)}) copy-start(s32[2]{0:T(128)} %refs_1_.13) | copy-start | bytes 28
  13.9 13.3 %copy-start.3 = (f32[2,256,128]{2,1,0:T(8,128)S(1)}, f32[2,256,128]{2,1,0:T(8,128)}, u32[]{:S(2)}) copy-start(f32[2,256,128]{2,1,0:T(8,128)} %refs_10_.1) | copy-start | bytes 786436
  14.0 13.3 %copy-start.8 = (s32[2,9]{1,0:T(2,128)S(1)}, s32[2,9]{1,0:T(2,128)}, u32[]{:S(2)}) copy-start(s32[2,9]{1,0:T(2,128)} %refs_0_.13) | copy-start | bytes 220
  14.0 11.9 %collective-permute-start.2 = (f32[2,2,64,128]{3,2,1,0:T(8,128)S(1)}, f32[2,2,64,128]{3,2,1,0:T(8,128)S(1)}, u32[]{:S(2)}, u32[]{:S(2)}) collective-permute-start(f32[2,2,64,128]{3,2,1,0:T(8,128)S(1)} %shard_map.121.refs_6_.refs_7_.refs_19_), channel_id=1, source_target_pairs={{0,48},{16,64},{32,80},{48,96},{64,112},{80,128},{96,144},{112,160... | collective-permute-start | bytes 393224 | tf_op jit(solution)/shard_map/ppermute | solution.py:437
  18.5 7.3 %collective-permute-start.1 = (f32[2,2,64,128]{3,2,1,0:T(8,128)S(1)}, f32[2,2,64,128]{3,2,1,0:T(8,128)S(1)}, u32[]{:S(2)}, u32[]{:S(2)}) collective-permute-start(f32[2,2,64,128]{3,2,1,0:T(8,128)S(1)} %shard_map.121.refs_6_.refs_7_.refs_19_), channel_id=1, source_target_pairs={{0,32},{16,48},{32,64},{48,80},{64,96},{80,112},{96,128},{112,144}... | collective-permute-start | bytes 393224 | tf_op jit(solution)/shard_map/ppermute | solution.py:437
  22.0 5.3 %collective-permute-start = (f32[2,2,64,128]{3,2,1,0:T(8,128)S(1)}, f32[2,2,64,128]{3,2,1,0:T(8,128)S(1)}, u32[]{:S(2)}, u32[]{:S(2)}) collective-permute-start(f32[2,2,64,128]{3,2,1,0:T(8,128)S(1)} %shard_map.121.refs_6_.refs_7_.refs_19_), channel_id=1, source_target_pairs={{0,16},{16,32},{32,48},{48,64},{64,80},{80,96},{96,112},{112,128},... | collective-permute-start | bytes 393224 | tf_op jit(solution)/shard_map/ppermute | solution.py:437
  49.5 3.7 %copy-start.4 = (s32[2,64,64]{2,1,0:T(8,128)S(1)}, s32[2,64,64]{2,1,0:T(8,128)}, u32[]{:S(2)}) copy-start(s32[2,64,64]{2,1,0:T(8,128)} %refs_6_.1) | copy-start | bytes 98308
  49.6 23.4 %all-to-all-start.2 = ((f32[4,8,7,8,128]{4,3,2,1,0:T(8,128)}), f32[4,8,7,8,128]{4,3,2,1,0:T(8,128)S(1)}, u32[]{:S(2)}, u32[]{:S(2)}) async-start(f32[4,8,7,8,128]{4,3,2,1,0:T(8,128)} %shard_map.124), calls=%async_computation.2 | async-start | bytes 1835008 | tf_op jit(solution)/shard_map/all_to_all | solution.py:441
  53.2 4.6 %copy-start.5 = (s32[2,256,64]{1,2,0:T(8,128)S(1)}, s32[2,256,64]{1,2,0:T(8,128)}, u32[]{:S(2)}) copy-start(s32[2,256,64]{1,2,0:T(8,128)} %param.17) | copy-start | bytes 393220
  53.2 4.6 %copy-start.6 = (s32[2,256,64]{1,2,0:T(8,128)S(1)}, s32[2,256,64]{1,2,0:T(8,128)}, u32[]{:S(2)}) copy-start(s32[2,256,64]{1,2,0:T(8,128)} %param.19) | copy-start | bytes 393220
  53.9 12.0 %collective-permute-start.5 = (f32[3,2,64,128]{3,2,1,0:T(8,128)S(1)}, f32[3,2,64,128]{3,2,1,0:T(8,128)S(1)}, u32[]{:S(2)}, u32[]{:S(2)}) collective-permute-start(f32[3,2,64,128]{3,2,1,0:T(8,128)S(1)} %shard_map.126.refs_15_), channel_id=1, source_target_pairs={{48,0},{64,16},{80,32},{96,48},{112,64},{128,80},{144,96},{160,112... | collective-permute-start | bytes 589832 | tf_op jit(solution)/shard_map/ppermute | solution.py:437
  55.2 17.1 %collective-permute-start.4 = (f32[3,2,64,128]{3,2,1,0:T(8,128)S(1)}, f32[3,2,64,128]{3,2,1,0:T(8,128)S(1)}, u32[]{:S(2)}, u32[]{:S(2)}) collective-permute-start(f32[3,2,64,128]{3,2,1,0:T(8,128)S(1)} %shard_map.126.refs_15_), channel_id=1, source_target_pairs={{32,0},{48,16},{64,32},{80,48},{96,64},{112,80},{128,96},{144,112}... | collective-permute-start | bytes 589832 | tf_op jit(solution)/shard_map/ppermute | solution.py:437
  56.5 16.5 %collective-permute-start.3 = (f32[3,2,64,128]{3,2,1,0:T(8,128)S(1)}, f32[3,2,64,128]{3,2,1,0:T(8,128)}, u32[]{:S(2)}, u32[]{:S(2)}) collective-permute-start(f32[3,2,64,128]{3,2,1,0:T(8,128)S(1)} %shard_map.126.refs_15_), channel_id=1, source_target_pairs={{16,0},{32,16},{48,32},{64,48},{80,64},{96,80},{112,96},{128,112},... | collective-permute-start | bytes 589832 | tf_op jit(solution)/shard_map/ppermute | solution.py:437
  65.8 7.1 %copy-start.10 = (f32[3,2,64,128]{3,2,1,0:T(8,128)}, f32[3,2,64,128]{3,2,1,0:T(8,128)S(1)}, u32[]{:S(2)}) copy-start(f32[3,2,64,128]{3,2,1,0:T(8,128)S(1)} %collective-permute-done.5.refs_18_) | copy-start | bytes 589828
  72.3 0.7 copy-start.11

commit v3 on v2

--- a/solution.py
+++ b/solution.py
@@ -104,12 +104,20 @@
 
 
 def prep_kernel(mid_off, x, o):
-    _, segment, _ = place_info()
+    _, segment, pos = place_info()
     heads, rows, _ = x.k.shape
+    words = x.drop_mid.shape[2]
     for head in range(heads):
         picked = pl.ds(mid_off[head, segment], rows // GROUP, stride=GROUP)
-        o.own_kv[0, head] = x.k[head, picked, :]
-        o.own_kv[1, head] = x.v[head, picked, :]
+        mid_q, mid_k, mid_v = x.q[head, picked, :], x.k[head, picked, :], x.v[head, picked, :]
+        mid_words = x.drop_mid[head].astype(jnp.float32)
+        mid_words = jnp.concatenate([mid_words] * (LANES // words), axis=1)
+        o.kv0[0, head] = mid_k
+        o.kv0[1, head] = mid_v
+        for step, ref in ((1, o.send1), (2, o.send2), (3, o.send3)):
+            later = pos + step < GROUP
+            ref[0, head] = jnp.where(later, mid_k, mid_q)
+            ref[1, head] = jnp.where(later, mid_v, mid_words)
 
 
 def local_kernel(mid_off, far_off, x, o):
@@ -179,26 +187,27 @@
 
 def rows_kernel(mid_off, far_off, x, o):
     _, segment, _ = place_info()
+    heads, rows, width = x.g.shape
+    quarter = rows // GROUP
+    _, lane = iotas(quarter, LANES)
+    part = lane // (LANES // (2 * heads))
+    facts = jnp.zeros((quarter, LANES), jnp.float32)
+    for head in range(heads):
+        mid = pl.ds(mid_off[head, segment], quarter, stride=GROUP)
+        o.rows[head] = x.g[head, mid, :]
+        facts = jnp.where(part == 2 * head, x.lse[head, mid, :], facts)
+        facts = jnp.where(part == 2 * head + 1, x.delta[head, mid, :], facts)
+    o.rows[heads] = facts
+
+
+def terms_kernel(mid_off, far_off, x, o, buf, keep_buf):
+    place, segment, pos = place_info()
     heads, rows, width = x.q.shape
     quarter = rows // GROUP
-    words = x.drop_mid.shape[2]
-    _, lane = iotas(quarter, LANES)
-    for head in range(heads):
-        mid = pl.ds(mid_off[head, segment], quarter, stride=GROUP)
-        o.rows[0, head] = x.q[head, mid, :]
-        o.rows[1, head] = x.g[head, mid, :]
-        o.rows[2, head] = jnp.where(
-            lane < words + (LANES - words) // 2, x.lse[head, mid, :], x.delta[head, mid, :]
-        )
-        o.rows[2, head, :, 0:words] = x.drop_mid[head].astype(jnp.float32)
-
-
-def terms_kernel(mid_off, far_off, x, o, buf, keep_buf):
-    place, segment, _ = place_info()
-    heads, rows, width = x.q.shape
     scale = width**-0.5
     words = x.drop_local.shape[1]
     far_rows = o.far_keep.shape[1]
+    key_spread = spread_matrix(words, pos * quarter, quarter)
     spread = spread_matrix(words, 0, rows)
     far_spread = spread_matrix(words, place * far_rows, far_rows)
     for head in range(heads):
@@ -208,9 +217,17 @@
         o.terms[head] = dot_nt(x.g[head], x.v[head]) * keep - wide(x.delta[head], rows)
         mid = pl.ds(mid_off[head, segment], rows // GROUP, stride=GROUP)
         gather_mid(x, 0, head, buf)
+        mid_q = x.q[head, mid, :]
         o.mid_k[head] = buf[...]
-        o.mid_scores[head] = dot_nt(x.q[head, mid, :], buf[...]) * scale
+        o.mid_scores[head] = dot_nt(mid_q, buf[...]) * scale
+        own_block = pl.ds(pos * quarter, quarter)
+        buf[own_block, :] = mid_q
+        o.key_pairs[head, :, 0:quarter] = dot_nt(buf[...], x.kv0[0, head]) * scale
         gather_mid(x, 1, head, buf)
+        keep_buf[:, 0:words] = buf[:, 0:words]
+        keep_buf[own_block, 0:words] = x.drop_mid[head].astype(jnp.float32)
+        flags = keep_flags(keep_buf[:, 0:words].astype(jnp.int32), 1)
+        o.key_pairs[head, :, quarter : 2 * quarter] = spread_flags(flags, key_spread, 1)
         keep = spread_flags(keep_flags(x.drop_mid[head], 1), spread, 1)
         o.mid_terms[head] = dot_nt(x.g[head, mid, :], buf[...]) * keep - wide(
             x.delta[head, mid, :], rows
@@ -226,8 +243,8 @@
 
 
 def grad_kernel(
-    mid_off, far_off, x, o, q_buf, lse_buf, far_lse, key_lse, gq_buf, gk_buf, gv_buf, score_buf,
-    far_ref,
+    mid_off, far_off, x, o, q_buf, lse_buf, far_lse, key_lse, gq_buf, gk_buf, gv_buf, mid_g,
+    key_delta, score_buf, far_ref,
 ):
     place, segment, pos = place_info()
     heads, rows, width = x.q.shape
@@ -240,7 +257,6 @@
     far_rows = rows // count
     scale = width**-0.5
     share = LANES // (2 * heads)
-    words = quarter
     row, col = iotas(rows, rows)
     causal = row >= col
     far_row, far_col = iotas(far_rows, rows)
@@ -249,12 +265,13 @@
     far_key_allowed = place * far_rows + key_col <= key_row
     mid_allowed = place_masks(place, pos, quarter, rows)
     mid_row, mid_col = iotas(rows, quarter)
-    distance = mid_row // quarter
-    later = (distance > 0) & (pos + distance < GROUP) & (place + distance < count)
-    mid_key_allowed = later | ((distance == 0) & (mid_row >= mid_col))
+    block = mid_row // quarter
+    mid_key_allowed = ((block > pos) & (place - pos + block < count)) | (
+        (block == pos) & (mid_row % quarter >= mid_col)
+    )
+    own_block = pl.ds(pos * quarter, quarter)
     facts = far_ref[:, 3 * heads].reshape(rows, LANES)
     own = pl.ds(place * far_rows, far_rows)
-    spread = spread_matrix(words, pos * quarter, quarter)
     for head in range(heads):
         mid_start = mid_off[head, segment]
         mid = pl.ds(mid_start, quarter, stride=GROUP)
@@ -291,29 +308,34 @@
         gq_buf[far, :] = gq_buf[far, :] + dot_nn(grad_scores, all_k) * scale
         o.stacked[:, 0, head] = gq_buf[...].reshape(parts, rows // parts, width)
 
-        key_lse[0:quarter, :] = lse_buf[mid, :]
         meets = far_off[head] % GROUP == mid_start
         first = jnp.where(meets, (far_off[head] - mid_start) // GROUP, 0)
-        for step in range(1, GROUP):
-            key_lse[step * quarter : (step + 1) * quarter, :] = jnp.broadcast_to(
-                x[f"rows{step}"][2, head][:, words : words + 1], (quarter, LANES)
+        for step in range(GROUP):
+            source = (pos + step) % GROUP
+            part = pl.ds(source * quarter, quarter)
+            rows_ref = x[f"rows{(GROUP - step) % GROUP}"]
+            mid_g[part, :] = rows_ref[head]
+            key_delta[part, :] = fact(rows_ref[heads], 2 * head + 1, share)
+            if step == 0:
+                key_lse[part, :] = lse_buf[mid, :]
+                continue
+            key_lse[part, :] = fact(rows_ref[heads], 2 * head, share)
+            spots = pl.ds(source * quarter + first, far_rows, stride=count // GROUP)
+            start = jnp.clip(place - pos + source, 0, count - 1) * far_rows
+            key_lse[spots, :] = jnp.where(
+                meets, far_lse[pl.ds(start, far_rows), :], key_lse[spots, :]
             )
-            spots = pl.ds(step * quarter + first, far_rows, stride=count // GROUP)
-            source = jnp.minimum(place + step, count - 1) * far_rows
-            key_lse[spots, :] = jnp.where(
-                meets, far_lse[pl.ds(source, far_rows), :], key_lse[spots, :]
-            )
-        mid_q = jnp.concatenate([x[f"rows{step}"][0, head] for step in range(GROUP)], axis=0)
-        mid_g = jnp.concatenate([x[f"rows{step}"][1, head] for step in range(GROUP)], axis=0)
-        mid_facts = jnp.concatenate([x[f"rows{step}"][2, head] for step in range(GROUP)], axis=0)
-        keep = spread_flags(keep_flags(mid_facts[:, 0:words].astype(jnp.int32), 1), spread, 1)
-        dropped, grad_scores = pair_terms(
-            dot_nt(mid_q, x.own_kv[0, head]) * scale, mid_key_allowed, key_lse[...],
-            jnp.broadcast_to(mid_facts[:, LANES - 1 : LANES], (rows, LANES)),
-            keep, mid_g, x.own_kv[1, head],
+        q_buf[...] = x.mid_k[head]
+        q_buf[own_block, :] = x.q[head, mid, :]
+        probs = jnp.where(
+            mid_key_allowed, jnp.exp(x.key_pairs[head, :, 0:quarter] - key_lse[:, 0:quarter]), 0.0
         )
-        gk_buf[mid, :] = gk_buf[mid, :] + dot_tn(grad_scores, mid_q) * scale
-        gv_buf[mid, :] = gv_buf[mid, :] + dot_tn(dropped, mid_g)
+        keep = x.key_pairs[head, :, quarter : 2 * quarter]
+        grad_scores = probs * (
+            dot_nt(mid_g[...], x.kv0[1, head]) * keep - key_delta[:, 0:quarter]
+        )
+        gk_buf[mid, :] = gk_buf[mid, :] + dot_tn(grad_scores, q_buf[...]) * scale
+        gv_buf[mid, :] = gv_buf[mid, :] + dot_tn(probs * keep, mid_g[...])
 
         far_k, far_v = far_ref[place, head], far_ref[place, heads + head]
         dropped, grad_scores = pair_terms(
@@ -327,21 +349,32 @@
         o.stacked[:, 2, head] = gv_buf[...].reshape(parts, rows // parts, width)
 
 
+class Fetched:
+    def __init__(self, copies, ref):
+        self.copies, self.ref, self.shape, self.seen = copies, ref, ref.shape, set()
+
+    def wait(self, head):
+        if head not in self.seen:
+            self.seen.add(head)
+            self.copies[head].wait()
+
+    def __getitem__(self, index):
+        leading = index[0] if isinstance(index, tuple) else index
+        for head in range(len(self.copies)):
+            if len(self.copies) == 1 or not isinstance(leading, int) or leading == head:
+                self.wait(head)
+        return self.ref[index]
+
+
 class Loaded:
-    def __init__(self, direct, fetched):
-        self.__dict__.update(direct=direct, fetched=fetched, seen=set())
+    def __init__(self, refs):
+        self.__dict__.update(refs=refs)
 
     def __getitem__(self, name):
-        if name in self.direct:
-            return self.direct[name]
-        copy, ref = self.fetched[name]
-        if name not in self.seen:
-            self.seen.add(name)
-            copy.wait()
-        return ref
+        return self.refs[name]
 
     def __getattr__(self, name):
-        return self[name]
+        return self.refs[name]
 
 
 class Stored:
@@ -353,6 +386,7 @@
 
 
 def call(kernel, scalars, arrays, outs, scratch=(), flops=0, fetched=()):
+    heads = 2
     names = list(arrays)
     loads = [name for name in names if name in fetched]
     out_names = [name.rstrip("+") for name in outs]
@@ -371,13 +405,20 @@
         in_bufs, out_bufs, extra = take(len(loads)), take(len(saves)), take(len(scratch))
         in_sems, out_sems = refs
         given, written = dict(zip(names, in_refs)), dict(zip(out_names, out_refs))
-        copies = {
-            name: (pltpu.make_async_copy(given[name], buf, in_sems.at[i]), buf)
-            for i, (name, buf) in enumerate(zip(loads, in_bufs))
-        }
-        for copy, _ in copies.values():
-            copy.start()
-        loaded = Loaded({name: given[name] for name in names if name not in loads}, copies)
+        copies = {name: {} for name in loads}
+        used = 0
+        for head in range(heads):
+            for name, buf in zip(loads, in_bufs):
+                whole = buf.shape[0] != heads
+                if whole and head:
+                    continue
+                part = slice(None) if whole else head
+                copy = pltpu.make_async_copy(given[name].at[part], buf.at[part], in_sems.at[used])
+                copy.start()
+                copies[name][head] = copy
+                used += 1
+        moving = {name: Fetched(copies[name], buf) for name, buf in zip(loads, in_bufs)}
+        loaded = Loaded({**given, **moving})
         buffers = dict(zip(saves, out_bufs))
         writes = []
 
@@ -392,7 +433,8 @@
         sent = set()
         kernel(*scalar_refs, loaded, Stored({**written, **buffers}, send), *extra)
         for name in loads:
-            loaded[name]
+            for head in copies[name]:
+                moving[name].wait(head)
         for name in saves:
             if name not in sent:
                 send(name)
@@ -416,7 +458,7 @@
         + [pltpu.VMEM(shapes[name], jnp.float32) for name in saves]
         + [pltpu.VMEM(shape, jnp.float32) for shape in scratch]
         + [
-            pltpu.SemaphoreType.DMA((max(len(loads), 1),)),
+            pltpu.SemaphoreType.DMA((max(heads * len(loads), 1),)),
             pltpu.SemaphoreType.DMA((max(2 * len(saves), 1),)),
         ],
         cost_estimate=pl.CostEstimate(flops=flops, transcendentals=0, bytes_accessed=moved),
@@ -431,10 +473,13 @@
     return dict(zip(out_names, result))
 
 
-def shifted(value, steps):
+def turned(value, steps):
     count = lax.axis_size("seq")
-    first, last = max(0, -steps), min(count, count - steps)
-    return lax.ppermute(value, "seq", [(source, source + steps) for source in range(first, last)])
+    pairs = []
+    for first in range(-HALF, count - HALF, GROUP):
+        for pos in range(GROUP):
+            pairs.append(((first + pos) % count, (first + (pos + steps) % GROUP) % count))
+    return lax.ppermute(value, "seq", pairs)
 
 
 def exchange(value, axis, groups=None):
@@ -462,10 +507,17 @@
     columns = [list(group) for group in zip(*rows_of)]
 
     g_parts = exchange(grad_output.reshape(parts, heads, rows // parts, width), "head")
-    own_kv = call(
-        prep_kernel, (mid_off,), {"k": k, "v": v}, {"own_kv+": (2, heads, quarter, width)}
-    )["own_kv"]
-    kv = {f"kv{step}": shifted(own_kv, step) if step else own_kv for step in range(GROUP)}
+    first = call(
+        prep_kernel,
+        (mid_off,),
+        {"q": q, "k": k, "v": v, "drop_mid": drop_mid},
+        {f"{name}+": (2, heads, quarter, width) for name in ("kv0", "send1", "send2", "send3")},
+        fetched=("v", "drop_mid"),
+    )
+    kv = {
+        f"kv{step}": turned(first[f"send{step}"], step) if step else first["kv0"]
+        for step in range(GROUP)
+    }
     lse = call(local_kernel, offsets, {"q": q, "k": k}, {"lse+": whole}, flops=block)["lse"]
     mid = call(
         mid_kernel,
@@ -482,12 +534,34 @@
     )
     column = exchange(mid.pop("far_send"), "seq", columns)
     own_rows = call(
-        rows_kernel, offsets, {"q": q, **mid, "drop_mid": drop_mid},
-        {"rows+": (3, heads, quarter, width)},
+        rows_kernel, offsets, mid, {"rows+": (heads + 1, quarter, width)}
     )["rows"]
     mid_rows = {
-        f"rows{step}": shifted(own_rows, -step) if step else own_rows for step in range(GROUP)
+        f"rows{step}": turned(own_rows, step) if step else own_rows for step in range(GROUP)
     }
+    term_shapes = {
+        "scores": pairs,
+        "terms": pairs,
+        "keep": pairs,
+        "mid_scores": mid_pairs,
+        "mid_terms": mid_pairs,
+        "mid_k": whole,
+        "far_keep": (heads, far_rows, rows),
+        "key_pairs": whole,
+        "far_cols": (rows, heads * far_rows),
+    }
+    terms = call(
+        terms_kernel,
+        offsets,
+        {
+            "q": q, "k": k, "v": v, "g": mid["g"], "delta": mid["delta"], **kv,
+            "drop_local": drop_local, "drop_mid": drop_mid, "drop_far": drop_far,
+        },
+        term_shapes,
+        scratch=((rows, width), (rows, rows)),
+        flops=2 * block,
+    )
+    column, own_rows, terms = lax.optimization_barrier((column, own_rows, terms))
     relay = call(
         relay_kernel,
         offsets,
@@ -495,35 +569,15 @@
         {"relay+": (ACROSS, lines, 3 * heads + 1, far_rows, width)},
     )["relay"]
     far = exchange(relay, "seq", rows_of)
-    terms = call(
-        terms_kernel,
-        offsets,
-        {
-            "q": q, "k": k, "v": v, "g": mid["g"], "delta": mid["delta"], **kv,
-            "drop_local": drop_local, "drop_mid": drop_mid, "drop_far": drop_far,
-        },
-        {
-            "scores": pairs,
-            "keep": pairs,
-            "terms": pairs,
-            "mid_scores": mid_pairs,
-            "mid_terms": mid_pairs,
-            "mid_k": whole,
-            "far_keep": (heads, far_rows, rows),
-            "far_cols": (rows, heads * far_rows),
-        },
-        scratch=((rows, width), (rows, rows)),
-        flops=2 * block,
-    )
     stacked = call(
         grad_kernel,
         offsets,
         {
             "far": far, "q": q, "k": k, "g": mid["g"], "lse": mid["lse"],
-            **terms, **mid_rows, "own_kv": own_kv,
+            **{name: terms[name] for name in term_shapes}, **mid_rows, "kv0": kv["kv0"],
         },
         {"stacked+": (parts, 3, heads, rows // parts, width)},
-        scratch=((rows, width),) * 7
+        scratch=((rows, width),) * 9
         + ((rows, rows), (count, 3 * heads + 1, far_rows, width)),
         flops=8 * block,
         fetched=("k", "rows1", "rows2", "rows3", *terms),

time: 117 us -> 116 us (level)
  blocking collectives: 53 us -> 32.2 us
  starting transfers between devices: 30 us -> 49.3 us
  waiting for transfers between devices: 12.3 us -> 8.52 us
  Pallas kernels: 18 us -> 21 us
    all_to_all x2 -> x1, blocking collectives: 53 us -> 32.2 us  [exchange(): lax.all_to_all(value, axis, split_axis=0, concat_axis=0, tiled=True, axis...]
    ppermute x6, starting transfers between devices: 14.4 us -> 27.4 us  [turned(): return lax.ppermute(value, 'seq', pairs)]
    ppermute x6, waiting for transfers between devices: 12.3 us -> 4.64 us  [turned(): return lax.ppermute(value, 'seq', pairs)]
    all_to_all x2 -> x3, starting transfers between devices: 15.6 us -> 21.9 us  [exchange(): lax.all_to_all(value, axis, split_axis=0, concat_axis=0, tiled=True, axis...]
    all_to_all x2 -> x3, waiting for transfers between devices: 0.01 us -> 3.88 us  [exchange(): lax.all_to_all(value, axis, split_axis=0, concat_axis=0, tiled=True, axis...]
    pallas_call x7, Pallas kernels: 18 us -> 21 us  [call(): pl.pallas_call(run, out_shape=[pltpu.HBM(shape, jnp.float32) if name in s...]
  transfers between devices with their start and end apart: 8 -> 9, of which waited for: 3 -> 4; matrix products, arithmetic and copies ran while one was open for 0% -> 0% of each run, Pallas kernels for 5% -> 7%
where the time goes in v3:
time: 116 us; the launch traced here: 115 us
  starting transfers between devices  49.3 us (42%)
  blocking collectives  32.2 us (28%)
  Pallas kernels  21 us (18%)
  waiting for transfers between devices  8.52 us (7%)
  local copies, waits for them, and re-layouts  2.62 us (2%)
    all_to_all x1, blocking collectives, exchange(): lax.all_to_all(value, axis, split_axis=0, concat_axis=0, tiled=True, axis...  32.2 us
    ppermute x6, starting transfers between devices, turned(): return lax.ppermute(value, 'seq', pairs)  27.4 us
    all_to_all x3, starting transfers between devices, exchange(): lax.all_to_all(value, axis, split_axis=0, concat_axis=0, tiled=True, axis...  21.9 us
    pallas_call x7, Pallas kernels, call(): pl.pallas_call(run, out_shape=[pltpu.HBM(shape, jnp.float32) if name in s...  21 us
    ppermute x6, waiting for transfers between devices, turned(): return lax.ppermute(value, 'seq', pairs)  4.64 us
    all_to_all x3, waiting for transfers between devices, exchange(): lax.all_to_all(value, axis, split_axis=0, concat_axis=0, tiled=True, axis...  3.88 us
  transfers between devices with their start and end apart: 9, of which 4 were waited for; matrix products, arithmetic and copies ran while one was open for 0% of the time, Pallas kernels for 7%

profile of v3, /device:TPU:1, one launch (start us, length us, event | category | flops | bytes accessed | tf_op | source)
XLA Modules:
  0.0 114.5 jit_solution(2316596014381331943)
XLA Ops:
  0.7 12.0 %all-to-all-start = ((f32[16,2,16,128]{3,2,1,0:T(8,128)}), f32[16,2,16,128]{3,2,1,0:T(8,128)S(1)}, u32[]{:S(2)}, u32[]{:S(2)}) async-start(f32[16,2,16,128]{3,2,1,0:T(8,128)} %bitcast.8), calls=%async_computation | async-start | bytes 524288 | tf_op jit(solution)/shard_map/all_to_all | solution.py:486
  12.7 0.7 copy-done.7
  13.3 1.7 %shard_map.121 = (f32[2,2,64,128]{3,2,1,0:T(8,128)S(1)}, f32[2,2,64,128]{3,2,1,0:T(8,128)S(1)}, f32[2,2,64,128]{3,2,1,0:T(8,128)S(1)}, f32[2,2,64,128]{3,2,1,0:T(8,128)S(1)}) custom-call(s32[2,9]{1,0:T(2,128)S(1)} %copy-done.7, f32[2,256,128]{2,1,0:T(8,128)S(1)} %copy-done, f32[2,256,128]{2,1,0:T(8,128)S(1)} %copy-done.1, f32[2,256,128]{2,1,0:T(8,128)} %refs_4_.6, ...), custom_call_target="tpu_custom_call" | custom-call | bytes 1343488 | tf_op jit(solution)/shard_map/pallas_call | solution.py:446
  15.0 3.1 %collective-permute-start = (f32[2,2,64,128]{3,2,1,0:T(8,128)S(1)}, f32[2,2,64,128]{3,2,1,0:T(8,128)S(1)}, u32[]{:S(2)}, u32[]{:S(2)}) collective-permute-start(f32[2,2,64,128]{3,2,1,0:T(8,128)S(1)} %get-tuple-element.31), channel_id=1, source_target_pairs={{480,496},{496,0},{0,16},{16,480},{32,48},{48,64},{64,80},{80,32},... | collective-permute-start | bytes 393224 | tf_op jit(solution)/shard_map/ppermute | solution.py:482
  18.2 7.3 %collective-permute-start.1 = (f32[2,2,64,128]{3,2,1,0:T(8,128)S(1)}, f32[2,2,64,128]{3,2,1,0:T(8,128)S(1)}, u32[]{:S(2)}, u32[]{:S(2)}) collective-permute-start(f32[2,2,64,128]{3,2,1,0:T(8,128)S(1)} %get-tuple-element.32), channel_id=1, source_target_pairs={{480,0},{496,16},{0,480},{16,496},{32,64},{48,80},{64,32},{80,48},... | collective-permute-start | bytes 393224 | tf_op jit(solution)/shard_map/ppermute | solution.py:482
  25.5 5.3 %collective-permute-start.2 = (f32[2,2,64,128]{3,2,1,0:T(8,128)S(1)}, f32[2,2,64,128]{3,2,1,0:T(8,128)S(1)}, u32[]{:S(2)}, u32[]{:S(2)}) collective-permute-start(f32[2,2,64,128]{3,2,1,0:T(8,128)S(1)} %get-tuple-element.33), channel_id=1, source_target_pairs={{480,16},{496,480},{0,496},{16,0},{32,80},{48,32},{64,48},{80,64},... | collective-permute-start | bytes 393224 | tf_op jit(solution)/shard_map/ppermute | solution.py:482
  30.8 1.3 %shard_map.122.refs_11_ = f32[2,256,128]{2,1,0:T(8,128)S(1)} custom-call(s32[2,9]{1,0:T(2,128)S(1)} %copy-done.8, s32[2]{0:T(128)S(1)} %copy-done.9, f32[2,256,128]{2,1,0:T(8,128)S(1)} %copy-done, f32[2,256,128]{2,1,0:T(8,128)S(1)} %copy-done.1), custom_call_target="tpu_custom_call" | custom-call | flops 201326592 | bytes 786432 | tf_op jit(solution)/shard_map/pallas_call | solution.py:446
  32.2 0.8 collective-permute-done.2.refs_9_.refs_10_
  33.0 1.9 %shard_map.123 = (f32[2,256,128]{2,1,0:T(8,128)S(1)}, f32[2,256,128]{2,1,0:T(8,128)S(1)}, f32[2,256,128]{2,1,0:T(8,128)S(1)}, f32[8,7,8,128]{3,2,1,0:T(8,128)}) custom-call(s32[2,9]{1,0:T(2,128)S(1)} %copy-done.8, s32[2]{0:T(128)S(1)} %copy-done.9, f32[16,2,16,128]{3,2,1,0:T(8,128)S(1)} %all-to-all-done.refs_2_, f32[2,256,128]{2,1,0:T(8,128)S(1)} %copy-done, ...), custom_call_target="tpu_custom_call" | custom-call | flops 50331648 | bytes 3112960 | tf_op jit(solution)/shard_map/pallas_call | solution.py:446
  34.9 3.8 %all-to-all-start.1 = ((f32[8,7,8,128]{3,2,1,0:T(8,128)}), f32[8,7,8,128]{3,2,1,0:T(8,128)S(1)}, u32[]{:S(2)}, u32[]{:S(2)}) async-start(f32[8,7,8,128]{3,2,1,0:T(8,128)} %get-tuple-element.34), calls=%async_computation.1 | async-start | bytes 458752 | tf_op jit(solution)/shard_map/all_to_all | solution.py:486
  38.7 0.6 shard_map.124.refs_16_
  39.7 4.0 %shard_map.125 = (f32[2,256,256]{2,1,0:T(8,128)}, f32[2,256,256]{2,1,0:T(8,128)}, f32[2,256,256]{2,1,0:T(8,128)}, f32[2,64,256]{2,1,0:T(8,128)}, f32[2,64,256]{2...) custom-call(s32[2,9]{1,0:T(2,128)S(1)} %copy-done.8, ...), custom_call_target="tpu_custom_call" | custom-call | flops 402653184 | bytes 4521984 | tf_op jit(solution)/shard_map/pallas_call | solution.py:446
  43.7 3.9 %all-to-all-done.1.refs_2_ = f32[8,7,8,128]{3,2,1,0:T(8,128)S(1)} async-done(((f32[8,7,8,128]{3,2,1,0:T(8,128)}), f32[8,7,8,128]{3,2,1,0:T(8,128)S(1)}, u32[]{:S(2)}, u32[]{:S(2)}) %all-to-all-start.1) | async-done | bytes 229408 | tf_op jit(solution)/shard_map/all_to_all | solution.py:486
  47.6 1.6 %shard_map.126 = f32[4,8,7,8,128]{4,3,2,1,0:T(8,128)} custom-call(s32[2,9]{1,0:T(2,128)S(1)} %copy-done.8, s32[2]{0:T(128)S(1)} %copy-done.9, f32[8,7,8,128]{3,2,1,0:T(8,128)S(1)} %all-to-all-done.1.refs_2_, f32[2,256,128]{2,1,0:T(8,128)S(1)} %copy-done), custom_call_target="tpu_custom_call" | custom-call | bytes 1409024 | tf_op jit(solution)/shard_map/pallas_call | solution.py:446
  49.2 6.1 %all-to-all-start.2 = ((f32[4,8,7,8,128]{4,3,2,1,0:T(8,128)}), f32[4,8,7,8,128]{4,3,2,1,0:T(8,128)S(1)}, u32[]{:S(2)}, u32[]{:S(2)}) async-start(f32[4,8,7,8,128]{4,3,2,1,0:T(8,128)} %shard_map.126), calls=%async_computation.2 | async-start | bytes 1835008 | tf_op jit(solution)/shard_map/all_to_all | solution.py:486
  55.3 3.4 %collective-permute-start.3 = (f32[3,64,128]{2,1,0:T(8,128)S(1)}, f32[3,64,128]{2,1,0:T(8,128)S(1)}, u32[]{:S(2)}, u32[]{:S(2)}) collective-permute-start(f32[3,64,128]{2,1,0:T(8,128)S(1)} %shard_map.124.refs_16_), channel_id=1, source_target_pairs={{480,496},{496,0},{0,16},{16,480},{32,48},{48,64},{64,80},{80,32},... | collective-permute-start | bytes 294920 | tf_op jit(solution)/shard_map/ppermute | solution.py:482
  58.6 2.2 %collective-permute-start.4 = (f32[3,64,128]{2,1,0:T(8,128)S(1)}, f32[3,64,128]{2,1,0:T(8,128)S(1)}, u32[]{:S(2)}, u32[]{:S(2)}) collective-permute-start(f32[3,64,128]{2,1,0:T(8,128)S(1)} %shard_map.124.refs_16_), channel_id=1, source_target_pairs={{480,0},{496,16},{0,480},{16,496},{32,64},{48,80},{64,32},{80,48},... | collective-permute-start | bytes 294920 | tf_op jit(solution)/shard_map/ppermute | solution.py:482
  60.8 6.2 %collective-permute-start.5 = (f32[3,64,128]{2,1,0:T(8,128)S(1)}, f32[3,64,128]{2,1,0:T(8,128)S(1)}, u32[]{:S(2)}, u32[]{:S(2)}) collective-permute-start(f32[3,64,128]{2,1,0:T(8,128)S(1)} %shard_map.124.refs_16_), channel_id=1, source_target_pairs={{480,16},{496,480},{0,496},{16,0},{32,80},{48,32},{64,48},{80,64},... | collective-permute-start | bytes 294920 | tf_op jit(solution)/shard_map/ppermute | solution.py:482
  67.0 1.2 %collective-permute-done.4.refs_18_ = f32[3,64,128]{2,1,0:T(8,128)S(1)} collective-permute-done((f32[3,64,128]{2,1,0:T(8,128)S(1)}, f32[3,64,128]{2,1,0:T(8,128)S(1)}, u32[]{:S(2)}, u32[]{:S(2)}) %collective-permute-start.4) | collective-permute-done | bytes 98336 | tf_op jit(solution)/shard_map/ppermute | solution.py:482
  68.2 2.6 %collective-permute-done.5.refs_19_ = f32[3,64,128]{2,1,0:T(8,128)S(1)} collective-permute-done((f32[3,64,128]{2,1,0:T(8,128)S(1)}, f32[3,64,128]{2,1,0:T(8,128)S(1)}, u32[]{:S(2)}, u32[]{:S(2)}) %collective-permute-start.5) | collective-permute-done | bytes 98336 | tf_op jit(solution)/shard_map/ppermute | solution.py:482
  70.8 0.6 copy-done.12
  71.5 9.9 %shard_map.127 = f32[16,3,2,16,128]{4,3,2,1,0:T(8,128)S(1)} custom-call(s32[2,9]{1,0:T(2,128)S(1)} %copy-done.8, s32[2]{0:T(128)S(1)} %copy-done.9, f32[4,8,7,8,128]{4,3,2,1,0:T(8,128)S(1)} %all-to-all-done.2.refs_2_, f32[2,256,128]{2,1,0:T(8,128)S(1)} %copy-done, f32[2,256,128]{2,1,0:T(8,128)} %refs_4_.7, ...), custom_call_target="tpu_custom_call" | custom-call | flops 1610612736 | bytes 5668864 | tf_op jit(solution)/shard_map/pallas_call | solution.py:446
  81.4 32.2 %all_to_all.20 = f32[16,3,2,16,128]{4,3,2,1,0:T(8,128)S(1)} all-to-all(f32[16,3,2,16,128]{4,3,2,1,0:T(8,128)S(1)} %shard_map.127), channel_id=1, replica_groups=mesh['seq'=32,'head'=16] {'head'}, dimensions={0} | all-to-all | bytes 1572864 | tf_op jit(solution)/shard_map/all_to_all | solution.py:486
  113.6 0.9 fusion
  (29 shorter events, 0.4 us)
Async XLA Ops:
  0.6 12.0 %copy-start = (f32[2,256,128]{2,1,0:T(8,128)S(1)}, f32[2,256,128]{2,1,0:T(8,128)}, u32[]{:S(2)}) copy-start(f32[2,256,128]{2,1,0:T(8,128)} %refs_3_.11) | copy-start | bytes 786436
  0.6 12.0 %copy-start.1 = (f32[2,256,128]{2,1,0:T(8,128)S(1)}, f32[2,256,128]{2,1,0:T(8,128)}, u32[]{:S(2)}) copy-start(f32[2,256,128]{2,1,0:T(8,128)} %refs_4_.7) | copy-start | bytes 786436
  0.7 32.3 %all-to-all-start = ((f32[16,2,16,128]{3,2,1,0:T(8,128)}), f32[16,2,16,128]{3,2,1,0:T(8,128)S(1)}, u32[]{:S(2)}, u32[]{:S(2)}) async-start(f32[16,2,16,128]{3,2,1,0:T(8,128)} %bitcast.8), calls=%async_computation | async-start | bytes 524288 | tf_op jit(solution)/shard_map/all_to_all | solution.py:486
  12.6 0.7 copy-start.7
  15.0 17.1 %collective-permute-start = (f32[2,2,64,128]{3,2,1,0:T(8,128)S(1)}, f32[2,2,64,128]{3,2,1,0:T(8,128)S(1)}, u32[]{:S(2)}, u32[]{:S(2)}) collective-permute-start(f32[2,2,64,128]{3,2,1,0:T(8,128)S(1)} %get-tuple-element.31), channel_id=1, source_target_pairs={{480,496},{496,0},{0,16},{16,480},{32,48},{48,64},{64,80},{80,32},... | collective-permute-start | bytes 393224 | tf_op jit(solution)/shard_map/ppermute | solution.py:482
  18.2 12.6 %copy-start.8 = (s32[2,9]{1,0:T(2,128)S(1)}, s32[2,9]{1,0:T(2,128)}, u32[]{:S(2)}) copy-start(s32[2,9]{1,0:T(2,128)} %refs_0_.13) | copy-start | bytes 220
  18.2 12.6 %copy-start.9 = (s32[2]{0:T(128)S(1)}, s32[2]{0:T(128)}, u32[]{:S(2)}) copy-start(s32[2]{0:T(128)} %refs_1_.13) | copy-start | bytes 28
  18.2 14.0 %collective-permute-start.1 = (f32[2,2,64,128]{3,2,1,0:T(8,128)S(1)}, f32[2,2,64,128]{3,2,1,0:T(8,128)S(1)}, u32[]{:S(2)}, u32[]{:S(2)}) collective-permute-start(f32[2,2,64,128]{3,2,1,0:T(8,128)S(1)} %get-tuple-element.32), channel_id=1, source_target_pairs={{480,0},{496,16},{0,480},{16,496},{32,64},{48,80},{64,32},{80,48},... | collective-permute-start | bytes 393224 | tf_op jit(solution)/shard_map/ppermute | solution.py:482
  25.4 7.5 %copy-start.2 = (f32[2,256,128]{2,1,0:T(8,128)S(1)}, f32[2,256,128]{2,1,0:T(8,128)}, u32[]{:S(2)}) copy-start(f32[2,256,128]{2,1,0:T(8,128)} %refs_4_.6) | copy-start | bytes 786436
  25.5 7.5 %copy-start.3 = (f32[2,256,128]{2,1,0:T(8,128)S(1)}, f32[2,256,128]{2,1,0:T(8,128)}, u32[]{:S(2)}) copy-start(f32[2,256,128]{2,1,0:T(8,128)} %refs_10_.1) | copy-start | bytes 786436
  25.5 7.5 %collective-permute-start.2 = (f32[2,2,64,128]{3,2,1,0:T(8,128)S(1)}, f32[2,2,64,128]{3,2,1,0:T(8,128)S(1)}, u32[]{:S(2)}, u32[]{:S(2)}) collective-permute-start(f32[2,2,64,128]{3,2,1,0:T(8,128)S(1)} %get-tuple-element.33), channel_id=1, source_target_pairs={{480,16},{496,480},{0,496},{16,0},{32,80},{48,32},{64,48},{80,64},... | collective-permute-start | bytes 393224 | tf_op jit(solution)/shard_map/ppermute | solution.py:482
  34.9 12.7 %all-to-all-start.1 = ((f32[8,7,8,128]{3,2,1,0:T(8,128)}), f32[8,7,8,128]{3,2,1,0:T(8,128)S(1)}, u32[]{:S(2)}, u32[]{:S(2)}) async-start(f32[8,7,8,128]{3,2,1,0:T(8,128)} %get-tuple-element.34), calls=%async_computation.1 | async-start | bytes 458752 | tf_op jit(solution)/shard_map/all_to_all | solution.py:486
  38.7 0.8 copy-start.4
  38.7 0.9 copy-start.5
  38.7 1.0 copy-start.6
  49.2 21.6 %all-to-all-start.2 = ((f32[4,8,7,8,128]{4,3,2,1,0:T(8,128)}), f32[4,8,7,8,128]{4,3,2,1,0:T(8,128)S(1)}, u32[]{:S(2)}, u32[]{:S(2)}) async-start(f32[4,8,7,8,128]{4,3,2,1,0:T(8,128)} %shard_map.126), calls=%async_computation.2 | async-start | bytes 1835008 | tf_op jit(solution)/shard_map/all_to_all | solution.py:486
  55.3 11.7 %collective-permute-start.3 = (f32[3,64,128]{2,1,0:T(8,128)S(1)}, f32[3,64,128]{2,1,0:T(8,128)S(1)}, u32[]{:S(2)}, u32[]{:S(2)}) collective-permute-start(f32[3,64,128]{2,1,0:T(8,128)S(1)} %shard_map.124.refs_16_), channel_id=1, source_target_pairs={{480,496},{496,0},{0,16},{16,480},{32,48},{48,64},{64,80},{80,32},... | collective-permute-start | bytes 294920 | tf_op jit(solution)/shard_map/ppermute | solution.py:482
  58.6 9.6 %collective-permute-start.4 = (f32[3,64,128]{2,1,0:T(8,128)S(1)}, f32[3,64,128]{2,1,0:T(8,128)S(1)}, u32[]{:S(2)}, u32[]{:S(2)}) collective-permute-start(f32[3,64,128]{2,1,0:T(8,128)S(1)} %shard_map.124.refs_16_), channel_id=1, source_target_pairs={{480,0},{496,16},{0,480},{16,496},{32,64},{48,80},{64,32},{80,48},... | collective-permute-start | bytes 294920 | tf_op jit(solution)/shard_map/ppermute | solution.py:482
  60.8 10.0 %collective-permute-start.5 = (f32[3,64,128]{2,1,0:T(8,128)S(1)}, f32[3,64,128]{2,1,0:T(8,128)S(1)}, u32[]{:S(2)}, u32[]{:S(2)}) collective-permute-start(f32[3,64,128]{2,1,0:T(8,128)S(1)} %shard_map.124.refs_16_), channel_id=1, source_target_pairs={{480,16},{496,480},{0,496},{16,0},{32,80},{48,32},{64,48},{80,64},... | collective-permute-start | bytes 294920 | tf_op jit(solution)/shard_map/ppermute | solution.py:482
  67.0 3.8 %copy-start.10 = (f32[3,64,128]{2,1,0:T(8,128)}, f32[3,64,128]{2,1,0:T(8,128)S(1)}, u32[]{:S(2)}) copy-start(f32[3,64,128]{2,1,0:T(8,128)S(1)} %collective-permute-done.3.refs_17_) | copy-start | bytes 294916
  68.2 2.6 %copy-start.11 = (f32[3,64,128]{2,1,0:T(8,128)}, f32[3,64,128]{2,1,0:T(8,128)S(1)}, u32[]{:S(2)}) copy-start(f32[3,64,128]{2,1,0:T(8,128)S(1)} %collective-permute-done.4.refs_18_) | copy-start | bytes 294916
  70.8 0.7 copy-start.12

commit v4 on v3

--- a/solution.py
+++ b/solution.py
@@ -243,7 +243,7 @@
 
 
 def grad_kernel(
-    mid_off, far_off, x, o, q_buf, lse_buf, far_lse, key_lse, gq_buf, gk_buf, gv_buf, mid_g,
+    mid_off, far_off, x, o, q_buf, lse_buf, far_lses, key_lse, gq_buf, gk_buf, gv_buf, mid_g,
     key_delta, score_buf, far_ref,
 ):
     place, segment, pos = place_info()
@@ -273,18 +273,25 @@
     facts = far_ref[:, 3 * heads].reshape(rows, LANES)
     own = pl.ds(place * far_rows, far_rows)
     for head in range(heads):
+        far = pl.ds(far_off[head], far_rows, stride=count)
+        q_buf[...] = far_ref[:, heads + head].reshape(rows, width)
+        q_buf[own, :] = x.q[head, far, :]
+        all_k = far_ref[:, head].reshape(rows, width)
+        score_buf[head] = dot_nt(q_buf[...], all_k) * scale
+        far_lses[head] = log_add(
+            fact(facts, 2 * head, share), masked_lse(score_buf[head], causal)
+        )
+    for head in range(heads):
         mid_start = mid_off[head, segment]
         mid = pl.ds(mid_start, quarter, stride=GROUP)
         far = pl.ds(far_off[head], far_rows, stride=count)
         all_k = far_ref[:, head].reshape(rows, width)
         all_v = far_ref[:, heads + head].reshape(rows, width)
         all_g = far_ref[:, 2 * heads + head].reshape(rows, width)
-        far_q = x.q[head, far, :]
         q_buf[...] = all_v
-        q_buf[own, :] = far_q
+        q_buf[own, :] = x.q[head, far, :]
         all_q = q_buf[...]
-        score_buf[...] = dot_nt(all_q, all_k) * scale
-        far_lse[...] = log_add(fact(facts, 2 * head, share), masked_lse(score_buf[...], causal))
+        far_lse = far_lses.at[head]
         lse_buf[...] = x.lse[head]
         lse_buf[far, :] = far_lse[own, :]
 
@@ -301,7 +308,7 @@
         gq_buf[mid, :] = gq_buf[mid, :] + dot_nn(grad_scores, x.mid_k[head]) * scale
 
         dropped, grad_scores = pair_terms(
-            score_buf[own, :], far_allowed, lse_buf[far, :],
+            score_buf[head, own, :], far_allowed, lse_buf[far, :],
             fact(far_ref[place, 3 * heads], 2 * head + 1, share),
             x.far_keep[head], far_ref[place, 2 * heads + head], all_v,
         )
@@ -350,19 +357,11 @@
 
 
 class Fetched:
-    def __init__(self, copies, ref):
-        self.copies, self.ref, self.shape, self.seen = copies, ref, ref.shape, set()
-
-    def wait(self, head):
-        if head not in self.seen:
-            self.seen.add(head)
-            self.copies[head].wait()
+    def __init__(self, ref, arrive):
+        self.ref, self.shape, self.arrive = ref, ref.shape, arrive
 
     def __getitem__(self, index):
-        leading = index[0] if isinstance(index, tuple) else index
-        for head in range(len(self.copies)):
-            if len(self.copies) == 1 or not isinstance(leading, int) or leading == head:
-                self.wait(head)
+        self.arrive()
         return self.ref[index]
 
 
@@ -386,7 +385,6 @@
 
 
 def call(kernel, scalars, arrays, outs, scratch=(), flops=0, fetched=()):
-    heads = 2
     names = list(arrays)
     loads = [name for name in names if name in fetched]
     out_names = [name.rstrip("+") for name in outs]
@@ -405,20 +403,20 @@
         in_bufs, out_bufs, extra = take(len(loads)), take(len(saves)), take(len(scratch))
         in_sems, out_sems = refs
         given, written = dict(zip(names, in_refs)), dict(zip(out_names, out_refs))
-        copies = {name: {} for name in loads}
-        used = 0
-        for head in range(heads):
-            for name, buf in zip(loads, in_bufs):
-                whole = buf.shape[0] != heads
-                if whole and head:
-                    continue
-                part = slice(None) if whole else head
-                copy = pltpu.make_async_copy(given[name].at[part], buf.at[part], in_sems.at[used])
-                copy.start()
-                copies[name][head] = copy
-                used += 1
-        moving = {name: Fetched(copies[name], buf) for name, buf in zip(loads, in_bufs)}
-        loaded = Loaded({**given, **moving})
+        copies = [
+            pltpu.make_async_copy(given[name], buf, in_sems.at[i])
+            for i, (name, buf) in enumerate(zip(loads, in_bufs))
+        ]
+        for copy in copies:
+            copy.start()
+
+        def arrive():
+            while copies:
+                copies.pop(0).wait()
+
+        loaded = Loaded(
+            {**given, **{name: Fetched(buf, arrive) for name, buf in zip(loads, in_bufs)}}
+        )
         buffers = dict(zip(saves, out_bufs))
         writes = []
 
@@ -432,9 +430,7 @@
 
         sent = set()
         kernel(*scalar_refs, loaded, Stored({**written, **buffers}, send), *extra)
-        for name in loads:
-            for head in copies[name]:
-                moving[name].wait(head)
+        arrive()
         for name in saves:
             if name not in sent:
                 send(name)
@@ -458,7 +454,7 @@
         + [pltpu.VMEM(shapes[name], jnp.float32) for name in saves]
         + [pltpu.VMEM(shape, jnp.float32) for shape in scratch]
         + [
-            pltpu.SemaphoreType.DMA((max(heads * len(loads), 1),)),
+            pltpu.SemaphoreType.DMA((max(len(loads), 1),)),
             pltpu.SemaphoreType.DMA((max(2 * len(saves), 1),)),
         ],
         cost_estimate=pl.CostEstimate(flops=flops, transcendentals=0, bytes_accessed=moved),
@@ -577,8 +573,10 @@
             **{name: terms[name] for name in term_shapes}, **mid_rows, "kv0": kv["kv0"],
         },
         {"stacked+": (parts, 3, heads, rows // parts, width)},
-        scratch=((rows, width),) * 9
-        + ((rows, rows), (count, 3 * heads + 1, far_rows, width)),
+        scratch=((rows, width),) * 2
+        + (whole,)
+        + ((rows, width),) * 6
+        + (pairs, (count, 3 * heads + 1, far_rows, width)),
         flops=8 * block,
         fetched=("k", "rows1", "rows2", "rows3", *terms),
     )["stacked"]

time: 116 us -> 113 us (0.974)
  Pallas kernels: 21 us -> 18.2 us
    pallas_call x7, Pallas kernels: 21 us -> 18.2 us  [call(): pl.pallas_call(run, out_shape=[pltpu.HBM(shape, jnp.float32) if name in s...]
where the time goes in v4:
time: 113 us; the launch traced here: 112 us
  starting transfers between devices  49.3 us (44%)
  blocking collectives  32.2 us (28%)
  Pallas kernels  18.2 us (16%)
  waiting for transfers between devices  8.51 us (8%)
  local copies, waits for them, and re-layouts  2.62 us (2%)
    all_to_all x1, blocking collectives, exchange(): lax.all_to_all(value, axis, split_axis=0, concat_axis=0, tiled=True, axis...  32.2 us
    ppermute x6, starting transfers between devices, turned(): return lax.ppermute(value, 'seq', pairs)  27.4 us
    all_to_all x3, starting transfers between devices, exchange(): lax.all_to_all(value, axis, split_axis=0, concat_axis=0, tiled=True, axis...  21.9 us
    pallas_call x7, Pallas kernels, call(): pl.pallas_call(run, out_shape=[pltpu.HBM(shape, jnp.float32) if name in s...  18.2 us
    ppermute x6, waiting for transfers between devices, turned(): return lax.ppermute(value, 'seq', pairs)  4.63 us
    all_to_all x3, waiting for transfers between devices, exchange(): lax.all_to_all(value, axis, split_axis=0, concat_axis=0, tiled=True, axis...  3.88 us
  transfers between devices with their start and end apart: 9, of which 4 were waited for; matrix products, arithmetic and copies ran while one was open for 0% of the time, Pallas kernels for 7%

profile of v4, /device:TPU:1, one launch (start us, length us, event | category | flops | bytes accessed | tf_op | source)
XLA Modules:
  0.0 111.6 jit_solution(14436576928041457760)
XLA Ops:
  0.7 12.0 %all-to-all-start = ((f32[16,2,16,128]{3,2,1,0:T(8,128)}), f32[16,2,16,128]{3,2,1,0:T(8,128)S(1)}, u32[]{:S(2)}, u32[]{:S(2)}) async-start(f32[16,2,16,128]{3,2,1,0:T(8,128)} %bitcast.8), calls=%async_computation | async-start | bytes 524288 | tf_op jit(solution)/shard_map/all_to_all | solution.py:482
  12.7 0.7 copy-done.7
  13.3 1.6 %shard_map.121 = (f32[2,2,64,128]{3,2,1,0:T(8,128)S(1)}, f32[2,2,64,128]{3,2,1,0:T(8,128)S(1)}, f32[2,2,64,128]{3,2,1,0:T(8,128)S(1)}, f32[2,2,64,128]{3,2,1,0:T(8,128)S(1)}) custom-call(s32[2,9]{1,0:T(2,128)S(1)} %copy-done.7, f32[2,256,128]{2,1,0:T(8,128)S(1)} %copy-done, f32[2,256,128]{2,1,0:T(8,128)S(1)} %copy-done.1, f32[2,256,128]{2,1,0:T(8,128)} %refs_4_.6, ...), custom_call_target="tpu_custom_call" | custom-call | bytes 1343488 | tf_op jit(solution)/shard_map/pallas_call | solution.py:442
  14.9 3.1 %collective-permute-start = (f32[2,2,64,128]{3,2,1,0:T(8,128)S(1)}, f32[2,2,64,128]{3,2,1,0:T(8,128)S(1)}, u32[]{:S(2)}, u32[]{:S(2)}) collective-permute-start(f32[2,2,64,128]{3,2,1,0:T(8,128)S(1)} %get-tuple-element.31), channel_id=1, source_target_pairs={{480,496},{496,0},{0,16},{16,480},{32,48},{48,64},{64,80},{80,32},... | collective-permute-start | bytes 393224 | tf_op jit(solution)/shard_map/ppermute | solution.py:478
  18.1 7.3 %collective-permute-start.1 = (f32[2,2,64,128]{3,2,1,0:T(8,128)S(1)}, f32[2,2,64,128]{3,2,1,0:T(8,128)S(1)}, u32[]{:S(2)}, u32[]{:S(2)}) collective-permute-start(f32[2,2,64,128]{3,2,1,0:T(8,128)S(1)} %get-tuple-element.32), channel_id=1, source_target_pairs={{480,0},{496,16},{0,480},{16,496},{32,64},{48,80},{64,32},{80,48},... | collective-permute-start | bytes 393224 | tf_op jit(solution)/shard_map/ppermute | solution.py:478
  25.4 5.3 %collective-permute-start.2 = (f32[2,2,64,128]{3,2,1,0:T(8,128)S(1)}, f32[2,2,64,128]{3,2,1,0:T(8,128)S(1)}, u32[]{:S(2)}, u32[]{:S(2)}) collective-permute-start(f32[2,2,64,128]{3,2,1,0:T(8,128)S(1)} %get-tuple-element.33), channel_id=1, source_target_pairs={{480,16},{496,480},{0,496},{16,0},{32,80},{48,32},{64,48},{80,64},... | collective-permute-start | bytes 393224 | tf_op jit(solution)/shard_map/ppermute | solution.py:478
  30.7 1.3 %shard_map.122.refs_11_ = f32[2,256,128]{2,1,0:T(8,128)S(1)} custom-call(s32[2,9]{1,0:T(2,128)S(1)} %copy-done.8, s32[2]{0:T(128)S(1)} %copy-done.9, f32[2,256,128]{2,1,0:T(8,128)S(1)} %copy-done, f32[2,256,128]{2,1,0:T(8,128)S(1)} %copy-done.1), custom_call_target="tpu_custom_call" | custom-call | flops 201326592 | bytes 786432 | tf_op jit(solution)/shard_map/pallas_call | solution.py:442
  32.1 0.8 collective-permute-done.2.refs_9_.refs_10_
  32.9 1.9 %shard_map.123 = (f32[2,256,128]{2,1,0:T(8,128)S(1)}, f32[2,256,128]{2,1,0:T(8,128)S(1)}, f32[2,256,128]{2,1,0:T(8,128)S(1)}, f32[8,7,8,128]{3,2,1,0:T(8,128)}) custom-call(s32[2,9]{1,0:T(2,128)S(1)} %copy-done.8, s32[2]{0:T(128)S(1)} %copy-done.9, f32[16,2,16,128]{3,2,1,0:T(8,128)S(1)} %all-to-all-done.refs_2_, f32[2,256,128]{2,1,0:T(8,128)S(1)} %copy-done, ...), custom_call_target="tpu_custom_call" | custom-call | flops 50331648 | bytes 3112960 | tf_op jit(solution)/shard_map/pallas_call | solution.py:442
  34.8 3.8 %all-to-all-start.1 = ((f32[8,7,8,128]{3,2,1,0:T(8,128)}), f32[8,7,8,128]{3,2,1,0:T(8,128)S(1)}, u32[]{:S(2)}, u32[]{:S(2)}) async-start(f32[8,7,8,128]{3,2,1,0:T(8,128)} %get-tuple-element.34), calls=%async_computation.1 | async-start | bytes 458752 | tf_op jit(solution)/shard_map/all_to_all | solution.py:482
  38.7 0.6 shard_map.124.refs_16_
  39.7 4.0 %shard_map.125 = (f32[2,256,256]{2,1,0:T(8,128)}, f32[2,256,256]{2,1,0:T(8,128)}, f32[2,256,256]{2,1,0:T(8,128)}, f32[2,64,256]{2,1,0:T(8,128)}, f32[2,64,256]{2...) custom-call(s32[2,9]{1,0:T(2,128)S(1)} %copy-done.8, ...), custom_call_target="tpu_custom_call" | custom-call | flops 402653184 | bytes 4521984 | tf_op jit(solution)/shard_map/pallas_call | solution.py:442
  43.7 3.9 %all-to-all-done.1.refs_2_ = f32[8,7,8,128]{3,2,1,0:T(8,128)S(1)} async-done(((f32[8,7,8,128]{3,2,1,0:T(8,128)}), f32[8,7,8,128]{3,2,1,0:T(8,128)S(1)}, u32[]{:S(2)}, u32[]{:S(2)}) %all-to-all-start.1) | async-done | bytes 229408 | tf_op jit(solution)/shard_map/all_to_all | solution.py:482
  47.5 1.6 %shard_map.126 = f32[4,8,7,8,128]{4,3,2,1,0:T(8,128)} custom-call(s32[2,9]{1,0:T(2,128)S(1)} %copy-done.8, s32[2]{0:T(128)S(1)} %copy-done.9, f32[8,7,8,128]{3,2,1,0:T(8,128)S(1)} %all-to-all-done.1.refs_2_, f32[2,256,128]{2,1,0:T(8,128)S(1)} %copy-done), custom_call_target="tpu_custom_call" | custom-call | bytes 1409024 | tf_op jit(solution)/shard_map/pallas_call | solution.py:442
  49.1 6.1 %all-to-all-start.2 = ((f32[4,8,7,8,128]{4,3,2,1,0:T(8,128)}), f32[4,8,7,8,128]{4,3,2,1,0:T(8,128)S(1)}, u32[]{:S(2)}, u32[]{:S(2)}) async-start(f32[4,8,7,8,128]{4,3,2,1,0:T(8,128)} %shard_map.126), calls=%async_computation.2 | async-start | bytes 1835008 | tf_op jit(solution)/shard_map/all_to_all | solution.py:482
  55.2 3.4 %collective-permute-start.3 = (f32[3,64,128]{2,1,0:T(8,128)S(1)}, f32[3,64,128]{2,1,0:T(8,128)S(1)}, u32[]{:S(2)}, u32[]{:S(2)}) collective-permute-start(f32[3,64,128]{2,1,0:T(8,128)S(1)} %shard_map.124.refs_16_), channel_id=1, source_target_pairs={{480,496},{496,0},{0,16},{16,480},{32,48},{48,64},{64,80},{80,32},... | collective-permute-start | bytes 294920 | tf_op jit(solution)/shard_map/ppermute | solution.py:478
  58.6 2.2 %collective-permute-start.4 = (f32[3,64,128]{2,1,0:T(8,128)S(1)}, f32[3,64,128]{2,1,0:T(8,128)S(1)}, u32[]{:S(2)}, u32[]{:S(2)}) collective-permute-start(f32[3,64,128]{2,1,0:T(8,128)S(1)} %shard_map.124.refs_16_), channel_id=1, source_target_pairs={{480,0},{496,16},{0,480},{16,496},{32,64},{48,80},{64,32},{80,48},... | collective-permute-start | bytes 294920 | tf_op jit(solution)/shard_map/ppermute | solution.py:478
  60.8 6.1 %collective-permute-start.5 = (f32[3,64,128]{2,1,0:T(8,128)S(1)}, f32[3,64,128]{2,1,0:T(8,128)S(1)}, u32[]{:S(2)}, u32[]{:S(2)}) collective-permute-start(f32[3,64,128]{2,1,0:T(8,128)S(1)} %shard_map.124.refs_16_), channel_id=1, source_target_pairs={{480,16},{496,480},{0,496},{16,0},{32,80},{48,32},{64,48},{80,64},... | collective-permute-start | bytes 294920 | tf_op jit(solution)/shard_map/ppermute | solution.py:478
  66.9 1.2 %collective-permute-done.4.refs_18_ = f32[3,64,128]{2,1,0:T(8,128)S(1)} collective-permute-done((f32[3,64,128]{2,1,0:T(8,128)S(1)}, f32[3,64,128]{2,1,0:T(8,128)S(1)}, u32[]{:S(2)}, u32[]{:S(2)}) %collective-permute-start.4) | collective-permute-done | bytes 98336 | tf_op jit(solution)/shard_map/ppermute | solution.py:478
  68.1 2.6 %collective-permute-done.5.refs_19_ = f32[3,64,128]{2,1,0:T(8,128)S(1)} collective-permute-done((f32[3,64,128]{2,1,0:T(8,128)S(1)}, f32[3,64,128]{2,1,0:T(8,128)S(1)}, u32[]{:S(2)}, u32[]{:S(2)}) %collective-permute-start.5) | collective-permute-done | bytes 98336 | tf_op jit(solution)/shard_map/ppermute | solution.py:478
  70.8 0.6 copy-done.12
  71.4 7.1 %shard_map.127 = f32[16,3,2,16,128]{4,3,2,1,0:T(8,128)S(1)} custom-call(s32[2,9]{1,0:T(2,128)S(1)} %copy-done.8, s32[2]{0:T(128)S(1)} %copy-done.9, f32[4,8,7,8,128]{4,3,2,1,0:T(8,128)S(1)} %all-to-all-done.2.refs_2_, f32[2,256,128]{2,1,0:T(8,128)S(1)} %copy-done, f32[2,256,128]{2,1,0:T(8,128)} %refs_4_.7, ...), custom_call_target="tpu_custom_call" | custom-call | flops 1610612736 | bytes 5668864 | tf_op jit(solution)/shard_map/pallas_call | solution.py:442
  78.6 32.2 %all_to_all.20 = f32[16,3,2,16,128]{4,3,2,1,0:T(8,128)S(1)} all-to-all(f32[16,3,2,16,128]{4,3,2,1,0:T(8,128)S(1)} %shard_map.127), channel_id=1, replica_groups=mesh['seq'=32,'head'=16] {'head'}, dimensions={0} | all-to-all | bytes 1572864 | tf_op jit(solution)/shard_map/all_to_all | solution.py:482
  110.7 0.9 fusion
  (29 shorter events, 0.4 us)
Async XLA Ops:
  0.6 12.0 %copy-start = (f32[2,256,128]{2,1,0:T(8,128)S(1)}, f32[2,256,128]{2,1,0:T(8,128)}, u32[]{:S(2)}) copy-start(f32[2,256,128]{2,1,0:T(8,128)} %refs_3_.11) | copy-start | bytes 786436
  0.6 12.0 %copy-start.1 = (f32[2,256,128]{2,1,0:T(8,128)S(1)}, f32[2,256,128]{2,1,0:T(8,128)}, u32[]{:S(2)}) copy-start(f32[2,256,128]{2,1,0:T(8,128)} %refs_4_.7) | copy-start | bytes 786436
  0.7 32.3 %all-to-all-start = ((f32[16,2,16,128]{3,2,1,0:T(8,128)}), f32[16,2,16,128]{3,2,1,0:T(8,128)S(1)}, u32[]{:S(2)}, u32[]{:S(2)}) async-start(f32[16,2,16,128]{3,2,1,0:T(8,128)} %bitcast.8), calls=%async_computation | async-start | bytes 524288 | tf_op jit(solution)/shard_map/all_to_all | solution.py:482
  12.6 0.7 copy-start.7
  14.9 17.1 %collective-permute-start = (f32[2,2,64,128]{3,2,1,0:T(8,128)S(1)}, f32[2,2,64,128]{3,2,1,0:T(8,128)S(1)}, u32[]{:S(2)}, u32[]{:S(2)}) collective-permute-start(f32[2,2,64,128]{3,2,1,0:T(8,128)S(1)} %get-tuple-element.31), channel_id=1, source_target_pairs={{480,496},{496,0},{0,16},{16,480},{32,48},{48,64},{64,80},{80,32},... | collective-permute-start | bytes 393224 | tf_op jit(solution)/shard_map/ppermute | solution.py:478
  18.1 12.6 %copy-start.8 = (s32[2,9]{1,0:T(2,128)S(1)}, s32[2,9]{1,0:T(2,128)}, u32[]{:S(2)}) copy-start(s32[2,9]{1,0:T(2,128)} %refs_0_.13) | copy-start | bytes 220
  18.1 12.6 %copy-start.9 = (s32[2]{0:T(128)S(1)}, s32[2]{0:T(128)}, u32[]{:S(2)}) copy-start(s32[2]{0:T(128)} %refs_1_.13) | copy-start | bytes 28
  18.1 14.0 %collective-permute-start.1 = (f32[2,2,64,128]{3,2,1,0:T(8,128)S(1)}, f32[2,2,64,128]{3,2,1,0:T(8,128)S(1)}, u32[]{:S(2)}, u32[]{:S(2)}) collective-permute-start(f32[2,2,64,128]{3,2,1,0:T(8,128)S(1)} %get-tuple-element.32), channel_id=1, source_target_pairs={{480,0},{496,16},{0,480},{16,496},{32,64},{48,80},{64,32},{80,48},... | collective-permute-start | bytes 393224 | tf_op jit(solution)/shard_map/ppermute | solution.py:478
  25.4 7.5 %copy-start.2 = (f32[2,256,128]{2,1,0:T(8,128)S(1)}, f32[2,256,128]{2,1,0:T(8,128)}, u32[]{:S(2)}) copy-start(f32[2,256,128]{2,1,0:T(8,128)} %refs_4_.6) | copy-start | bytes 786436
  25.4 7.5 %copy-start.3 = (f32[2,256,128]{2,1,0:T(8,128)S(1)}, f32[2,256,128]{2,1,0:T(8,128)}, u32[]{:S(2)}) copy-start(f32[2,256,128]{2,1,0:T(8,128)} %refs_10_.1) | copy-start | bytes 786436
  25.4 7.5 %collective-permute-start.2 = (f32[2,2,64,128]{3,2,1,0:T(8,128)S(1)}, f32[2,2,64,128]{3,2,1,0:T(8,128)S(1)}, u32[]{:S(2)}, u32[]{:S(2)}) collective-permute-start(f32[2,2,64,128]{3,2,1,0:T(8,128)S(1)} %get-tuple-element.33), channel_id=1, source_target_pairs={{480,16},{496,480},{0,496},{16,0},{32,80},{48,32},{64,48},{80,64},... | collective-permute-start | bytes 393224 | tf_op jit(solution)/shard_map/ppermute | solution.py:478
  34.8 12.7 %all-to-all-start.1 = ((f32[8,7,8,128]{3,2,1,0:T(8,128)}), f32[8,7,8,128]{3,2,1,0:T(8,128)S(1)}, u32[]{:S(2)}, u32[]{:S(2)}) async-start(f32[8,7,8,128]{3,2,1,0:T(8,128)} %get-tuple-element.34), calls=%async_computation.1 | async-start | bytes 458752 | tf_op jit(solution)/shard_map/all_to_all | solution.py:482
  38.7 0.8 copy-start.4
  38.7 0.9 copy-start.5
  38.7 1.0 copy-start.6
  49.1 21.6 %all-to-all-start.2 = ((f32[4,8,7,8,128]{4,3,2,1,0:T(8,128)}), f32[4,8,7,8,128]{4,3,2,1,0:T(8,128)S(1)}, u32[]{:S(2)}, u32[]{:S(2)}) async-start(f32[4,8,7,8,128]{4,3,2,1,0:T(8,128)} %shard_map.126), calls=%async_computation.2 | async-start | bytes 1835008 | tf_op jit(solution)/shard_map/all_to_all | solution.py:482
  55.2 11.7 %collective-permute-start.3 = (f32[3,64,128]{2,1,0:T(8,128)S(1)}, f32[3,64,128]{2,1,0:T(8,128)S(1)}, u32[]{:S(2)}, u32[]{:S(2)}) collective-permute-start(f32[3,64,128]{2,1,0:T(8,128)S(1)} %shard_map.124.refs_16_), channel_id=1, source_target_pairs={{480,496},{496,0},{0,16},{16,480},{32,48},{48,64},{64,80},{80,32},... | collective-permute-start | bytes 294920 | tf_op jit(solution)/shard_map/ppermute | solution.py:478
  58.6 9.6 %collective-permute-start.4 = (f32[3,64,128]{2,1,0:T(8,128)S(1)}, f32[3,64,128]{2,1,0:T(8,128)S(1)}, u32[]{:S(2)}, u32[]{:S(2)}) collective-permute-start(f32[3,64,128]{2,1,0:T(8,128)S(1)} %shard_map.124.refs_16_), channel_id=1, source_target_pairs={{480,0},{496,16},{0,480},{16,496},{32,64},{48,80},{64,32},{80,48},... | collective-permute-start | bytes 294920 | tf_op jit(solution)/shard_map/ppermute | solution.py:478
  60.8 10.0 %collective-permute-start.5 = (f32[3,64,128]{2,1,0:T(8,128)S(1)}, f32[3,64,128]{2,1,0:T(8,128)S(1)}, u32[]{:S(2)}, u32[]{:S(2)}) collective-permute-start(f32[3,64,128]{2,1,0:T(8,128)S(1)} %shard_map.124.refs_16_), channel_id=1, source_target_pairs={{480,16},{496,480},{0,496},{16,0},{32,80},{48,32},{64,48},{80,64},... | collective-permute-start | bytes 294920 | tf_op jit(solution)/shard_map/ppermute | solution.py:478
  66.9 3.8 %copy-start.10 = (f32[3,64,128]{2,1,0:T(8,128)}, f32[3,64,128]{2,1,0:T(8,128)S(1)}, u32[]{:S(2)}) copy-start(f32[3,64,128]{2,1,0:T(8,128)S(1)} %collective-permute-done.3.refs_17_) | copy-start | bytes 294916
  68.1 2.6 %copy-start.11 = (f32[3,64,128]{2,1,0:T(8,128)}, f32[3,64,128]{2,1,0:T(8,128)S(1)}, u32[]{:S(2)}) copy-start(f32[3,64,128]{2,1,0:T(8,128)S(1)} %collective-permute-done.4.refs_18_) | copy-start | bytes 294916
  70.8 0.7 copy-start.12

commit v5 on v4

--- a/solution.py
+++ b/solution.py
@@ -469,12 +469,16 @@
     return dict(zip(out_names, result))
 
 
-def turned(value, steps):
+def turned(value, steps, back_only=False):
     count = lax.axis_size("seq")
     pairs = []
     for first in range(-HALF, count - HALF, GROUP):
         for pos in range(GROUP):
-            pairs.append(((first + pos) % count, (first + (pos + steps) % GROUP) % count))
+            source, target = first + pos, first + (pos + steps) % GROUP
+            crosses = (source < count) != (target < count) or (source < 0) != (target < 0)
+            if crosses or (back_only and target > source):
+                continue
+            pairs.append((source % count, target % count))
     return lax.ppermute(value, "seq", pairs)
 
 
@@ -533,7 +537,7 @@
         rows_kernel, offsets, mid, {"rows+": (heads + 1, quarter, width)}
     )["rows"]
     mid_rows = {
-        f"rows{step}": turned(own_rows, step) if step else own_rows for step in range(GROUP)
+        f"rows{step}": turned(own_rows, step, True) if step else own_rows for step in range(GROUP)
     }
     term_shapes = {
         "scores": pairs,

time: 113 us -> 112 us (level)
  starting transfers between devices: 49.3 us -> 34.3 us
  waiting for transfers between devices: 8.51 us -> 22 us
  blocking collectives: 32.2 us -> 33.7 us
    ppermute x6, starting transfers between devices: 27.4 us -> 7.85 us  [turned(): return lax.ppermute(value, 'seq', pairs)]
    ppermute x6, waiting for transfers between devices: 4.63 us -> 18.1 us  [turned(): return lax.ppermute(value, 'seq', pairs)]
    all_to_all x3, starting transfers between devices: 21.9 us -> 26.4 us  [exchange(): lax.all_to_all(value, axis, split_axis=0, concat_axis=0, tiled=True, axis...]
    all_to_all x1, blocking collectives: 32.2 us -> 33.7 us  [exchange(): lax.all_to_all(value, axis, split_axis=0, concat_axis=0, tiled=True, axis...]
  transfers between devices with their start and end apart: 9 -> 9, of which waited for: 4 -> 3; matrix products, arithmetic and copies ran while one was open for 0% -> 0% of each run, Pallas kernels for 7% -> 7%
where the time goes in v5:
time: 112 us
  starting transfers between devices  34.3 us (31%)
  blocking collectives  33.7 us (30%)
  waiting for transfers between devices  22 us (20%)
  Pallas kernels  18.1 us (16%)
  local copies, waits for them, and re-layouts  2.62 us (2%)
    all_to_all x1, blocking collectives, exchange(): lax.all_to_all(value, axis, split_axis=0, concat_axis=0, tiled=True, axis...  33.7 us
    all_to_all x3, starting transfers between devices, exchange(): lax.all_to_all(value, axis, split_axis=0, concat_axis=0, tiled=True, axis...  26.4 us
    pallas_call x7, Pallas kernels, call(): pl.pallas_call(run, out_shape=[pltpu.HBM(shape, jnp.float32) if name in s...  18.1 us
    ppermute x6, waiting for transfers between devices, turned(): return lax.ppermute(value, 'seq', pairs)  18.1 us
    ppermute x6, starting transfers between devices, turned(): return lax.ppermute(value, 'seq', pairs)  7.85 us
    all_to_all x3, waiting for transfers between devices, exchange(): lax.all_to_all(value, axis, split_axis=0, concat_axis=0, tiled=True, axis...  3.88 us
  transfers between devices with their start and end apart: 9, of which 3 were waited for; matrix products, arithmetic and copies ran while one was open for 0% of the time, Pallas kernels for 7%

profile of v5, /device:TPU:1, one launch (start us, length us, event | category | flops | bytes accessed | tf_op | source)
XLA Modules:
  0.0 111.6 jit_solution(7116699856243397465)
XLA Ops:
  0.7 12.0 %all-to-all-start = ((f32[16,2,16,128]{3,2,1,0:T(8,128)}), f32[16,2,16,128]{3,2,1,0:T(8,128)S(1)}, u32[]{:S(2)}, u32[]{:S(2)}) async-start(f32[16,2,16,128]{3,2,1,0:T(8,128)} %bitcast.8), calls=%async_computation | async-start | bytes 524288 | tf_op jit(solution)/shard_map/all_to_all | solution.py:486
  12.7 0.7 copy-done.7
  13.3 1.6 %shard_map.121 = (f32[2,2,64,128]{3,2,1,0:T(8,128)S(1)}, f32[2,2,64,128]{3,2,1,0:T(8,128)S(1)}, f32[2,2,64,128]{3,2,1,0:T(8,128)S(1)}, f32[2,2,64,128]{3,2,1,0:T(8,128)S(1)}) custom-call(s32[2,9]{1,0:T(2,128)S(1)} %copy-done.7, f32[2,256,128]{2,1,0:T(8,128)S(1)} %copy-done, f32[2,256,128]{2,1,0:T(8,128)S(1)} %copy-done.1, f32[2,256,128]{2,1,0:T(8,128)} %refs_4_.6, ...), custom_call_target="tpu_custom_call" | custom-call | bytes 1343488 | tf_op jit(solution)/shard_map/pallas_call | solution.py:442
  14.9 3.1 %collective-permute-start = (f32[2,2,64,128]{3,2,1,0:T(8,128)S(1)}, f32[2,2,64,128]{3,2,1,0:T(8,128)S(1)}, u32[]{:S(2)}, u32[]{:S(2)}) collective-permute-start(f32[2,2,64,128]{3,2,1,0:T(8,128)S(1)} %get-tuple-element.31), channel_id=1, source_target_pairs={{480,496},{0,16},{32,48},{48,64},{64,80},{80,32},{96,112},{112,128... | collective-permute-start | bytes 393224 | tf_op jit(solution)/shard_map/ppermute | solution.py:482
  18.1 0.7 collective-permute-start.1
  18.8 1.4 %collective-permute-start.2 = (f32[2,2,64,128]{3,2,1,0:T(8,128)S(1)}, f32[2,2,64,128]{3,2,1,0:T(8,128)S(1)}, u32[]{:S(2)}, u32[]{:S(2)}) collective-permute-start(f32[2,2,64,128]{3,2,1,0:T(8,128)S(1)} %get-tuple-element.33), channel_id=1, source_target_pairs={{496,480},{16,0},{32,80},{48,32},{64,48},{80,64},{96,144},{112,96}... | collective-permute-start | bytes 393224 | tf_op jit(solution)/shard_map/ppermute | solution.py:482
  20.3 1.3 %shard_map.122.refs_11_ = f32[2,256,128]{2,1,0:T(8,128)S(1)} custom-call(s32[2,9]{1,0:T(2,128)S(1)} %copy-done.8, s32[2]{0:T(128)S(1)} %copy-done.9, f32[2,256,128]{2,1,0:T(8,128)S(1)} %copy-done, f32[2,256,128]{2,1,0:T(8,128)S(1)} %copy-done.1), custom_call_target="tpu_custom_call" | custom-call | flops 201326592 | bytes 786432 | tf_op jit(solution)/shard_map/pallas_call | solution.py:442
  21.6 6.8 %collective-permute-done.2.refs_9_.refs_10_ = f32[2,2,64,128]{3,2,1,0:T(8,128)S(1)} collective-permute-done((f32[2,2,64,128]{3,2,1,0:T(8,128)S(1)}, f32[2,2,64,128]{3,2,1,0:T(8,128)S(1)}, u32[]{:S(2)}, u32[]{:S(2)}) %collective-permute-start.2) | collective-permute-done | bytes 131104 | tf_op jit(solution)/shard_map/ppermute | solution.py:482
  28.4 1.9 %shard_map.123 = (f32[2,256,128]{2,1,0:T(8,128)S(1)}, f32[2,256,128]{2,1,0:T(8,128)S(1)}, f32[2,256,128]{2,1,0:T(8,128)S(1)}, f32[8,7,8,128]{3,2,1,0:T(8,128)}) custom-call(s32[2,9]{1,0:T(2,128)S(1)} %copy-done.8, s32[2]{0:T(128)S(1)} %copy-done.9, f32[16,2,16,128]{3,2,1,0:T(8,128)S(1)} %all-to-all-done.refs_2_, f32[2,256,128]{2,1,0:T(8,128)S(1)} %copy-done, ...), custom_call_target="tpu_custom_call" | custom-call | flops 50331648 | bytes 3112960 | tf_op jit(solution)/shard_map/pallas_call | solution.py:442
  30.3 8.4 %all-to-all-start.1 = ((f32[8,7,8,128]{3,2,1,0:T(8,128)}), f32[8,7,8,128]{3,2,1,0:T(8,128)S(1)}, u32[]{:S(2)}, u32[]{:S(2)}) async-start(f32[8,7,8,128]{3,2,1,0:T(8,128)} %get-tuple-element.34), calls=%async_computation.1 | async-start | bytes 458752 | tf_op jit(solution)/shard_map/all_to_all | solution.py:486
  38.7 0.6 shard_map.124.refs_16_
  39.3 0.2 copy-done.4
  39.7 4.0 %shard_map.125 = (f32[2,256,256]{2,1,0:T(8,128)}, f32[2,256,256]{2,1,0:T(8,128)}, f32[2,256,256]{2,1,0:T(8,128)}, f32[2,64,256]{2,1,0:T(8,128)}, f32[2,64,256]{2...) custom-call(s32[2,9]{1,0:T(2,128)S(1)} %copy-done.8, ...), custom_call_target="tpu_custom_call" | custom-call | flops 402653184 | bytes 4521984 | tf_op jit(solution)/shard_map/pallas_call | solution.py:442
  43.7 3.9 %all-to-all-done.1.refs_2_ = f32[8,7,8,128]{3,2,1,0:T(8,128)S(1)} async-done(((f32[8,7,8,128]{3,2,1,0:T(8,128)}), f32[8,7,8,128]{3,2,1,0:T(8,128)S(1)}, u32[]{:S(2)}, u32[]{:S(2)}) %all-to-all-start.1) | async-done | bytes 229408 | tf_op jit(solution)/shard_map/all_to_all | solution.py:486
  47.5 1.6 %shard_map.126 = f32[4,8,7,8,128]{4,3,2,1,0:T(8,128)} custom-call(s32[2,9]{1,0:T(2,128)S(1)} %copy-done.8, s32[2]{0:T(128)S(1)} %copy-done.9, f32[8,7,8,128]{3,2,1,0:T(8,128)S(1)} %all-to-all-done.1.refs_2_, f32[2,256,128]{2,1,0:T(8,128)S(1)} %copy-done), custom_call_target="tpu_custom_call" | custom-call | bytes 1409024 | tf_op jit(solution)/shard_map/pallas_call | solution.py:442
  49.1 6.1 %all-to-all-start.2 = ((f32[4,8,7,8,128]{4,3,2,1,0:T(8,128)}), f32[4,8,7,8,128]{4,3,2,1,0:T(8,128)S(1)}, u32[]{:S(2)}, u32[]{:S(2)}) async-start(f32[4,8,7,8,128]{4,3,2,1,0:T(8,128)} %shard_map.126), calls=%async_computation.2 | async-start | bytes 1835008 | tf_op jit(solution)/shard_map/all_to_all | solution.py:486
  55.2 0.7 collective-permute-start.3
  55.9 0.7 collective-permute-start.4
  56.5 1.3 %collective-permute-start.5 = (f32[3,64,128]{2,1,0:T(8,128)S(1)}, f32[3,64,128]{2,1,0:T(8,128)S(1)}, u32[]{:S(2)}, u32[]{:S(2)}) collective-permute-start(f32[3,64,128]{2,1,0:T(8,128)S(1)} %shard_map.124.refs_16_), channel_id=1, source_target_pairs={{496,480},{16,0},{48,32},{64,48},{80,64},{112,96},{128,112},{144,1... | collective-permute-start | bytes 294920 | tf_op jit(solution)/shard_map/ppermute | solution.py:482
  57.9 11.3 %collective-permute-done.5.refs_19_ = f32[3,64,128]{2,1,0:T(8,128)S(1)} collective-permute-done((f32[3,64,128]{2,1,0:T(8,128)S(1)}, f32[3,64,128]{2,1,0:T(8,128)S(1)}, u32[]{:S(2)}, u32[]{:S(2)}) %collective-permute-start.5) | collective-permute-done | bytes 98336 | tf_op jit(solution)/shard_map/ppermute | solution.py:482
  69.3 0.6 copy-done.12
  69.9 7.1 %shard_map.127 = f32[16,3,2,16,128]{4,3,2,1,0:T(8,128)S(1)} custom-call(s32[2,9]{1,0:T(2,128)S(1)} %copy-done.8, s32[2]{0:T(128)S(1)} %copy-done.9, f32[4,8,7,8,128]{4,3,2,1,0:T(8,128)S(1)} %all-to-all-done.2.refs_2_, f32[2,256,128]{2,1,0:T(8,128)S(1)} %copy-done, f32[2,256,128]{2,1,0:T(8,128)} %refs_4_.7, ...), custom_call_target="tpu_custom_call" | custom-call | flops 1610612736 | bytes 5668864 | tf_op jit(solution)/shard_map/pallas_call | solution.py:442
  77.0 33.7 %all_to_all.20 = f32[16,3,2,16,128]{4,3,2,1,0:T(8,128)S(1)} all-to-all(f32[16,3,2,16,128]{4,3,2,1,0:T(8,128)S(1)} %shard_map.127), channel_id=1, replica_groups=mesh['seq'=32,'head'=16] {'head'}, dimensions={0} | all-to-all | bytes 1572864 | tf_op jit(solution)/shard_map/all_to_all | solution.py:486
  110.7 0.9 fusion
  (29 shorter events, 0.2 us)
Async XLA Ops:
  0.6 12.0 %copy-start = (f32[2,256,128]{2,1,0:T(8,128)S(1)}, f32[2,256,128]{2,1,0:T(8,128)}, u32[]{:S(2)}) copy-start(f32[2,256,128]{2,1,0:T(8,128)} %refs_3_.11) | copy-start | bytes 786436
  0.6 12.0 %copy-start.1 = (f32[2,256,128]{2,1,0:T(8,128)S(1)}, f32[2,256,128]{2,1,0:T(8,128)}, u32[]{:S(2)}) copy-start(f32[2,256,128]{2,1,0:T(8,128)} %refs_4_.7) | copy-start | bytes 786436
  0.7 27.7 %all-to-all-start = ((f32[16,2,16,128]{3,2,1,0:T(8,128)}), f32[16,2,16,128]{3,2,1,0:T(8,128)S(1)}, u32[]{:S(2)}, u32[]{:S(2)}) async-start(f32[16,2,16,128]{3,2,1,0:T(8,128)} %bitcast.8), calls=%async_computation | async-start | bytes 524288 | tf_op jit(solution)/shard_map/all_to_all | solution.py:486
  12.6 0.7 copy-start.7
  14.9 6.7 %collective-permute-start = (f32[2,2,64,128]{3,2,1,0:T(8,128)S(1)}, f32[2,2,64,128]{3,2,1,0:T(8,128)S(1)}, u32[]{:S(2)}, u32[]{:S(2)}) collective-permute-start(f32[2,2,64,128]{3,2,1,0:T(8,128)S(1)} %get-tuple-element.31), channel_id=1, source_target_pairs={{480,496},{0,16},{32,48},{48,64},{64,80},{80,32},{96,112},{112,128... | collective-permute-start | bytes 393224 | tf_op jit(solution)/shard_map/ppermute | solution.py:482
  18.1 2.2 %copy-start.8 = (s32[2,9]{1,0:T(2,128)S(1)}, s32[2,9]{1,0:T(2,128)}, u32[]{:S(2)}) copy-start(s32[2,9]{1,0:T(2,128)} %refs_0_.13) | copy-start | bytes 220
  18.1 2.2 %copy-start.9 = (s32[2]{0:T(128)S(1)}, s32[2]{0:T(128)}, u32[]{:S(2)}) copy-start(s32[2]{0:T(128)} %refs_1_.13) | copy-start | bytes 28
  18.1 3.5 %collective-permute-start.1 = (f32[2,2,64,128]{3,2,1,0:T(8,128)S(1)}, f32[2,2,64,128]{3,2,1,0:T(8,128)S(1)}, u32[]{:S(2)}, u32[]{:S(2)}) collective-permute-start(f32[2,2,64,128]{3,2,1,0:T(8,128)S(1)} %get-tuple-element.32), channel_id=1, source_target_pairs={{32,64},{48,80},{64,32},{80,48},{96,128},{112,144},{128,96},{144,1... | collective-permute-start | bytes 393224 | tf_op jit(solution)/shard_map/ppermute | solution.py:482
  18.8 9.6 %copy-start.2 = (f32[2,256,128]{2,1,0:T(8,128)S(1)}, f32[2,256,128]{2,1,0:T(8,128)}, u32[]{:S(2)}) copy-start(f32[2,256,128]{2,1,0:T(8,128)} %refs_4_.6) | copy-start | bytes 786436
  18.8 9.6 %copy-start.3 = (f32[2,256,128]{2,1,0:T(8,128)S(1)}, f32[2,256,128]{2,1,0:T(8,128)}, u32[]{:S(2)}) copy-start(f32[2,256,128]{2,1,0:T(8,128)} %refs_10_.1) | copy-start | bytes 786436
  18.8 9.6 %collective-permute-start.2 = (f32[2,2,64,128]{3,2,1,0:T(8,128)S(1)}, f32[2,2,64,128]{3,2,1,0:T(8,128)S(1)}, u32[]{:S(2)}, u32[]{:S(2)}) collective-permute-start(f32[2,2,64,128]{3,2,1,0:T(8,128)S(1)} %get-tuple-element.33), channel_id=1, source_target_pairs={{496,480},{16,0},{32,80},{48,32},{64,48},{80,64},{96,144},{112,96}... | collective-permute-start | bytes 393224 | tf_op jit(solution)/shard_map/ppermute | solution.py:482
  30.3 17.2 %all-to-all-start.1 = ((f32[8,7,8,128]{3,2,1,0:T(8,128)}), f32[8,7,8,128]{3,2,1,0:T(8,128)S(1)}, u32[]{:S(2)}, u32[]{:S(2)}) async-start(f32[8,7,8,128]{3,2,1,0:T(8,128)} %get-tuple-element.34), calls=%async_computation.1 | async-start | bytes 458752 | tf_op jit(solution)/shard_map/all_to_all | solution.py:486
  38.7 0.8 copy-start.4
  38.7 0.9 copy-start.5
  38.7 1.0 copy-start.6
  49.1 20.1 %all-to-all-start.2 = ((f32[4,8,7,8,128]{4,3,2,1,0:T(8,128)}), f32[4,8,7,8,128]{4,3,2,1,0:T(8,128)S(1)}, u32[]{:S(2)}, u32[]{:S(2)}) async-start(f32[4,8,7,8,128]{4,3,2,1,0:T(8,128)} %shard_map.126), calls=%async_computation.2 | async-start | bytes 1835008 | tf_op jit(solution)/shard_map/all_to_all | solution.py:486
  55.2 2.6 %collective-permute-start.3 = (f32[3,64,128]{2,1,0:T(8,128)S(1)}, f32[3,64,128]{2,1,0:T(8,128)S(1)}, u32[]{:S(2)}, u32[]{:S(2)}) collective-permute-start(f32[3,64,128]{2,1,0:T(8,128)S(1)} %shard_map.124.refs_16_), channel_id=1, source_target_pairs={{80,32},{144,96},{208,160},{272,224},{336,288},{400,352},{464,416}... | collective-permute-start | bytes 294920 | tf_op jit(solution)/shard_map/ppermute | solution.py:482
  55.9 2.0 %collective-permute-start.4 = (f32[3,64,128]{2,1,0:T(8,128)S(1)}, f32[3,64,128]{2,1,0:T(8,128)S(1)}, u32[]{:S(2)}, u32[]{:S(2)}) collective-permute-start(f32[3,64,128]{2,1,0:T(8,128)S(1)} %shard_map.124.refs_16_), channel_id=1, source_target_pairs={{64,32},{80,48},{128,96},{144,112},{192,160},{208,176},{256,224},{... | collective-permute-start | bytes 294920 | tf_op jit(solution)/shard_map/ppermute | solution.py:482
  56.5 12.7 %collective-permute-start.5 = (f32[3,64,128]{2,1,0:T(8,128)S(1)}, f32[3,64,128]{2,1,0:T(8,128)S(1)}, u32[]{:S(2)}, u32[]{:S(2)}) collective-permute-start(f32[3,64,128]{2,1,0:T(8,128)S(1)} %shard_map.124.refs_16_), channel_id=1, source_target_pairs={{496,480},{16,0},{48,32},{64,48},{80,64},{112,96},{128,112},{144,1... | collective-permute-start | bytes 294920 | tf_op jit(solution)/shard_map/ppermute | solution.py:482
  57.9 11.4 %copy-start.10 = (f32[3,64,128]{2,1,0:T(8,128)}, f32[3,64,128]{2,1,0:T(8,128)S(1)}, u32[]{:S(2)}) copy-start(f32[3,64,128]{2,1,0:T(8,128)S(1)} %collective-permute-done.3.refs_17_) | copy-start | bytes 294916
  57.9 11.4 %copy-start.11 = (f32[3,64,128]{2,1,0:T(8,128)}, f32[3,64,128]{2,1,0:T(8,128)S(1)}, u32[]{:S(2)}) copy-start(f32[3,64,128]{2,1,0:T(8,128)S(1)} %collective-permute-done.4.refs_18_) | copy-start | bytes 294916
  69.2 0.7 copy-start.12

commit v6 on v5

--- a/solution.py
+++ b/solution.py
@@ -561,7 +561,7 @@
         scratch=((rows, width), (rows, rows)),
         flops=2 * block,
     )
-    column, own_rows, terms = lax.optimization_barrier((column, own_rows, terms))
+    column, mid_rows = lax.optimization_barrier((column, mid_rows))
     relay = call(
         relay_kernel,
         offsets,

time: 112 us -> 111 us (level)
  starting transfers between devices: 34.3 us -> 37.1 us
  waiting for transfers between devices: 22 us -> 19.7 us
    ppermute x6, waiting for transfers between devices: 18.1 us -> 10.5 us  [turned(): return lax.ppermute(value, 'seq', pairs)]
    all_to_all x3, waiting for transfers between devices: 3.88 us -> 9.18 us  [exchange(): lax.all_to_all(value, axis, split_axis=0, concat_axis=0, tiled=True, axis...]
    all_to_all x3, starting transfers between devices: 26.4 us -> 29.3 us  [exchange(): lax.all_to_all(value, axis, split_axis=0, concat_axis=0, tiled=True, axis...]
  transfers between devices with their start and end apart: 9 -> 9, of which waited for: 3 -> 4; matrix products, arithmetic and copies ran while one was open for 0% -> 0% of each run, Pallas kernels for 7% -> 7%
where the time goes in v6:
time: 111 us; the launch traced here: 110 us
  starting transfers between devices  37.1 us (33%)
  blocking collectives  32.8 us (30%)
  waiting for transfers between devices  19.7 us (18%)
  Pallas kernels  18.2 us (16%)
  local copies, waits for them, and re-layouts  1.63 us (1%)
    all_to_all x1, blocking collectives, exchange(): lax.all_to_all(value, axis, split_axis=0, concat_axis=0, tiled=True, axis...  32.8 us
    all_to_all x3, starting transfers between devices, exchange(): lax.all_to_all(value, axis, split_axis=0, concat_axis=0, tiled=True, axis...  29.3 us
    pallas_call x7, Pallas kernels, call(): pl.pallas_call(run, out_shape=[pltpu.HBM(shape, jnp.float32) if name in s...  18.2 us
    ppermute x6, waiting for transfers between devices, turned(): return lax.ppermute(value, 'seq', pairs)  10.5 us
    all_to_all x3, waiting for transfers between devices, exchange(): lax.all_to_all(value, axis, split_axis=0, concat_axis=0, tiled=True, axis...  9.18 us
    ppermute x6, starting transfers between devices, turned(): return lax.ppermute(value, 'seq', pairs)  7.86 us
  transfers between devices with their start and end apart: 9, of which 4 were waited for; matrix products, arithmetic and copies ran while one was open for 0% of the time, Pallas kernels for 7%

profile of v6, /device:TPU:1, one launch (start us, length us, event | category | flops | bytes accessed | tf_op | source)
XLA Modules:
  0.0 110.3 jit_solution(6641897392371461715)
XLA Ops:
  0.6 0.0 copy-start.1
  0.7 12.0 %all-to-all-start = ((f32[16,2,16,128]{3,2,1,0:T(8,128)}), f32[16,2,16,128]{3,2,1,0:T(8,128)S(1)}, u32[]{:S(2)}, u32[]{:S(2)}) async-start(f32[16,2,16,128]{3,2,1,0:T(8,128)} %bitcast.8), calls=%async_computation | async-start | bytes 524288 | tf_op jit(solution)/shard_map/all_to_all | solution.py:486
  12.7 0.7 copy-done.7
  13.3 1.6 %shard_map.121 = (f32[2,2,64,128]{3,2,1,0:T(8,128)S(1)}, f32[2,2,64,128]{3,2,1,0:T(8,128)S(1)}, f32[2,2,64,128]{3,2,1,0:T(8,128)S(1)}, f32[2,2,64,128]{3,2,1,0:T(8,128)S(1)}) custom-call(s32[2,9]{1,0:T(2,128)S(1)} %copy-done.7, f32[2,256,128]{2,1,0:T(8,128)S(1)} %copy-done, f32[2,256,128]{2,1,0:T(8,128)S(1)} %copy-done.1, f32[2,256,128]{2,1,0:T(8,128)} %refs_4_.6, ...), custom_call_target="tpu_custom_call" | custom-call | bytes 1343488 | tf_op jit(solution)/shard_map/pallas_call | solution.py:442
  14.9 3.1 %collective-permute-start = (f32[2,2,64,128]{3,2,1,0:T(8,128)S(1)}, f32[2,2,64,128]{3,2,1,0:T(8,128)S(1)}, u32[]{:S(2)}, u32[]{:S(2)}) collective-permute-start(f32[2,2,64,128]{3,2,1,0:T(8,128)S(1)} %get-tuple-element.26), channel_id=1, source_target_pairs={{480,496},{0,16},{32,48},{48,64},{64,80},{80,32},{96,112},{112,128... | collective-permute-start | bytes 393224 | tf_op jit(solution)/shard_map/ppermute | solution.py:482
  18.1 0.7 collective-permute-start.1
  18.8 1.4 %collective-permute-start.2 = (f32[2,2,64,128]{3,2,1,0:T(8,128)S(1)}, f32[2,2,64,128]{3,2,1,0:T(8,128)S(1)}, u32[]{:S(2)}, u32[]{:S(2)}) collective-permute-start(f32[2,2,64,128]{3,2,1,0:T(8,128)S(1)} %get-tuple-element.28), channel_id=1, source_target_pairs={{496,480},{16,0},{32,80},{48,32},{64,48},{80,64},{96,144},{112,96}... | collective-permute-start | bytes 393224 | tf_op jit(solution)/shard_map/ppermute | solution.py:482
  20.3 1.3 %shard_map.122.refs_11_ = f32[2,256,128]{2,1,0:T(8,128)S(1)} custom-call(s32[2,9]{1,0:T(2,128)S(1)} %copy-done.8, s32[2]{0:T(128)S(1)} %copy-done.9, f32[2,256,128]{2,1,0:T(8,128)S(1)} %copy-done, f32[2,256,128]{2,1,0:T(8,128)S(1)} %copy-done.1), custom_call_target="tpu_custom_call" | custom-call | flops 201326592 | bytes 786432 | tf_op jit(solution)/shard_map/pallas_call | solution.py:442
  21.6 6.8 %collective-permute-done.2.refs_9_.refs_10_ = f32[2,2,64,128]{3,2,1,0:T(8,128)S(1)} collective-permute-done((f32[2,2,64,128]{3,2,1,0:T(8,128)S(1)}, f32[2,2,64,128]{3,2,1,0:T(8,128)S(1)}, u32[]{:S(2)}, u32[]{:S(2)}) %collective-permute-start.2) | collective-permute-done | bytes 131104 | tf_op jit(solution)/shard_map/ppermute | solution.py:482
  28.4 1.9 %shard_map.123 = (f32[2,256,128]{2,1,0:T(8,128)S(1)}, f32[2,256,128]{2,1,0:T(8,128)S(1)}, f32[2,256,128]{2,1,0:T(8,128)S(1)}, f32[8,7,8,128]{3,2,1,0:T(8,128)}) custom-call(s32[2,9]{1,0:T(2,128)S(1)} %copy-done.8, s32[2]{0:T(128)S(1)} %copy-done.9, f32[16,2,16,128]{3,2,1,0:T(8,128)S(1)} %all-to-all-done.refs_2_, f32[2,256,128]{2,1,0:T(8,128)S(1)} %copy-done, ...), custom_call_target="tpu_custom_call" | custom-call | flops 50331648 | bytes 3112960 | tf_op jit(solution)/shard_map/pallas_call | solution.py:442
  30.3 8.4 %all-to-all-start.1 = ((f32[8,7,8,128]{3,2,1,0:T(8,128)}), f32[8,7,8,128]{3,2,1,0:T(8,128)S(1)}, u32[]{:S(2)}, u32[]{:S(2)}) async-start(f32[8,7,8,128]{3,2,1,0:T(8,128)} %get-tuple-element.29), calls=%async_computation.1 | async-start | bytes 458752 | tf_op jit(solution)/shard_map/all_to_all | solution.py:486
  38.7 0.6 shard_map.124.refs_16_
  39.3 1.3 %collective-permute-start.5 = (f32[3,64,128]{2,1,0:T(8,128)S(1)}, f32[3,64,128]{2,1,0:T(8,128)S(1)}, u32[]{:S(2)}, u32[]{:S(2)}) collective-permute-start(f32[3,64,128]{2,1,0:T(8,128)S(1)} %shard_map.124.refs_16_), channel_id=1, source_target_pairs={{496,480},{16,0},{48,32},{64,48},{80,64},{112,96},{128,112},{144,1... | collective-permute-start | bytes 294920 | tf_op jit(solution)/shard_map/ppermute | solution.py:482
  40.6 0.7 collective-permute-start.4
  41.3 0.7 collective-permute-start.3
  41.9 3.8 %collective-permute-done.5.refs_19_ = f32[3,64,128]{2,1,0:T(8,128)S(1)} collective-permute-done((f32[3,64,128]{2,1,0:T(8,128)S(1)}, f32[3,64,128]{2,1,0:T(8,128)S(1)}, u32[]{:S(2)}, u32[]{:S(2)}) %collective-permute-start.5) | collective-permute-done | bytes 98336 | tf_op jit(solution)/shard_map/ppermute | solution.py:482
  45.7 1.8 %all-to-all-done.1.refs_2_ = f32[8,7,8,128]{3,2,1,0:T(8,128)S(1)} async-done(((f32[8,7,8,128]{3,2,1,0:T(8,128)}), f32[8,7,8,128]{3,2,1,0:T(8,128)S(1)}, u32[]{:S(2)}, u32[]{:S(2)}) %all-to-all-start.1) | async-done | bytes 229408 | tf_op jit(solution)/shard_map/all_to_all | solution.py:486
  47.5 1.6 %shard_map.125 = f32[4,8,7,8,128]{4,3,2,1,0:T(8,128)} custom-call(s32[2,9]{1,0:T(2,128)S(1)} %copy-done.8, s32[2]{0:T(128)S(1)} %copy-done.9, f32[8,7,8,128]{3,2,1,0:T(8,128)S(1)} %all-to-all-done.1.refs_2_, f32[2,256,128]{2,1,0:T(8,128)S(1)} %copy-done), custom_call_target="tpu_custom_call" | custom-call | bytes 1409024 | tf_op jit(solution)/shard_map/pallas_call | solution.py:442
  49.2 8.9 %all-to-all-start.2 = ((f32[4,8,7,8,128]{4,3,2,1,0:T(8,128)}), f32[4,8,7,8,128]{4,3,2,1,0:T(8,128)S(1)}, u32[]{:S(2)}, u32[]{:S(2)}) async-start(f32[4,8,7,8,128]{4,3,2,1,0:T(8,128)} %shard_map.125), calls=%async_computation.2 | async-start | bytes 1835008 | tf_op jit(solution)/shard_map/all_to_all | solution.py:486
  58.1 4.0 %shard_map.126 = (f32[2,256,256]{2,1,0:T(8,128)}, f32[2,256,256]{2,1,0:T(8,128)}, f32[2,256,256]{2,1,0:T(8,128)}, f32[2,64,256]{2,1,0:T(8,128)}, f32[2,64,256]{2...) custom-call(s32[2,9]{1,0:T(2,128)S(1)} %copy-done.8, ...), custom_call_target="tpu_custom_call" | custom-call | flops 402653184 | bytes 4521984 | tf_op jit(solution)/shard_map/pallas_call | solution.py:442
  62.2 7.4 %all-to-all-done.2.refs_2_ = f32[4,8,7,8,128]{4,3,2,1,0:T(8,128)S(1)} async-done(((f32[4,8,7,8,128]{4,3,2,1,0:T(8,128)}), f32[4,8,7,8,128]{4,3,2,1,0:T(8,128)S(1)}, u32[]{:S(2)}, u32[]{:S(2)}) %all-to-all-start.2) | async-done | bytes 917536 | tf_op jit(solution)/shard_map/all_to_all | solution.py:486
  69.5 7.1 %shard_map.127 = f32[16,3,2,16,128]{4,3,2,1,0:T(8,128)S(1)} custom-call(s32[2,9]{1,0:T(2,128)S(1)} %copy-done.8, s32[2]{0:T(128)S(1)} %copy-done.9, f32[4,8,7,8,128]{4,3,2,1,0:T(8,128)S(1)} %all-to-all-done.2.refs_2_, f32[2,256,128]{2,1,0:T(8,128)S(1)} %copy-done, f32[2,256,128]{2,1,0:T(8,128)} %refs_4_.7, ...), custom_call_target="tpu_custom_call" | custom-call | flops 1610612736 | bytes 5668864 | tf_op jit(solution)/shard_map/pallas_call | solution.py:442
  76.7 32.8 %all_to_all.20 = f32[16,3,2,16,128]{4,3,2,1,0:T(8,128)S(1)} all-to-all(f32[16,3,2,16,128]{4,3,2,1,0:T(8,128)S(1)} %shard_map.127), channel_id=1, replica_groups=mesh['seq'=32,'head'=16] {'head'}, dimensions={0} | all-to-all | bytes 1572864 | tf_op jit(solution)/shard_map/all_to_all | solution.py:486
  109.5 0.9 fusion
  (29 shorter events, 0.1 us)
Async XLA Ops:
  0.6 12.0 %copy-start = (f32[2,256,128]{2,1,0:T(8,128)S(1)}, f32[2,256,128]{2,1,0:T(8,128)}, u32[]{:S(2)}) copy-start(f32[2,256,128]{2,1,0:T(8,128)} %refs_3_.11) | copy-start | bytes 786436
  0.6 12.0 %copy-start.1 = (f32[2,256,128]{2,1,0:T(8,128)S(1)}, f32[2,256,128]{2,1,0:T(8,128)}, u32[]{:S(2)}) copy-start(f32[2,256,128]{2,1,0:T(8,128)} %refs_4_.7) | copy-start | bytes 786436
  0.7 27.7 %all-to-all-start = ((f32[16,2,16,128]{3,2,1,0:T(8,128)}), f32[16,2,16,128]{3,2,1,0:T(8,128)S(1)}, u32[]{:S(2)}, u32[]{:S(2)}) async-start(f32[16,2,16,128]{3,2,1,0:T(8,128)} %bitcast.8), calls=%async_computation | async-start | bytes 524288 | tf_op jit(solution)/shard_map/all_to_all | solution.py:486
  12.6 0.7 copy-start.7
  14.9 6.7 %collective-permute-start = (f32[2,2,64,128]{3,2,1,0:T(8,128)S(1)}, f32[2,2,64,128]{3,2,1,0:T(8,128)S(1)}, u32[]{:S(2)}, u32[]{:S(2)}) collective-permute-start(f32[2,2,64,128]{3,2,1,0:T(8,128)S(1)} %get-tuple-element.26), channel_id=1, source_target_pairs={{480,496},{0,16},{32,48},{48,64},{64,80},{80,32},{96,112},{112,128... | collective-permute-start | bytes 393224 | tf_op jit(solution)/shard_map/ppermute | solution.py:482
  18.1 2.2 %copy-start.8 = (s32[2,9]{1,0:T(2,128)S(1)}, s32[2,9]{1,0:T(2,128)}, u32[]{:S(2)}) copy-start(s32[2,9]{1,0:T(2,128)} %refs_0_.13) | copy-start | bytes 220
  18.1 2.2 %copy-start.9 = (s32[2]{0:T(128)S(1)}, s32[2]{0:T(128)}, u32[]{:S(2)}) copy-start(s32[2]{0:T(128)} %refs_1_.13) | copy-start | bytes 28
  18.1 3.5 %collective-permute-start.1 = (f32[2,2,64,128]{3,2,1,0:T(8,128)S(1)}, f32[2,2,64,128]{3,2,1,0:T(8,128)S(1)}, u32[]{:S(2)}, u32[]{:S(2)}) collective-permute-start(f32[2,2,64,128]{3,2,1,0:T(8,128)S(1)} %get-tuple-element.27), channel_id=1, source_target_pairs={{32,64},{48,80},{64,32},{80,48},{96,128},{112,144},{128,96},{144,1... | collective-permute-start | bytes 393224 | tf_op jit(solution)/shard_map/ppermute | solution.py:482
  18.8 9.6 %copy-start.2 = (f32[2,256,128]{2,1,0:T(8,128)S(1)}, f32[2,256,128]{2,1,0:T(8,128)}, u32[]{:S(2)}) copy-start(f32[2,256,128]{2,1,0:T(8,128)} %refs_4_.6) | copy-start | bytes 786436
  18.8 9.6 %copy-start.3 = (f32[2,256,128]{2,1,0:T(8,128)S(1)}, f32[2,256,128]{2,1,0:T(8,128)}, u32[]{:S(2)}) copy-start(f32[2,256,128]{2,1,0:T(8,128)} %refs_10_.1) | copy-start | bytes 786436
  18.8 9.6 %collective-permute-start.2 = (f32[2,2,64,128]{3,2,1,0:T(8,128)S(1)}, f32[2,2,64,128]{3,2,1,0:T(8,128)S(1)}, u32[]{:S(2)}, u32[]{:S(2)}) collective-permute-start(f32[2,2,64,128]{3,2,1,0:T(8,128)S(1)} %get-tuple-element.28), channel_id=1, source_target_pairs={{496,480},{16,0},{32,80},{48,32},{64,48},{80,64},{96,144},{112,96}... | collective-permute-start | bytes 393224 | tf_op jit(solution)/shard_map/ppermute | solution.py:482
  30.3 17.2 %all-to-all-start.1 = ((f32[8,7,8,128]{3,2,1,0:T(8,128)}), f32[8,7,8,128]{3,2,1,0:T(8,128)S(1)}, u32[]{:S(2)}, u32[]{:S(2)}) async-start(f32[8,7,8,128]{3,2,1,0:T(8,128)} %get-tuple-element.29), calls=%async_computation.1 | async-start | bytes 458752 | tf_op jit(solution)/shard_map/all_to_all | solution.py:486
  39.3 6.4 %collective-permute-start.5 = (f32[3,64,128]{2,1,0:T(8,128)S(1)}, f32[3,64,128]{2,1,0:T(8,128)S(1)}, u32[]{:S(2)}, u32[]{:S(2)}) collective-permute-start(f32[3,64,128]{2,1,0:T(8,128)S(1)} %shard_map.124.refs_16_), channel_id=1, source_target_pairs={{496,480},{16,0},{48,32},{64,48},{80,64},{112,96},{128,112},{144,1... | collective-permute-start | bytes 294920 | tf_op jit(solution)/shard_map/ppermute | solution.py:482
  40.6 5.1 %collective-permute-start.4 = (f32[3,64,128]{2,1,0:T(8,128)S(1)}, f32[3,64,128]{2,1,0:T(8,128)S(1)}, u32[]{:S(2)}, u32[]{:S(2)}) collective-permute-start(f32[3,64,128]{2,1,0:T(8,128)S(1)} %shard_map.124.refs_16_), channel_id=1, source_target_pairs={{64,32},{80,48},{128,96},{144,112},{192,160},{208,176},{256,224},{... | collective-permute-start | bytes 294920 | tf_op jit(solution)/shard_map/ppermute | solution.py:482
  41.3 4.5 %collective-permute-start.3 = (f32[3,64,128]{2,1,0:T(8,128)S(1)}, f32[3,64,128]{2,1,0:T(8,128)S(1)}, u32[]{:S(2)}, u32[]{:S(2)}) collective-permute-start(f32[3,64,128]{2,1,0:T(8,128)S(1)} %shard_map.124.refs_16_), channel_id=1, source_target_pairs={{80,32},{144,96},{208,160},{272,224},{336,288},{400,352},{464,416}... | collective-permute-start | bytes 294920 | tf_op jit(solution)/shard_map/ppermute | solution.py:482
  45.7 3.4 %copy-start.10 = (f32[3,64,128]{2,1,0:T(8,128)}, f32[3,64,128]{2,1,0:T(8,128)S(1)}, u32[]{:S(2)}) copy-start(f32[3,64,128]{2,1,0:T(8,128)S(1)} %collective-permute-done.5.refs_19_) | copy-start | bytes 294916
  45.7 3.4 %copy-start.11 = (f32[3,64,128]{2,1,0:T(8,128)}, f32[3,64,128]{2,1,0:T(8,128)S(1)}, u32[]{:S(2)}) copy-start(f32[3,64,128]{2,1,0:T(8,128)S(1)} %collective-permute-done.4.refs_18_) | copy-start | bytes 294916
  45.7 3.4 %copy-start.12 = (f32[3,64,128]{2,1,0:T(8,128)}, f32[3,64,128]{2,1,0:T(8,128)S(1)}, u32[]{:S(2)}) copy-start(f32[3,64,128]{2,1,0:T(8,128)S(1)} %collective-permute-done.3.refs_17_) | copy-start | bytes 294916
  49.2 9.0 %copy-start.4 = (s32[2,64,64]{2,1,0:T(8,128)S(1)}, s32[2,64,64]{2,1,0:T(8,128)}, u32[]{:S(2)}) copy-start(s32[2,64,64]{2,1,0:T(8,128)} %refs_12_.1) | copy-start | bytes 98308
  49.2 9.0 %copy-start.5 = (s32[2,256,64]{1,2,0:T(8,128)S(1)}, s32[2,256,64]{1,2,0:T(8,128)}, u32[]{:S(2)}) copy-start(s32[2,256,64]{1,2,0:T(8,128)} %param.17) | copy-start | bytes 393220
  49.2 9.0 %copy-start.6 = (s32[2,256,64]{1,2,0:T(8,128)S(1)}, s32[2,256,64]{1,2,0:T(8,128)}, u32[]{:S(2)}) copy-start(s32[2,256,64]{1,2,0:T(8,128)} %param.19) | copy-start | bytes 393220
  49.2 20.3 %all-to-all-start.2 = ((f32[4,8,7,8,128]{4,3,2,1,0:T(8,128)}), f32[4,8,7,8,128]{4,3,2,1,0:T(8,128)S(1)}, u32[]{:S(2)}, u32[]{:S(2)}) async-start(f32[4,8,7,8,128]{4,3,2,1,0:T(8,128)} %shard_map.125), calls=%async_computation.2 | async-start | bytes 1835008 | tf_op jit(solution)/shard_map/all_to_all | solution.py:486
